TPU v7x, 32 devices: a whole 2x2x4 slice. The times are simulated.
32 devices in a mesh: gx: 2 (over y), gy: 4 (over x, core), gz: 4 (over z).
Axes of the slice: x: 2, y: 2, z: 4, core: 2. Of those that a mesh axis runs over, the one named last changes fastest.
Arguments:
- displacement: float32 [6, 8, 32, 512], P(None, 'gx', 'gy', 'gz'), may hold values from -6 to 6
- velocity: float32 [6, 8, 32, 512], P(None, 'gx', 'gy', 'gz'), may hold values from -6 to 6
- moments: float32 [6, 8, 32, 512], P(None, 'gx', 'gy', 'gz'), may hold values from -6 to 6
- sector_bit: int32 [2, 8, 32, 512], P(None, 'gx', 'gy', 'gz'), may hold values from 0 to 1
- weight_in: bfloat16 [32, 256], replicated, may hold values from -1 to 1
- bias_in: float32 [256], replicated, may hold values from -3 to 3
- weight_mid: bfloat16 [256, 256], replicated, may hold values from -0.375 to 0.375
- weight_out: bfloat16 [256, 4], replicated, may hold values from -0.375 to 0.375
Outputs:
- displacement_out: float32 [6, 8, 32, 512], P(None, 'gx', 'gy', 'gz')
- velocity_out: float32 [6, 8, 32, 512], P(None, 'gx', 'gy', 'gz')
- moments_out: float32 [6, 8, 32, 512], P(None, 'gx', 'gy', 'gz')
All inputs are finite; a program needn't handle non-finite values.
Results may differ from a plain program's by a relative error of at most 0.0014.
Values sent between devices are 32-bit elements; how exact they have to be, the bound alone decides.
No kernel may reach another device: no remote copies, remote signals or barrier semaphores. Data moves between devices by JAX's collectives and lax.ppermute only.
A program may use at most 64 MiB of HBM per device.

v0:
```python
import functools

import jax
import jax.numpy as jnp
import numpy as np
from jax import lax
from jax.experimental import pallas as pl
from jax.experimental.pallas import tpu as pltpu
from jax.sharding import PartitionSpec as P


half_step = 0.1
lattice_step = 0.25
second_shell = 0.5

f32 = jnp.float32
bf16 = jnp.bfloat16
SUB, LANE = 8, 128
SLAB = 32
XL = 4
ORDER = (0, 2, 1, 3)
TILE = (SUB, LANE)


def iota(dim):
    return lax.broadcasted_iota(jnp.int32, TILE, dim)


def odd_mask(par):
    return ((iota(0) + iota(1) + par) & 1) == 1


def lane_block():
    return ((iota(1) + SLAB // 2) // SLAB) & 3


def lanes(v, shift):
    shift = shift % LANE
    return v if shift == 0 else pltpu.roll(v, shift, 1)


def rows(v, shift):
    return pltpu.roll(v, shift % SUB, 0)


def merge_blocks(tiles):
    block = lane_block()
    out = lanes(tiles[0], 0)
    for b in range(1, 4):
        out = jnp.where(block == b, lanes(tiles[b], SLAB * b), out)
    return out


def vmem_call(body, out_shapes, *args, scratch=(), cost=None, space=None, grant=24 << 20):
    spec = pl.BlockSpec(memory_space=pltpu.VMEM)
    given = pl.BlockSpec(memory_space=space or pltpu.VMEM)
    return pl.pallas_call(
        body,
        out_shape=tuple(jax.ShapeDtypeStruct(s, d) for s, d in out_shapes),
        in_specs=[given] * len(args),
        out_specs=tuple(spec for _ in out_shapes),
        scratch_shapes=list(scratch),
        compiler_params=pltpu.CompilerParams(vmem_limit_bytes=grant),
        cost_estimate=cost,
    )(*args)


def pack_body(disp_in, mom_in, bit_in, out, disp, mom, bit, sems):
    copies = [
        pltpu.make_async_copy(source, target, sems.at[n])
        for n, (source, target) in enumerate(((disp_in, disp), (mom_in, mom), (bit_in, bit)))
    ]
    for copy in copies:
        copy.start()
    for copy in copies:
        copy.wait()
    for i in range(14):
        if i < 6:
            tiles = [disp[i, x] for x in ORDER]
        elif i < 12:
            tiles = [mom[i - 6, x] for x in ORDER]
        else:
            tiles = [bit[i - 12, x].astype(f32) for x in ORDER]
        out[i] = merge_blocks(tiles)


def halo_body(disp, mom, bit, low, high, slab, brick, faces, yup, ydn):
    upper = (iota(1) & (SLAB - 1)) >= SLAB // 2
    e0 = odd_mask(0)
    for i in range(14):
        slab[i] = jnp.where(upper, low[i], high[i])
    for p in range(2):
        for k in range(4):
            i = 6 + 3 * p + k if k < 3 else 12 + p
            tiles = [mom[3 * p + k, x] if k < 3 else bit[p, x].astype(f32) for x in range(XL)]
            for xh in range(2):
                even, odd = tiles[2 * xh], tiles[2 * xh + 1]
                brick[xh, 4 * p + k] = jnp.where(e0, odd, even)
                brick[2 + xh, 4 * p + k] = jnp.where(e0, even, odd)
            h = slab[i]
            brick[4, 4 * p + k] = jnp.where(e0, lanes(h, 64), h)
    for i in range(6):
        src = disp if i < 3 else mom
        k = i % 3
        base = 0 if i < 3 else 6
        faces[0, 2 * i] = src[3 + k, XL - 1]
        faces[0, 2 * i + 1] = slab[base + 3 + k]
        faces[1, 2 * i] = src[k, 0]
        faces[1, 2 * i + 1] = slab[base + k]
        yup[i] = jnp.zeros(TILE, f32)
        ydn[i] = jnp.zeros(TILE, f32)
        for x in range(XL):
            yup[i, x : x + 1, :] = src[3 + k, x, SUB - 1 : SUB, :]
            ydn[i, x : x + 1, :] = src[k, x, 0:1, :]
        yup[i, XL : XL + 1, :] = slab[base + 3 + k, SUB - 1 : SUB, :]
        ydn[i, XL : XL + 1, :] = slab[base + k, 0:1, :]


def near_tiles(p, disp, mom, slab, xf, yr, xyr, near):
    q = 1 - p
    lane, sub = iota(1), iota(0)
    block = lane_block()
    edge_x = XL - 1 if p == 0 else 0
    for i in range(6):
        src = disp if i < 3 else mom
        k = i % 3
        c = [src[3 * q + k, x] for x in range(XL)]
        h = slab[(0 if i < 3 else 6) + 3 * q + k]
        fc, fh = xf[2 * i], xf[2 * i + 1]

        def wide(row):
            return jnp.broadcast_to(row, TILE)

        for dy in range(2):
            if dy:
                step = 1 if p == 0 else -1
                put = sub == (0 if p == 0 else SUB - 1)
                c = [jnp.where(put, wide(yr[i, x : x + 1, :]), rows(c[x], step)) for x in range(XL)]
                h = jnp.where(put, wide(yr[i, XL : XL + 1, :]), rows(h, step))
                fc = jnp.where(put, wide(xyr[i, edge_x : edge_x + 1, :]), rows(fc, step))
                fh = jnp.where(put, wide(xyr[i, XL : XL + 1, :]), rows(fh, step))
            for dz in range(2):
                if dz == 0:
                    cs, hs, fcs, fhs = c, h, fc, fh
                else:
                    step = 1 if p == 0 else -1
                    seam = LANE - 1 if p == 0 else 0
                    at_seam = lane == seam
                    at_seams = (lane & (SLAB - 1)) == (SLAB - 1 if p == 0 else 0)
                    cs = [
                        lanes(jnp.where(at_seam, lanes(h, -SLAB * ORDER[x]), c[x]), step)
                        for x in range(XL)
                    ]
                    hs = lanes(jnp.where(at_seams, merge_blocks([c[x] for x in ORDER]), h), step)
                    fcs = lanes(jnp.where(at_seam, lanes(fh, -SLAB * ORDER[edge_x]), fc), step)
                    fhs = lanes(jnp.where(at_seams, lanes(fc, SLAB * ORDER[edge_x]), fh), step)
                at = 2 * dy + dz
                line = [fcs] + cs if p == 0 else cs + [fcs]
                for j in range(XL + 1):
                    near[i, at, j] = line[j]
                near[i, at, XL + 1] = hs
                if p == 0:
                    moved = jnp.where(block == 0, lanes(fhs, SLAB), lanes(hs, 2 * SLAB))
                    moved = jnp.where(block == 1, lanes(hs, -SLAB), moved)
                else:
                    moved = jnp.where(block == 3, lanes(fhs, -SLAB), lanes(hs, 2 * SLAB))
                    moved = jnp.where(block == 2, lanes(hs, SLAB), moved)
                near[i, at, XL + 2] = moved


def feature_rows(p, disp, mom, slab, near, table):
    for slot in range(XL + 1):
        if slot < XL:
            own = [disp[3 * p + k, slot] for k in range(3)]
            own += [mom[3 * p + k, slot] for k in range(3)]
        else:
            own = [slab[3 * p + k] for k in range(3)] + [slab[6 + 3 * p + k] for k in range(3)]
        for o in range(8):
            dx, at = o >> 2, o & 3
            if slot == XL:
                j = XL + 1 + dx
            else:
                j = slot + 1 - dx if p == 0 else slot + dx
            for k in range(3):
                table[slot, SUB * (4 * o + k) : SUB * (4 * o + k + 1), :] = near[k, at, j] - own[k]
            dot = own[3] * near[3, at, j] + own[4] * near[4, at, j] + own[5] * near[5, at, j]
            table[slot, SUB * (4 * o + 3) : SUB * (4 * o + 4), :] = dot


def silu_half(u):
    return (u + u * jnp.tanh(u)).astype(bf16)


def perceptron(table, heads, w_in, b_in, w_mid, w_out, one, two, count):
    def step(slot, carry):
        source = jnp.minimum(slot, count - 1)
        before = jnp.where(slot == 0, count, slot - 1)
        for c in range(4):
            block = jnp.concatenate(
                [
                    jnp.concatenate(
                        [
                            table[source, pl.ds(SUB * SUB * m + 2 * c + j, SUB, stride=SUB), :]
                            for m in range(4)
                        ],
                        axis=0,
                    )
                    for j in range(2)
                ],
                axis=1,
            ).astype(bf16)
            bias = b_in[...]
            hidden, last = one[...], two[...]
            u = jnp.dot(w_in[...], block, preferred_element_type=f32)
            u = u + jnp.concatenate([bias, bias], axis=1)
            v = jnp.dot(w_mid[...], hidden, preferred_element_type=f32)
            out = jnp.dot(w_out[...], last, preferred_element_type=f32)
            one[...] = silu_half(u)
            two[...] = silu_half(v)
            done = 2 * c - 4 if c >= 2 else 2 * c + 4
            target = slot if c >= 2 else before
            for j in range(2):
                heads[target, pl.ds(done + j, SUB, stride=SUB), :] = out[:, LANE * j : LANE * (j + 1)]
        return carry

    one[...] = jnp.zeros(one.shape, bf16)
    two[...] = jnp.zeros(two.shape, bf16)
    lax.fori_loop(0, count + 1, step, 0)


def network_body(
    disp, mom, vel, slab, xup, xdn, yup, ydn, xyup, xydn, w_in, b_in, w_mid, w_out,
    disp_out, vel_out, cbrick, near, table, heads, one, two,
):
    e0 = odd_mask(0)
    slots = XL + 1
    for p in range(2):
        args = (xup.at[0], yup, xyup) if p == 0 else (xdn.at[xdn.shape[0] - 1], ydn, xydn)
        near_tiles(p, disp, mom, slab, *args, near)
        feature_rows(p, disp, mom, slab, near, table.at[pl.ds(slots * p, slots)])
    perceptron(table, heads, w_in, b_in, w_mid, w_out, one, two, 2 * slots)
    for p in range(2):
        coupling = []
        for slot in range(slots):
            at = slots * p + slot
            coupling.append(1.0 + 0.5 * jnp.tanh(heads[at, 3 * SUB : 4 * SUB, :]))
            if slot < XL:
                for k in range(3):
                    v = vel[3 * p + k, slot] + lattice_step * heads[at, k * SUB : (k + 1) * SUB, :]
                    vel_out[3 * p + k, slot] = v
                    disp_out[3 * p + k, slot] = disp[3 * p + k, slot] + lattice_step * v
        for xh in range(2):
            even, odd = coupling[2 * xh], coupling[2 * xh + 1]
            cbrick[xh, p] = jnp.where(e0, odd, even)
            cbrick[2 + xh, p] = jnp.where(e0, even, odd)
        cbrick[4, p] = jnp.where(e0, lanes(coupling[4], 64), coupling[4])


def even_fit(func, terms):
    edge = (np.pi / 2) ** 2 * 1.0001
    node = np.cos((np.arange(400) + 0.5) * np.pi / 400)
    w = 0.5 * edge * (1 + node)
    basis = np.stack([w**n for n in range(terms)], 1)
    return [float(c) for c in np.linalg.lstsq(basis, func(np.sqrt(w)), rcond=None)[0]]


ROOT = float(np.sqrt(2.0))
SIN = [ROOT * c * np.pi ** (2 * n + 1) for n, c in enumerate(even_fit(lambda r: np.sin(r) / r, 5))]
COS = [ROOT * c * np.pi ** (2 * n) for n, c in enumerate(even_fit(np.cos, 5))]


def horner(coeffs, w):
    out = float(coeffs[-1])
    for c in reversed(coeffs[:-1]):
        out = out * w + float(c)
    return out


def crossed(a, b):
    return (a[1] * b[2] - a[2] * b[1], a[2] * b[0] - a[0] * b[2], a[0] * b[1] - a[1] * b[0])


def rotated(s, b, half_turns, hit):
    square = b[0] * b[0] + b[1] * b[1] + b[2] * b[2]
    inverse = lax.rsqrt(jnp.maximum(square, 1e-30))
    angle = (square * inverse) * half_turns
    angle = angle - jnp.round(angle)
    w = angle * angle
    sine = jnp.where(hit, horner(SIN, w) * (angle * inverse), 0.0)
    cosine = horner(COS, w)
    axis = [sine * b[k] for k in range(3)]
    first = crossed(axis, s)
    second = crossed(axis, [cosine * s[k] + first[k] for k in range(3)])
    return [s[k] + second[k] for k in range(3)]


def turns_body(nx, ny, masks, *refs):
    count = len(masks)
    bricks, cbricks = refs[:count], refs[count : 2 * count]
    out = refs[2 * count]
    mc, mh, sc, sh, cc, ch, tc, th, nc, nh = refs[2 * count + 1 :]
    xh_all, groups = 2 * nx, nx // 2
    ix, iy = lax.axis_index("gx"), lax.axis_index("gy")
    lane = iota(1)
    block = lane_block()
    first_half = block < 2
    e0 = odd_mask(0)

    def row_mask(r, par):
        return ((lane + (r + par)) & 1) == 1

    def place(source, comps):
        for n, (mx, my) in enumerate(masks):
            bx, by = ix ^ mx, iy ^ my
            own_rows = pl.ds(pl.multiple_of(by * SUB, SUB), SUB)
            for k in range(comps):
                for par in range(2):
                    for xh in range(2):
                        sc[par, k, 2 * bx + xh, own_rows, :] = source[n][2 * par + xh, k]
                sh[k, bx, own_rows, :] = source[n][4, k]

    def spread(comps, put_c, put_h):
        for k in range(comps):
            for r in range(ny):
                part = pl.ds(r, SUB, stride=ny)
                for par in range(2):
                    for j in range(xh_all):
                        put_c(k, par, r, j, sc[par, k, j, part, :])
                for g in range(groups):
                    even, odd = sh[k, 2 * g, part, :], sh[k, 2 * g + 1, part, :]
                    put_h(k, 0, r, g, jnp.where(first_half, even, lanes(odd, 64)))
                    put_h(k, 1, r, g, jnp.where(first_half, lanes(even, 64), odd))

    def put_mc(k, par, r, j, v):
        mc[k // 4, par, k % 4, r, j] = v

    def put_mh(k, par, r, g, v):
        mh[k // 4, par, k % 4, r, g] = v

    def put_cc(k, par, r, j, v):
        cc[k, par, r, j] = v * (1.0 / second_shell)

    def put_ch(k, par, r, g, v):
        ch[k, par, r, g] = v * (1.0 / second_shell)

    def next_block(tiles, g):
        other = tiles[(g + 1) % groups]
        return lanes(jnp.where(block == 0, other, tiles[g]) if groups > 1 else tiles[g], -SLAB)

    def last_block(tiles, g):
        other = tiles[(g - 1) % groups]
        return lanes(jnp.where(block == 3, other, tiles[g]) if groups > 1 else tiles[g], SLAB)

    def seams(c, h):
        return (
            [lanes(h[x // 4], -SLAB * (x % 4)) for x in range(xh_all)],
            [merge_blocks(c[4 * g : 4 * g + 4]) for g in range(groups)],
        )

    def z_next(c, h, seam):
        cs = [lanes(jnp.where(lane == 0, seam[0][x], c[x]), -1) for x in range(xh_all)]
        at = (lane & (SLAB - 1)) == 0
        return cs, [lanes(jnp.where(at, seam[1][g], h[g]), -1) for g in range(groups)]

    def z_last(c, h, seam):
        cs = [lanes(jnp.where(lane == LANE - 1, seam[0][x], c[x]), 1) for x in range(xh_all)]
        at = (lane & (SLAB - 1)) == SLAB - 1
        return cs, [lanes(jnp.where(at, seam[1][g], h[g]), 1) for g in range(groups)]

    def y_next(ref, head, r, j):
        return rows(ref[*head, 0, j], -1) if r == ny - 1 else ref[*head, r + 1, j]

    def y_last(ref, head, r, j):
        return rows(ref[*head, ny - 1, j], 1) if r == 0 else ref[*head, r - 1, j]

    def near_total(p):
        q = 1 - p
        y_move = y_last if p == 0 else y_next
        z_move = z_last if p == 0 else z_next
        for k in range(3):
            for r in range(ny):
                e = row_mask(r, 0)
                for ref, to, size in ((mc, tc, xh_all), (mh, th, groups)):
                    zero = [ref[q, 0, k, r, j] for j in range(size)]
                    one = [ref[q, 1, k, r, j] for j in range(size)]
                    even = [jnp.where(e, one[j], zero[j]) for j in range(size)]
                    odd = [jnp.where(e, zero[j], one[j]) for j in range(size)]
                    for j in range(size):
                        to[k, 0, r, j] = zero[j] + one[j]
                        if p == 0:
                            prev = odd[(j - 1) % size] if ref is mc else last_block(odd, j)
                            to[k, 1, r, j] = even[j] + prev
                        else:
                            after = even[(j + 1) % size] if ref is mc else next_block(even, j)
                            to[k, 1, r, j] = odd[j] + after
            for r in range(ny):
                e = row_mask(r, 0)
                got = []
                for t in range(2):
                    c = [tc[k, t, r, j] + y_move(tc, (k, t), r, j) for j in range(xh_all)]
                    h = [th[k, t, r, j] + y_move(th, (k, t), r, j) for j in range(groups)]
                    cs, hs = z_move(c, h, seams(c, h))
                    got.append(
                        ([c[j] + cs[j] for j in range(xh_all)], [h[j] + hs[j] for j in range(groups)])
                    )
                for kind, to, size in ((0, nc, xh_all), (1, nh, groups)):
                    for j in range(size):
                        whole, split = got[0][kind][j], got[1][kind][j]
                        if p == 1:
                            whole, split = split, whole
                        to[0, k, r, j] = jnp.where(e, whole, split)
                        to[1, k, r, j] = jnp.where(e, split, whole)

    def turn(p, par, bit, half_turns):
        opp = 1 - par
        for r in range(ny):
            e = row_mask(r, par)
            shell_c, shell_h = [], []
            for k in range(3):
                head = (p, opp, k)
                c = [mc[*head, r, j] for j in range(xh_all)]
                h = [mh[*head, r, g] for g in range(groups)]
                seam = seams(c, h)
                cn, hn = z_next(c, h, seam)
                cl, hl = z_last(c, h, seam)
                one, two = [], []
                for j in range(xh_all):
                    x = c[j] + jnp.where(e, c[(j + 1) % xh_all], c[(j - 1) % xh_all])
                    y = y_next(mc, head, r, j) + y_last(mc, head, r, j)
                    one.append(x + y + (cn[j] + cl[j]))
                for g in range(groups):
                    x = h[g] + jnp.where(e, next_block(h, g), last_block(h, g))
                    y = y_next(mh, head, r, g) + y_last(mh, head, r, g)
                    two.append(x + y + (hn[g] + hl[g]))
                shell_c.append(one)
                shell_h.append(two)
            for state, couple, near, shell, size in (
                (mc, cc, nc, shell_c, xh_all),
                (mh, ch, nh, shell_h, groups),
            ):
                for j in range(size):
                    cpl = couple[p, par, r, j]
                    field = [cpl * near[par, k, r, j] + shell[k][j] for k in range(3)]
                    own = [state[p, par, k, r, j] for k in range(3)]
                    new = rotated(own, field, half_turns, state[p, par, 3, r, j] == bit)
                    for k in range(3):
                        state[p, par, k, r, j] = new[k]

    unit = second_shell * half_step / (2.0 * np.pi)

    def sweep(p, sector, half_turns):
        turn(p, sector & 1, (sector >> 1).astype(f32), half_turns)

    def climb(i, carry):
        sweep(0, i, unit)
        return carry

    def middle(i, carry):
        sector = 3 - jnp.abs(3 - i)
        sweep(1, sector, jnp.where(i == 3, 2 * unit, unit).astype(f32))
        return carry

    def descend(i, carry):
        sweep(0, 3 - i, unit)
        return carry

    place(bricks, 8)
    spread(8, put_mc, put_mh)
    place(cbricks, 2)
    spread(2, put_cc, put_ch)
    near_total(0)
    lax.fori_loop(0, 4, climb, 0)
    near_total(1)
    lax.fori_loop(0, 7, middle, 0)
    near_total(0)
    lax.fori_loop(0, 4, descend, 0)

    for p in range(2):
        for k in range(3):
            for par in range(2):
                for xh in range(2):
                    for r in range(ny):
                        sc[par, k, xh, pl.ds(r, SUB, stride=ny), :] = mc[p, par, k, r, 2 * ix + xh]
            own_rows = pl.ds(pl.multiple_of(iy * SUB, SUB), SUB)
            for xh in range(2):
                zero, one = sc[0, k, xh, own_rows, :], sc[1, k, xh, own_rows, :]
                out[3 * p + k, 2 * xh] = jnp.where(e0, one, zero)
                out[3 * p + k, 2 * xh + 1] = jnp.where(e0, zero, one)


def on_device(nx, ny, nz, displacement, velocity, moments, sector_bit, weight_in, bias_in, weight_mid, weight_out):
    assert displacement.shape == (6, XL, SUB, LANE)
    assert nx % 2 == 0 and nx & (nx - 1) == 0 and ny & (ny - 1) == 0 and ny % 2 == 0
    plane = ("gx", "gy")

    def pairs(move):
        out = []
        for x in range(nx):
            for y in range(ny):
                tx, ty = move(x, y)
                out.append((x * ny + y, tx % nx * ny + ty % ny))
        return out

    def shift(v, dx, dy):
        return lax.ppermute(v, plane, pairs(lambda x, y: (x + dx, y + dy)))

    def swap(v, mx, my):
        return lax.ppermute(v, plane, pairs(lambda x, y: (x ^ mx, y ^ my)))

    def along_z(v, step):
        return lax.ppermute(v, "gz", [(i, (i + step) % nz) for i in range(nz)])

    w_in = (weight_in.T.astype(f32) * 0.5).astype(bf16)
    w_mid = (weight_mid.T.astype(f32) * 0.5).astype(bf16)
    w_out = jnp.pad(weight_out.T, ((0, SUB - 4), (0, 0)))
    hidden = weight_mid.shape[0]
    b_in = jnp.broadcast_to((0.5 * bias_in)[:, None], (hidden, LANE))

    (packed,) = vmem_call(
        pack_body, [((14, *TILE), f32)], displacement, moments, sector_bit,
        space=pltpu.HBM,
        grant=60 << 20,
        scratch=[
            pltpu.VMEM(displacement.shape, f32),
            pltpu.VMEM(moments.shape, f32),
            pltpu.VMEM(sector_bit.shape, sector_bit.dtype),
            pltpu.SemaphoreType.DMA((3,)),
        ],
    )
    low, high = along_z(packed, 1), along_z(packed, -1)
    slab, brick, faces, yup, ydn = vmem_call(
        halo_body,
        [((14, *TILE), f32), ((5, 8, *TILE), f32)] + [((2, 12, *TILE), f32)] + [((6, *TILE), f32)] * 2,
        displacement, moments, sector_bit, low, high,
    )
    if nx == 2:
        faces = shift(faces, 1, 0)
        xup, xdn = faces, faces
    else:
        xup, xdn = shift(faces[:1], 1, 0), shift(faces[1:], -1, 0)
    xyup, xydn = shift(yup, 1, 1), shift(ydn, -1, -1)
    yup, ydn = shift(yup, 0, 1), shift(ydn, 0, -1)

    far = [(mx, my) for mx in range(nx) for my in range(0, ny, 2) if mx or my]
    held = {(0, 0): brick}
    for mask in far:
        held[mask] = swap(brick, *mask)

    disp_out, vel_out, cbrick = vmem_call(
        network_body,
        [((6, XL, *TILE), f32), ((6, XL, *TILE), f32), ((5, 2, *TILE), f32)],
        displacement, moments, velocity, slab, xup, xdn, yup, ydn, xyup, xydn, w_in, b_in, w_mid, w_out,
        scratch=[
            pltpu.VMEM((6, 4, XL + 3, *TILE), f32),
            pltpu.VMEM((2 * XL + 2, 32 * SUB, LANE), f32),
            pltpu.VMEM((2 * XL + 3, SUB * SUB, LANE), f32),
            pltpu.VMEM((hidden, 2 * LANE), bf16),
            pltpu.VMEM((hidden, 2 * LANE), bf16),
        ],
    )
    near_masks = [(0, 0)] + far
    late = lax.optimization_barrier((cbrick, *[held[m] for m in near_masks]))
    cbrick = late[0]
    held.update(zip(near_masks, late[1:]))
    cheld = {(0, 0): cbrick}
    for mask in far:
        cheld[mask] = swap(cbrick, *mask)
    for mx, my in near_masks:
        held[mx, my + 1] = swap(held[mx, my], 0, 1)
    for mx, my in near_masks:
        cheld[mx, my + 1] = swap(cheld[mx, my], 0, 1)

    masks = sorted(held)
    xh_all, groups = 2 * nx, nx // 2
    (moments_out,) = vmem_call(
        functools.partial(turns_body, nx, ny, masks),
        [((6, XL, *TILE), f32)],
        *[held[m] for m in masks],
        *[cheld[m] for m in masks],
        scratch=[
            pltpu.VMEM((2, 2, 4, ny, xh_all, *TILE), f32),
            pltpu.VMEM((2, 2, 4, ny, groups, *TILE), f32),
            pltpu.VMEM((2, 8, xh_all, ny * SUB, LANE), f32),
            pltpu.VMEM((8, nx, ny * SUB, LANE), f32),
            pltpu.VMEM((2, 2, ny, xh_all, *TILE), f32),
            pltpu.VMEM((2, 2, ny, groups, *TILE), f32),
            pltpu.VMEM((3, 2, ny, xh_all, *TILE), f32),
            pltpu.VMEM((3, 2, ny, groups, *TILE), f32),
            pltpu.VMEM((2, 3, ny, xh_all, *TILE), f32),
            pltpu.VMEM((2, 3, ny, groups, *TILE), f32),
        ],
    )
    return disp_out, vel_out, moments_out


def solution(mesh):
    placed = P(None, "gx", "gy", "gz")
    sizes = [mesh.shape[axis] for axis in ("gx", "gy", "gz")]
    return jax.shard_map(
        functools.partial(on_device, *sizes),
        mesh=mesh,
        in_specs=(placed,) * 4 + (P(),) * 4,
        out_specs=(placed,) * 3,
        check_vma=False,
    )
```

profile of v0, /device:TPU:0, one launch (start us, length us, event | category | flops | bytes accessed | tf_op | source)
XLA Modules:
  0.0 65.6 jit_solution(12688145774918649636)
XLA Ops:
  0.6 1.7 %shard_map.103 = f32[14,8,128]{2,1,0:T(8,128)} custom-call(f32[6,4,8,128]{3,2,1,0:T(8,128)} %disp.3, f32[6,4,8,128]{3,2,1,0:T(8,128)} %mom.3, s32[2,4,8,128]{3,2,1,0:T(8,128)} %bit.1), custom_call_target="tpu_custom_call" | custom-call | tf_op jit(solution)/shard_map/pallas_call | solution.py:57
  2.4 5.1 %collective-permute-start.1 = (f32[14,8,128]{2,1,0:T(8,128)}, f32[14,8,128]{2,1,0:T(8,128)S(1)}, u32[]{:S(2)}, u32[]{:S(2)}) collective-permute-start(f32[14,8,128]{2,1,0:T(8,128)} %shard_map.103), channel_id=1, source_target_pairs={{0,3},{1,0},{2,1},{3,2},{4,7},{5,4},{6,5},{7,6},{8,11},{9,8},{10,9... | collective-permute-start | bytes 172040 | tf_op jit(solution)/shard_map/ppermute | solution.py:511
  7.5 0.0 collective-permute-start
  7.5 0.1 copy.14
  7.6 0.0 copy-start.5
  7.6 0.0 copy-start.1
  7.7 0.7 %copy-done.5 = bf16[32,256]{1,0:T(8,128)(2,1)S(1)} copy-done((bf16[32,256]{1,0:T(8,128)(2,1)S(1)}, bf16[32,256]{1,0:T(8,128)(2,1)}, u32[]{:S(2)}) %copy-start.5) | copy-done | bytes 16408
  8.4 0.1 copy.13
  8.5 1.2 %collective-permute-done.1.high = f32[14,8,128]{2,1,0:T(8,128)S(1)} collective-permute-done((f32[14,8,128]{2,1,0:T(8,128)}, f32[14,8,128]{2,1,0:T(8,128)S(1)}, u32[]{:S(2)}, u32[]{:S(2)}) %collective-permute-start.1) | collective-permute-done | bytes 57376 | tf_op jit(solution)/shard_map/ppermute | solution.py:511
  9.7 4.0 %collective-permute-done.low = f32[14,8,128]{2,1,0:T(8,128)S(1)} collective-permute-done((f32[14,8,128]{2,1,0:T(8,128)}, f32[14,8,128]{2,1,0:T(8,128)S(1)}, u32[]{:S(2)}, u32[]{:S(2)}) %collective-permute-start) | collective-permute-done | bytes 57376 | tf_op jit(solution)/shard_map/ppermute | solution.py:511
  13.7 0.1 shard_map.104
  13.8 0.1 collective-permute-start.5
  13.9 2.5 %collective-permute-start.3 = (f32[6,8,128]{2,1,0:T(8,128)S(1)}, f32[6,8,128]{2,1,0:T(8,128)S(1)}, u32[]{:S(2)}, u32[]{:S(2)}) collective-permute-start(f32[6,8,128]{2,1,0:T(8,128)S(1)} %get-tuple-element.18), channel_id=1, source_target_pairs={{0,4},{4,8},{8,12},{12,0},{16,20},{20,24},{24,28},{28,16},{1,5},{5... | collective-permute-start | bytes 73736 | tf_op jit(solution)/shard_map/ppermute | solution.py:505
  16.4 0.2 collective-permute-start.6
  16.7 0.0 copy-start.3
  16.7 0.6 collective-permute-start.4
  17.3 2.4 %collective-permute-start.9 = (f32[5,8,8,128]{3,2,1,0:T(8,128)S(1)}, f32[5,8,8,128]{3,2,1,0:T(8,128)S(1)}, u32[]{:S(2)}, u32[]{:S(2)}) collective-permute-start(f32[5,8,8,128]{3,2,1,0:T(8,128)S(1)} %get-tuple-element.24.refs_0_), channel_id=1, source_target_pairs={{0,24},{4,28},{8,16},{12,20},{16,8},{20,12},{24,0},{28,4},{1,25},{... | collective-permute-start | bytes 491528 | tf_op jit(solution)/shard_map/ppermute | solution.py:508
  19.7 0.0 collective-permute-done.5.xyup
  19.7 0.5 collective-permute-start.8
  20.2 0.0 collective-permute-done.3.yup
  20.2 0.8 %collective-permute-start.7 = (f32[5,8,8,128]{3,2,1,0:T(8,128)S(1)}, f32[5,8,8,128]{3,2,1,0:T(8,128)S(1)}, u32[]{:S(2)}, u32[]{:S(2)}) collective-permute-start(f32[5,8,8,128]{3,2,1,0:T(8,128)S(1)} %get-tuple-element.24.refs_0_), channel_id=1, source_target_pairs={{0,8},{4,12},{8,0},{12,4},{16,24},{20,28},{24,16},{28,20},{1,9},{5... | collective-permute-start | bytes 491528 | tf_op jit(solution)/shard_map/ppermute | solution.py:508
  21.0 0.0 collective-permute-done.6.xydn
  21.0 1.3 %collective-permute-start.2 = (f32[2,12,8,128]{3,2,1,0:T(8,128)S(1)}, f32[2,12,8,128]{3,2,1,0:T(8,128)S(1)}, u32[]{:S(2)}, u32[]{:S(2)}) collective-permute-start(f32[2,12,8,128]{3,2,1,0:T(8,128)S(1)} %get-tuple-element.17), channel_id=1, source_target_pairs={{0,16},{4,20},{8,24},{12,28},{16,0},{20,4},{24,8},{28,12},{1,17},{... | collective-permute-start | bytes 294920 | tf_op jit(solution)/shard_map/ppermute | solution.py:505
  22.3 0.0 collective-permute-done.4.ydn
  22.3 7.8 %collective-permute-done.2.xup.xdn = f32[2,12,8,128]{3,2,1,0:T(8,128)S(1)} collective-permute-done((f32[2,12,8,128]{3,2,1,0:T(8,128)S(1)}, f32[2,12,8,128]{3,2,1,0:T(8,128)S(1)}, u32[]{:S(2)}, u32[]{:S(2)}) %collective-permute-start.2) | collective-permute-done | bytes 98336 | tf_op jit(solution)/shard_map/ppermute | solution.py:505
  30.2 0.1 broadcast_in_dim.2.b_in
  30.3 12.2 %shard_map.105 = (f32[6,4,8,128]{3,2,1,0:T(8,128)}, f32[6,4,8,128]{3,2,1,0:T(8,128)}, f32[5,2,8,128]{3,2,1,0:T(8,128)S(1)}) custom-call(f32[6,4,8,128]{3,2,1,0:T(8,128)S(1)} %copy-done, f32[6,4,8,128]{3,2,1,0:T(8,128)S(1)} %copy-done.1, f32[6,4,8,128]{3,2,1,0:T(8,128)S(1)} %copy-done.3, f32[14,8,128]{2,1,0:T(8,128)S(1)} %get-tuple-element.16.slab, ...), custom_call_target="tpu_custom_call" | custom-call | tf_op jit(solution)/shard_map/pallas_call | solution.py:57
  42.5 0.0 collective-permute-done.9.refs_6_
  42.5 0.0 collective-permute-done.7.refs_2_
  42.5 1.5 %collective-permute-start.19 = (f32[5,2,8,128]{3,2,1,0:T(8,128)S(1)}, f32[5,2,8,128]{3,2,1,0:T(8,128)S(1)}, u32[]{:S(2)}, u32[]{:S(2)}) collective-permute-start(f32[5,2,8,128]{3,2,1,0:T(8,128)S(1)} %get-tuple-element.28.refs_8_), channel_id=1, source_target_pairs={{0,24},{4,28},{8,16},{12,20},{16,8},{20,12},{24,0},{28,4},{1,25},{... | collective-permute-start | bytes 122888 | tf_op jit(solution)/shard_map/ppermute | solution.py:508
  44.0 1.2 %collective-permute-start.17 = (f32[5,2,8,128]{3,2,1,0:T(8,128)S(1)}, f32[5,2,8,128]{3,2,1,0:T(8,128)S(1)}, u32[]{:S(2)}, u32[]{:S(2)}) collective-permute-start(f32[5,2,8,128]{3,2,1,0:T(8,128)S(1)} %get-tuple-element.28.refs_8_), channel_id=1, source_target_pairs={{0,16},{4,20},{8,24},{12,28},{16,0},{20,4},{24,8},{28,12},{1,17},{... | collective-permute-start | bytes 122888 | tf_op jit(solution)/shard_map/ppermute | solution.py:508
  45.2 0.8 %collective-permute-start.15 = (f32[5,2,8,128]{3,2,1,0:T(8,128)S(1)}, f32[5,2,8,128]{3,2,1,0:T(8,128)S(1)}, u32[]{:S(2)}, u32[]{:S(2)}) collective-permute-start(f32[5,2,8,128]{3,2,1,0:T(8,128)S(1)} %get-tuple-element.28.refs_8_), channel_id=1, source_target_pairs={{0,8},{4,12},{8,0},{12,4},{16,24},{20,28},{24,16},{28,20},{1,9},{5... | collective-permute-start | bytes 122888 | tf_op jit(solution)/shard_map/ppermute | solution.py:508
  46.1 0.0 collective-permute-start.14
  46.1 0.5 collective-permute-start.10
  46.6 1.3 %collective-permute-done.19.refs_14_ = f32[5,2,8,128]{3,2,1,0:T(8,128)S(1)} collective-permute-done((f32[5,2,8,128]{3,2,1,0:T(8,128)S(1)}, f32[5,2,8,128]{3,2,1,0:T(8,128)S(1)}, u32[]{:S(2)}, u32[]{:S(2)}) %collective-permute-start.19) | collective-permute-done | bytes 40992 | tf_op jit(solution)/shard_map/ppermute | solution.py:508
  47.9 0.3 collective-permute-done.17.refs_12_
  48.2 0.2 collective-permute-start.12
  48.4 0.8 %collective-permute-done.15.refs_10_ = f32[5,2,8,128]{3,2,1,0:T(8,128)S(1)} collective-permute-done((f32[5,2,8,128]{3,2,1,0:T(8,128)S(1)}, f32[5,2,8,128]{3,2,1,0:T(8,128)S(1)}, u32[]{:S(2)}, u32[]{:S(2)}) %collective-permute-start.15) | collective-permute-done | bytes 40992 | tf_op jit(solution)/shard_map/ppermute | solution.py:508
  49.2 0.0 collective-permute-start.13
  49.2 0.0 collective-permute-done.14.refs_9_
  49.2 0.5 collective-permute-start.20
  49.8 0.9 %collective-permute-done.20.refs_15_ = f32[5,2,8,128]{3,2,1,0:T(8,128)S(1)} collective-permute-done((f32[5,2,8,128]{3,2,1,0:T(8,128)S(1)}, f32[5,2,8,128]{3,2,1,0:T(8,128)S(1)}, u32[]{:S(2)}, u32[]{:S(2)}) %collective-permute-start.20) | collective-permute-done | bytes 40992 | tf_op jit(solution)/shard_map/ppermute | solution.py:508
  50.7 0.3 collective-permute-start.18
  51.0 0.9 %collective-permute-done.18.refs_13_ = f32[5,2,8,128]{3,2,1,0:T(8,128)S(1)} collective-permute-done((f32[5,2,8,128]{3,2,1,0:T(8,128)S(1)}, f32[5,2,8,128]{3,2,1,0:T(8,128)S(1)}, u32[]{:S(2)}, u32[]{:S(2)}) %collective-permute-start.18) | collective-permute-done | bytes 40992 | tf_op jit(solution)/shard_map/ppermute | solution.py:508
  51.9 0.3 collective-permute-start.16
  52.2 0.9 %collective-permute-done.16.refs_11_ = f32[5,2,8,128]{3,2,1,0:T(8,128)S(1)} collective-permute-done((f32[5,2,8,128]{3,2,1,0:T(8,128)S(1)}, f32[5,2,8,128]{3,2,1,0:T(8,128)S(1)}, u32[]{:S(2)}, u32[]{:S(2)}) %collective-permute-start.16) | collective-permute-done | bytes 40992 | tf_op jit(solution)/shard_map/ppermute | solution.py:508
  53.2 0.0 collective-permute-done.13.refs_7_
  53.2 12.4 %shard_map.106 = f32[6,4,8,128]{3,2,1,0:T(8,128)} custom-call(f32[5,8,8,128]{3,2,1,0:T(8,128)S(1)} %get-tuple-element.24.refs_0_, f32[5,8,8,128]{3,2,1,0:T(8,128)S(1)} %collective-permute-done.10.refs_1_, f32[5,8,8,128]{3,2,1,0:T(8,128)S(1)} %collective-permute-done.7.refs_2_, f32[5,8,8,128]{3,2,1,0:T(8,128)S(1)} %collective-permute-done.11.refs_3_, ...), custom_call_target="tpu_custom_call" | custom-call | tf_op jit(solution)/shard_map/pallas_call | solution.py:57
  (21 shorter events, 0.1 us)
Async XLA Ops:
  0.6 6.9 %copy-start.4 = (bf16[256,256]{1,0:T(8,128)(2,1)S(1)}, bf16[256,256]{1,0:T(8,128)(2,1)}, u32[]{:S(2)}) copy-start(bf16[256,256]{1,0:T(8,128)(2,1)} %param.14) | copy-start | bytes 393220
  2.4 7.3 %collective-permute-start.1 = (f32[14,8,128]{2,1,0:T(8,128)}, f32[14,8,128]{2,1,0:T(8,128)S(1)}, u32[]{:S(2)}, u32[]{:S(2)}) collective-permute-start(f32[14,8,128]{2,1,0:T(8,128)} %shard_map.103), channel_id=1, source_target_pairs={{0,3},{1,0},{2,1},{3,2},{4,7},{5,4},{6,5},{7,6},{8,11},{9,8},{10,9... | collective-permute-start | bytes 172040 | tf_op jit(solution)/shard_map/ppermute | solution.py:511
  7.5 6.2 %collective-permute-start = (f32[14,8,128]{2,1,0:T(8,128)}, f32[14,8,128]{2,1,0:T(8,128)S(1)}, u32[]{:S(2)}, u32[]{:S(2)}) collective-permute-start(f32[14,8,128]{2,1,0:T(8,128)} %shard_map.103), channel_id=1, source_target_pairs={{0,1},{1,2},{2,3},{3,0},{4,5},{5,6},{6,7},{7,4},{8,9},{9,10},{10,1... | collective-permute-start | bytes 172040 | tf_op jit(solution)/shard_map/ppermute | solution.py:511
  7.6 0.7 %copy-start.5 = (bf16[32,256]{1,0:T(8,128)(2,1)S(1)}, bf16[32,256]{1,0:T(8,128)(2,1)}, u32[]{:S(2)}) copy-start(bf16[32,256]{1,0:T(8,128)(2,1)} %param.12) | copy-start | bytes 49156
  7.6 6.1 %copy-start.1 = (f32[6,4,8,128]{3,2,1,0:T(8,128)S(1)}, f32[6,4,8,128]{3,2,1,0:T(8,128)}, u32[]{:S(2)}) copy-start(f32[6,4,8,128]{3,2,1,0:T(8,128)} %mom.3) | copy-start | bytes 294916
  8.3 5.4 %copy-start = (f32[6,4,8,128]{3,2,1,0:T(8,128)S(1)}, f32[6,4,8,128]{3,2,1,0:T(8,128)}, u32[]{:S(2)}) copy-start(f32[6,4,8,128]{3,2,1,0:T(8,128)} %disp.3) | copy-start | bytes 294916
  8.4 5.4 %copy-start.2 = (s32[2,4,8,128]{3,2,1,0:T(8,128)S(1)}, s32[2,4,8,128]{3,2,1,0:T(8,128)}, u32[]{:S(2)}) copy-start(s32[2,4,8,128]{3,2,1,0:T(8,128)} %bit.1) | copy-start | bytes 98308
  13.8 5.9 %collective-permute-start.5 = (f32[6,8,128]{2,1,0:T(8,128)S(1)}, f32[6,8,128]{2,1,0:T(8,128)S(1)}, u32[]{:S(2)}, u32[]{:S(2)}) collective-permute-start(f32[6,8,128]{2,1,0:T(8,128)S(1)} %get-tuple-element.18), channel_id=1, source_target_pairs={{0,20},{4,24},{8,28},{12,16},{16,4},{20,8},{24,12},{28,0},{1,21},{... | collective-permute-start | bytes 73736 | tf_op jit(solution)/shard_map/ppermute | solution.py:505
  13.9 6.4 %collective-permute-start.3 = (f32[6,8,128]{2,1,0:T(8,128)S(1)}, f32[6,8,128]{2,1,0:T(8,128)S(1)}, u32[]{:S(2)}, u32[]{:S(2)}) collective-permute-start(f32[6,8,128]{2,1,0:T(8,128)S(1)} %get-tuple-element.18), channel_id=1, source_target_pairs={{0,4},{4,8},{8,12},{12,0},{16,20},{20,24},{24,28},{28,16},{1,5},{5... | collective-permute-start | bytes 73736 | tf_op jit(solution)/shard_map/ppermute | solution.py:505
  16.4 4.6 %collective-permute-start.6 = (f32[6,8,128]{2,1,0:T(8,128)S(1)}, f32[6,8,128]{2,1,0:T(8,128)S(1)}, u32[]{:S(2)}, u32[]{:S(2)}) collective-permute-start(f32[6,8,128]{2,1,0:T(8,128)S(1)} %get-tuple-element.19), channel_id=1, source_target_pairs={{0,28},{4,16},{8,20},{12,24},{16,12},{20,0},{24,4},{28,8},{1,29},{... | collective-permute-start | bytes 73736 | tf_op jit(solution)/shard_map/ppermute | solution.py:505
  16.6 5.7 %copy-start.7 = (f32[256]{0:T(256)S(1)}, f32[256]{0:T(256)}, u32[]{:S(2)}) copy-start(f32[256]{0:T(256)} %param.13) | copy-start | bytes 3076
  16.6 5.7 %copy-start.6 = (bf16[256,4]{0,1:T(4,128)(2,1)S(1)}, bf16[256,4]{0,1:T(4,128)(2,1)}, u32[]{:S(2)}) copy-start(bf16[256,4]{0,1:T(4,128)(2,1)} %param.15) | copy-start | bytes 6148
  16.7 13.6 %copy-start.3 = (f32[6,4,8,128]{3,2,1,0:T(8,128)S(1)}, f32[6,4,8,128]{3,2,1,0:T(8,128)}, u32[]{:S(2)}) copy-start(f32[6,4,8,128]{3,2,1,0:T(8,128)} %vel.1) | copy-start | bytes 294916
  16.7 5.6 %collective-permute-start.4 = (f32[6,8,128]{2,1,0:T(8,128)S(1)}, f32[6,8,128]{2,1,0:T(8,128)S(1)}, u32[]{:S(2)}, u32[]{:S(2)}) collective-permute-start(f32[6,8,128]{2,1,0:T(8,128)S(1)} %get-tuple-element.19), channel_id=1, source_target_pairs={{0,12},{4,0},{8,4},{12,8},{16,28},{20,16},{24,20},{28,24},{1,13},{... | collective-permute-start | bytes 73736 | tf_op jit(solution)/shard_map/ppermute | solution.py:505
  17.3 25.2 %collective-permute-start.9 = (f32[5,8,8,128]{3,2,1,0:T(8,128)S(1)}, f32[5,8,8,128]{3,2,1,0:T(8,128)S(1)}, u32[]{:S(2)}, u32[]{:S(2)}) collective-permute-start(f32[5,8,8,128]{3,2,1,0:T(8,128)S(1)} %get-tuple-element.24.refs_0_), channel_id=1, source_target_pairs={{0,24},{4,28},{8,16},{12,20},{16,8},{20,12},{24,0},{28,4},{1,25},{... | collective-permute-start | bytes 491528 | tf_op jit(solution)/shard_map/ppermute | solution.py:508
  19.7 22.8 %collective-permute-start.8 = (f32[5,8,8,128]{3,2,1,0:T(8,128)S(1)}, f32[5,8,8,128]{3,2,1,0:T(8,128)S(1)}, u32[]{:S(2)}, u32[]{:S(2)}) collective-permute-start(f32[5,8,8,128]{3,2,1,0:T(8,128)S(1)} %get-tuple-element.24.refs_0_), channel_id=1, source_target_pairs={{0,16},{4,20},{8,24},{12,28},{16,0},{20,4},{24,8},{28,12},{1,17},{... | collective-permute-start | bytes 491528 | tf_op jit(solution)/shard_map/ppermute | solution.py:508
  20.2 22.3 %collective-permute-start.7 = (f32[5,8,8,128]{3,2,1,0:T(8,128)S(1)}, f32[5,8,8,128]{3,2,1,0:T(8,128)S(1)}, u32[]{:S(2)}, u32[]{:S(2)}) collective-permute-start(f32[5,8,8,128]{3,2,1,0:T(8,128)S(1)} %get-tuple-element.24.refs_0_), channel_id=1, source_target_pairs={{0,8},{4,12},{8,0},{12,4},{16,24},{20,28},{24,16},{28,20},{1,9},{5... | collective-permute-start | bytes 491528 | tf_op jit(solution)/shard_map/ppermute | solution.py:508
  21.0 9.1 %collective-permute-start.2 = (f32[2,12,8,128]{3,2,1,0:T(8,128)S(1)}, f32[2,12,8,128]{3,2,1,0:T(8,128)S(1)}, u32[]{:S(2)}, u32[]{:S(2)}) collective-permute-start(f32[2,12,8,128]{3,2,1,0:T(8,128)S(1)} %get-tuple-element.17), channel_id=1, source_target_pairs={{0,16},{4,20},{8,24},{12,28},{16,0},{20,4},{24,8},{28,12},{1,17},{... | collective-permute-start | bytes 294920 | tf_op jit(solution)/shard_map/ppermute | solution.py:505
  42.5 5.4 %collective-permute-start.19 = (f32[5,2,8,128]{3,2,1,0:T(8,128)S(1)}, f32[5,2,8,128]{3,2,1,0:T(8,128)S(1)}, u32[]{:S(2)}, u32[]{:S(2)}) collective-permute-start(f32[5,2,8,128]{3,2,1,0:T(8,128)S(1)} %get-tuple-element.28.refs_8_), channel_id=1, source_target_pairs={{0,24},{4,28},{8,16},{12,20},{16,8},{20,12},{24,0},{28,4},{1,25},{... | collective-permute-start | bytes 122888 | tf_op jit(solution)/shard_map/ppermute | solution.py:508
  44.0 4.2 %collective-permute-start.17 = (f32[5,2,8,128]{3,2,1,0:T(8,128)S(1)}, f32[5,2,8,128]{3,2,1,0:T(8,128)S(1)}, u32[]{:S(2)}, u32[]{:S(2)}) collective-permute-start(f32[5,2,8,128]{3,2,1,0:T(8,128)S(1)} %get-tuple-element.28.refs_8_), channel_id=1, source_target_pairs={{0,16},{4,20},{8,24},{12,28},{16,0},{20,4},{24,8},{28,12},{1,17},{... | collective-permute-start | bytes 122888 | tf_op jit(solution)/shard_map/ppermute | solution.py:508
  45.2 4.0 %collective-permute-start.15 = (f32[5,2,8,128]{3,2,1,0:T(8,128)S(1)}, f32[5,2,8,128]{3,2,1,0:T(8,128)S(1)}, u32[]{:S(2)}, u32[]{:S(2)}) collective-permute-start(f32[5,2,8,128]{3,2,1,0:T(8,128)S(1)} %get-tuple-element.28.refs_8_), channel_id=1, source_target_pairs={{0,8},{4,12},{8,0},{12,4},{16,24},{20,28},{24,16},{28,20},{1,9},{5... | collective-permute-start | bytes 122888 | tf_op jit(solution)/shard_map/ppermute | solution.py:508
  46.1 3.2 %collective-permute-start.14 = (f32[5,2,8,128]{3,2,1,0:T(8,128)S(1)}, f32[5,2,8,128]{3,2,1,0:T(8,128)S(1)}, u32[]{:S(2)}, u32[]{:S(2)}) collective-permute-start(f32[5,2,8,128]{3,2,1,0:T(8,128)S(1)} %get-tuple-element.28.refs_8_), channel_id=1, source_target_pairs={{0,4},{4,0},{8,12},{12,8},{16,20},{20,16},{24,28},{28,24},{1,5},{5... | collective-permute-start | bytes 122888 | tf_op jit(solution)/shard_map/ppermute | solution.py:508
  46.1 7.1 %collective-permute-start.10 = (f32[5,8,8,128]{3,2,1,0:T(8,128)S(1)}, f32[5,8,8,128]{3,2,1,0:T(8,128)S(1)}, u32[]{:S(2)}, u32[]{:S(2)}) collective-permute-start(f32[5,8,8,128]{3,2,1,0:T(8,128)S(1)} %get-tuple-element.24.refs_0_), channel_id=1, source_target_pairs={{0,4},{4,0},{8,12},{12,8},{16,20},{20,16},{24,28},{28,24},{1,5},{5... | collective-permute-start | bytes 491528 | tf_op jit(solution)/shard_map/ppermute | solution.py:508
  47.9 5.2 %collective-permute-start.11 = (f32[5,8,8,128]{3,2,1,0:T(8,128)S(1)}, f32[5,8,8,128]{3,2,1,0:T(8,128)S(1)}, u32[]{:S(2)}, u32[]{:S(2)}) collective-permute-start(f32[5,8,8,128]{3,2,1,0:T(8,128)S(1)} %collective-permute-done.7.refs_2_), channel_id=1, source_target_pairs={{0,4},{4,0},{8,12},{12,8},{16,20},{20,16},{24,28},{28,24},{1,5},{5... | collective-permute-start | bytes 491528 | tf_op jit(solution)/shard_map/ppermute | solution.py:508
  48.2 4.9 %collective-permute-start.12 = (f32[5,8,8,128]{3,2,1,0:T(8,128)S(1)}, f32[5,8,8,128]{3,2,1,0:T(8,128)S(1)}, u32[]{:S(2)}, u32[]{:S(2)}) collective-permute-start(f32[5,8,8,128]{3,2,1,0:T(8,128)S(1)} %collective-permute-done.8.refs_4_), channel_id=1, source_target_pairs={{0,4},{4,0},{8,12},{12,8},{16,20},{20,16},{24,28},{28,24},{1,5},{5... | collective-permute-start | bytes 491528 | tf_op jit(solution)/shard_map/ppermute | solution.py:508
  49.2 3.9 %collective-permute-start.13 = (f32[5,8,8,128]{3,2,1,0:T(8,128)S(1)}, f32[5,8,8,128]{3,2,1,0:T(8,128)S(1)}, u32[]{:S(2)}, u32[]{:S(2)}) collective-permute-start(f32[5,8,8,128]{3,2,1,0:T(8,128)S(1)} %collective-permute-done.9.refs_6_), channel_id=1, source_target_pairs={{0,4},{4,0},{8,12},{12,8},{16,20},{20,16},{24,28},{28,24},{1,5},{5... | collective-permute-start | bytes 491528 | tf_op jit(solution)/shard_map/ppermute | solution.py:508
  49.2 1.4 %collective-permute-start.20 = (f32[5,2,8,128]{3,2,1,0:T(8,128)S(1)}, f32[5,2,8,128]{3,2,1,0:T(8,128)S(1)}, u32[]{:S(2)}, u32[]{:S(2)}) collective-permute-start(f32[5,2,8,128]{3,2,1,0:T(8,128)S(1)} %collective-permute-done.19.refs_14_), channel_id=1, source_target_pairs={{0,4},{4,0},{8,12},{12,8},{16,20},{20,16},{24,28},{28,24},{1,5},{5... | collective-permute-start | bytes 122888 | tf_op jit(solution)/shard_map/ppermute | solution.py:508
  50.7 1.2 %collective-permute-start.18 = (f32[5,2,8,128]{3,2,1,0:T(8,128)S(1)}, f32[5,2,8,128]{3,2,1,0:T(8,128)S(1)}, u32[]{:S(2)}, u32[]{:S(2)}) collective-permute-start(f32[5,2,8,128]{3,2,1,0:T(8,128)S(1)} %collective-permute-done.17.refs_12_), channel_id=1, source_target_pairs={{0,4},{4,0},{8,12},{12,8},{16,20},{20,16},{24,28},{28,24},{1,5},{5... | collective-permute-start | bytes 122888 | tf_op jit(solution)/shard_map/ppermute | solution.py:508
  51.9 1.2 %collective-permute-start.16 = (f32[5,2,8,128]{3,2,1,0:T(8,128)S(1)}, f32[5,2,8,128]{3,2,1,0:T(8,128)S(1)}, u32[]{:S(2)}, u32[]{:S(2)}) collective-permute-start(f32[5,2,8,128]{3,2,1,0:T(8,128)S(1)} %collective-permute-done.15.refs_10_), channel_id=1, source_target_pairs={{0,4},{4,0},{8,12},{12,8},{16,20},{20,16},{24,28},{28,24},{1,5},{5... | collective-permute-start | bytes 122888 | tf_op jit(solution)/shard_map/ppermute | solution.py:508
where the time goes:
time: 65.8 us; the launch traced here: 65.6 us
  Pallas kernels  26.5 us (40%)
  starting transfers between devices  18.9 us (29%)
  waiting for transfers between devices  18.4 us (28%)
  local copies, waits for them, and re-layouts  0.99 us (2%)
  between operations  0.77 us (1%)
    pallas_call x4, Pallas kernels, vmem_call(): pl.pallas_call(body, out_shape=tuple((jax.ShapeDtypeStruct(s, d) for s, d...  26.5 us
    ppermute x14, starting transfers between devices, swap(): return lax.ppermute(v, plane, pairs(lambda x, y: (x ^ mx, y ^ my)))  9.1 us
    ppermute x5, waiting for transfers between devices, shift(): return lax.ppermute(v, plane, pairs(lambda x, y: (x + dx, y + dy)))  7.84 us
    ppermute x14, waiting for transfers between devices, swap(): return lax.ppermute(v, plane, pairs(lambda x, y: (x ^ mx, y ^ my)))  5.28 us
    ppermute x2, waiting for transfers between devices, along_z(): return lax.ppermute(v, 'gz', [(i, (i + step) % nz) for i in range(nz)])  5.25 us
    ppermute x2, starting transfers between devices, along_z(): return lax.ppermute(v, 'gz', [(i, (i + step) % nz) for i in range(nz)])  5.13 us
    ppermute x5, starting transfers between devices, shift(): return lax.ppermute(v, plane, pairs(lambda x, y: (x + dx, y + dy)))  4.67 us
  transfers between devices with their start and end apart: 21, of which 9 were waited for; matrix products, arithmetic and copies ran while one was open for 0% of the time, Pallas kernels for 19%

commit v1 on v0

--- a/solution.py
+++ b/solution.py
@@ -65,7 +65,7 @@
     )(*args)
 
 
-def pack_body(disp_in, mom_in, bit_in, out, disp, mom, bit, sems):
+def pack_body(disp_in, mom_in, bit_in, out, brick, disp, mom, bit, sems):
     copies = [
         pltpu.make_async_copy(source, target, sems.at[n])
         for n, (source, target) in enumerate(((disp_in, disp), (mom_in, mom), (bit_in, bit)))
@@ -82,23 +82,20 @@
         else:
             tiles = [bit[i - 12, x].astype(f32) for x in ORDER]
         out[i] = merge_blocks(tiles)
-
-
-def halo_body(disp, mom, bit, low, high, slab, brick, faces, yup, ydn):
-    upper = (iota(1) & (SLAB - 1)) >= SLAB // 2
     e0 = odd_mask(0)
-    for i in range(14):
-        slab[i] = jnp.where(upper, low[i], high[i])
     for p in range(2):
         for k in range(4):
-            i = 6 + 3 * p + k if k < 3 else 12 + p
             tiles = [mom[3 * p + k, x] if k < 3 else bit[p, x].astype(f32) for x in range(XL)]
             for xh in range(2):
                 even, odd = tiles[2 * xh], tiles[2 * xh + 1]
                 brick[xh, 4 * p + k] = jnp.where(e0, odd, even)
                 brick[2 + xh, 4 * p + k] = jnp.where(e0, even, odd)
-            h = slab[i]
-            brick[4, 4 * p + k] = jnp.where(e0, lanes(h, 64), h)
+
+
+def halo_body(disp, mom, low, high, slab, faces, yup, ydn):
+    upper = (iota(1) & (SLAB - 1)) >= SLAB // 2
+    for i in range(14):
+        slab[i] = jnp.where(upper, low[i], high[i])
     for i in range(6):
         src = disp if i < 3 else mom
         k = i % 3
@@ -116,7 +113,8 @@
         ydn[i, XL : XL + 1, :] = slab[base + k, 0:1, :]
 
 
-def near_tiles(p, disp, mom, slab, xf, yr, xyr, near):
+def near_tiles(p, disp, mom, slab, halo, near):
+    xf, yr, xyr = halo or (None, None, None)
     q = 1 - p
     lane, sub = iota(1), iota(0)
     block = lane_block()
@@ -126,7 +124,7 @@
         k = i % 3
         c = [src[3 * q + k, x] for x in range(XL)]
         h = slab[(0 if i < 3 else 6) + 3 * q + k]
-        fc, fh = xf[2 * i], xf[2 * i + 1]
+        fc, fh = (xf[2 * i], xf[2 * i + 1]) if halo else (None, None)
 
         def wide(row):
             return jnp.broadcast_to(row, TILE)
@@ -135,10 +133,13 @@
             if dy:
                 step = 1 if p == 0 else -1
                 put = sub == (0 if p == 0 else SUB - 1)
-                c = [jnp.where(put, wide(yr[i, x : x + 1, :]), rows(c[x], step)) for x in range(XL)]
-                h = jnp.where(put, wide(yr[i, XL : XL + 1, :]), rows(h, step))
-                fc = jnp.where(put, wide(xyr[i, edge_x : edge_x + 1, :]), rows(fc, step))
-                fh = jnp.where(put, wide(xyr[i, XL : XL + 1, :]), rows(fh, step))
+                c = [rows(c[x], step) for x in range(XL)]
+                h = rows(h, step)
+                if halo:
+                    c = [jnp.where(put, wide(yr[i, x : x + 1, :]), c[x]) for x in range(XL)]
+                    h = jnp.where(put, wide(yr[i, XL : XL + 1, :]), h)
+                    fc = jnp.where(put, wide(xyr[i, edge_x : edge_x + 1, :]), rows(fc, step))
+                    fh = jnp.where(put, wide(xyr[i, XL : XL + 1, :]), rows(fh, step))
             for dz in range(2):
                 if dz == 0:
                     cs, hs, fcs, fhs = c, h, fc, fh
@@ -151,13 +152,16 @@
                         lanes(jnp.where(at_seam, lanes(h, -SLAB * ORDER[x]), c[x]), step)
                         for x in range(XL)
                     ]
-                    hs = lanes(jnp.where(at_seams, merge_blocks([c[x] for x in ORDER]), h), step)
-                    fcs = lanes(jnp.where(at_seam, lanes(fh, -SLAB * ORDER[edge_x]), fc), step)
-                    fhs = lanes(jnp.where(at_seams, lanes(fc, SLAB * ORDER[edge_x]), fh), step)
+                    if halo:
+                        hs = lanes(jnp.where(at_seams, merge_blocks([c[x] for x in ORDER]), h), step)
+                        fcs = lanes(jnp.where(at_seam, lanes(fh, -SLAB * ORDER[edge_x]), fc), step)
+                        fhs = lanes(jnp.where(at_seams, lanes(fc, SLAB * ORDER[edge_x]), fh), step)
                 at = 2 * dy + dz
-                line = [fcs] + cs if p == 0 else cs + [fcs]
-                for j in range(XL + 1):
-                    near[i, at, j] = line[j]
+                for x in range(XL):
+                    near[i, at, x + 1 - p] = cs[x]
+                if not halo:
+                    continue
+                near[i, at, XL * p] = fcs
                 near[i, at, XL + 1] = hs
                 if p == 0:
                     moved = jnp.where(block == 0, lanes(fhs, SLAB), lanes(hs, 2 * SLAB))
@@ -168,8 +172,8 @@
                 near[i, at, XL + 2] = moved
 
 
-def feature_rows(p, disp, mom, slab, near, table):
-    for slot in range(XL + 1):
+def feature_rows(p, disp, mom, slab, near, table, slots):
+    for slot in slots:
         if slot < XL:
             own = [disp[3 * p + k, slot] for k in range(3)]
             own += [mom[3 * p + k, slot] for k in range(3)]
@@ -191,24 +195,24 @@
     return (u + u * jnp.tanh(u)).astype(bf16)
 
 
-def perceptron(table, heads, w_in, b_in, w_mid, w_out, one, two, count):
-    def step(slot, carry):
-        source = jnp.minimum(slot, count - 1)
-        before = jnp.where(slot == 0, count, slot - 1)
-        for c in range(4):
-            block = jnp.concatenate(
-                [
+def perceptron(table, heads, w_in, b_in, w_mid, w_out, one, two, row_of, total, unroll):
+    slots = 2 * XL + 2
+    chunks = total // 2
+
+    def step(i, carry):
+        for c in range(unroll):
+            now = i * unroll + c
+            source = jnp.minimum(now, chunks - 1)
+            parts = []
+            for j in range(2):
+                slot, y = row_of(2 * source + j)
+                parts.append(
                     jnp.concatenate(
-                        [
-                            table[source, pl.ds(SUB * SUB * m + 2 * c + j, SUB, stride=SUB), :]
-                            for m in range(4)
-                        ],
+                        [table[slot, pl.ds(SUB * SUB * m + y, SUB, stride=SUB), :] for m in range(4)],
                         axis=0,
                     )
-                    for j in range(2)
-                ],
-                axis=1,
-            ).astype(bf16)
+                )
+            block = jnp.concatenate(parts, axis=1).astype(bf16)
             bias = b_in[...]
             hidden, last = one[...], two[...]
             u = jnp.dot(w_in[...], block, preferred_element_type=f32)
@@ -217,28 +221,58 @@
             out = jnp.dot(w_out[...], last, preferred_element_type=f32)
             one[...] = silu_half(u)
             two[...] = silu_half(v)
-            done = 2 * c - 4 if c >= 2 else 2 * c + 4
-            target = slot if c >= 2 else before
+            done = now - 2
             for j in range(2):
-                heads[target, pl.ds(done + j, SUB, stride=SUB), :] = out[:, LANE * j : LANE * (j + 1)]
+                slot, y = row_of(2 * jnp.clip(done, 0, chunks - 1) + j)
+                slot = jnp.where((done >= 0) & (done < chunks), slot, slots)
+                heads[slot, pl.ds(y, SUB, stride=SUB), :] = out[:, LANE * j : LANE * (j + 1)]
         return carry
 
     one[...] = jnp.zeros(one.shape, bf16)
     two[...] = jnp.zeros(two.shape, bf16)
-    lax.fori_loop(0, count + 1, step, 0)
-
-
-def network_body(
-    disp, mom, vel, slab, xup, xdn, yup, ydn, xyup, xydn, w_in, b_in, w_mid, w_out,
+    lax.fori_loop(0, -(-(chunks + 2) // unroll), step, 0)
+
+
+def inner_row(n):
+    slot, y = n // (SUB - 1), n % (SUB - 1)
+    p = (slot >= XL - 1).astype(jnp.int32)
+    return slot + 1 + p, y + 1 - p
+
+
+def outer_row(n):
+    each = 2 * SUB + XL - 1
+    p = (n >= each).astype(jnp.int32)
+    t = n - p * each
+    face, slab = t < SUB, t < 2 * SUB
+    slot = jnp.where(face, (XL - 1) * p, jnp.where(slab, XL, t - 2 * SUB + 1 - p))
+    y = jnp.where(face, t, jnp.where(slab, t - SUB, (SUB - 1) * p))
+    return slot + (XL + 1) * p, y
+
+
+def inner_body(disp, mom, slab, w_in, b_in, w_mid, w_out, heads, near, table, one, two):
+    for p in range(2):
+        near_tiles(p, disp, mom, slab, None, near)
+        inner = range(1, XL) if p == 0 else range(XL - 1)
+        feature_rows(p, disp, mom, slab, near, table.at[pl.ds((XL + 1) * p, XL + 1)], inner)
+    total = 2 * (XL - 1) * (SUB - 1)
+    perceptron(table, heads, w_in, b_in, w_mid, w_out, one, two, inner_row, total, 4)
+
+
+def outer_body(
+    disp, mom, vel, slab, xup, xdn, yup, ydn, xyup, xydn, w_in, b_in, w_mid, w_out, inner,
     disp_out, vel_out, cbrick, near, table, heads, one, two,
 ):
     e0 = odd_mask(0)
     slots = XL + 1
+    for n in range(2 * slots):
+        heads[n] = inner[n]
     for p in range(2):
         args = (xup.at[0], yup, xyup) if p == 0 else (xdn.at[xdn.shape[0] - 1], ydn, xydn)
-        near_tiles(p, disp, mom, slab, *args, near)
-        feature_rows(p, disp, mom, slab, near, table.at[pl.ds(slots * p, slots)])
-    perceptron(table, heads, w_in, b_in, w_mid, w_out, one, two, 2 * slots)
+        near_tiles(p, disp, mom, slab, args, near)
+        part = table.at[pl.ds(slots * p, slots)]
+        feature_rows(p, disp, mom, slab, near, part, range(slots))
+    total = 2 * (2 * SUB + XL - 1)
+    perceptron(table, heads, w_in, b_in, w_mid, w_out, one, two, outer_row, total, 3)
     for p in range(2):
         coupling = []
         for slot in range(slots):
@@ -251,9 +285,12 @@
                     disp_out[3 * p + k, slot] = disp[3 * p + k, slot] + lattice_step * v
         for xh in range(2):
             even, odd = coupling[2 * xh], coupling[2 * xh + 1]
-            cbrick[xh, p] = jnp.where(e0, odd, even)
-            cbrick[2 + xh, p] = jnp.where(e0, even, odd)
-        cbrick[4, p] = jnp.where(e0, lanes(coupling[4], 64), coupling[4])
+            cbrick[2 * xh + p] = jnp.where(e0, odd, even)
+            cbrick[2 * (2 + xh) + p] = jnp.where(e0, even, odd)
+        cbrick[8 + p] = jnp.where(e0, lanes(coupling[4], 64), coupling[4])
+        for k in range(4):
+            h = slab[6 + 3 * p + k if k < 3 else 12 + p]
+            cbrick[10 + 4 * p + k] = jnp.where(e0, lanes(h, 64), h)
 
 
 def even_fit(func, terms):
@@ -309,15 +346,17 @@
     def row_mask(r, par):
         return ((lane + (r + par)) & 1) == 1
 
-    def place(source, comps):
+    def own_rows(by):
+        return pl.ds(pl.multiple_of(by * SUB, SUB), SUB)
+
+    def place(comps, cell, slab):
         for n, (mx, my) in enumerate(masks):
             bx, by = ix ^ mx, iy ^ my
-            own_rows = pl.ds(pl.multiple_of(by * SUB, SUB), SUB)
             for k in range(comps):
                 for par in range(2):
                     for xh in range(2):
-                        sc[par, k, 2 * bx + xh, own_rows, :] = source[n][2 * par + xh, k]
-                sh[k, bx, own_rows, :] = source[n][4, k]
+                        sc[par, k, 2 * bx + xh, own_rows(by), :] = cell(n, 2 * par + xh, k)
+                sh[k, bx, own_rows(by), :] = slab(n, k)
 
     def spread(comps, put_c, put_h):
         for k in range(comps):
@@ -464,9 +503,9 @@
         sweep(0, 3 - i, unit)
         return carry
 
-    place(bricks, 8)
+    place(8, lambda n, at, k: bricks[n][at, k], lambda n, k: cbricks[n][10 + k])
     spread(8, put_mc, put_mh)
-    place(cbricks, 2)
+    place(2, lambda n, at, k: cbricks[n][2 * at + k], lambda n, k: cbricks[n][8 + k])
     spread(2, put_cc, put_ch)
     near_total(0)
     lax.fori_loop(0, 4, climb, 0)
@@ -481,9 +520,8 @@
                 for xh in range(2):
                     for r in range(ny):
                         sc[par, k, xh, pl.ds(r, SUB, stride=ny), :] = mc[p, par, k, r, 2 * ix + xh]
-            own_rows = pl.ds(pl.multiple_of(iy * SUB, SUB), SUB)
             for xh in range(2):
-                zero, one = sc[0, k, xh, own_rows, :], sc[1, k, xh, own_rows, :]
+                zero, one = sc[0, k, xh, own_rows(iy), :], sc[1, k, xh, own_rows(iy), :]
                 out[3 * p + k, 2 * xh] = jnp.where(e0, one, zero)
                 out[3 * p + k, 2 * xh + 1] = jnp.where(e0, zero, one)
 
@@ -516,8 +554,8 @@
     hidden = weight_mid.shape[0]
     b_in = jnp.broadcast_to((0.5 * bias_in)[:, None], (hidden, LANE))
 
-    (packed,) = vmem_call(
-        pack_body, [((14, *TILE), f32)], displacement, moments, sector_bit,
+    packed, brick = vmem_call(
+        pack_body, [((14, *TILE), f32), ((4, 8, *TILE), f32)], displacement, moments, sector_bit,
         space=pltpu.HBM,
         grant=60 << 20,
         scratch=[
@@ -528,10 +566,14 @@
         ],
     )
     low, high = along_z(packed, 1), along_z(packed, -1)
-    slab, brick, faces, yup, ydn = vmem_call(
+    far = [(mx, my) for mx in range(nx) for my in range(0, ny, 2) if mx or my]
+    held = {(0, 0): brick}
+    for mask in far:
+        held[mask] = swap(brick, *mask)
+    slab, faces, yup, ydn = vmem_call(
         halo_body,
-        [((14, *TILE), f32), ((5, 8, *TILE), f32)] + [((2, 12, *TILE), f32)] + [((6, *TILE), f32)] * 2,
-        displacement, moments, sector_bit, low, high,
+        [((14, *TILE), f32), ((2, 12, *TILE), f32)] + [((6, *TILE), f32)] * 2,
+        displacement, moments, low, high,
     )
     if nx == 2:
         faces = shift(faces, 1, 0)
@@ -541,22 +583,24 @@
     xyup, xydn = shift(yup, 1, 1), shift(ydn, -1, -1)
     yup, ydn = shift(yup, 0, 1), shift(ydn, 0, -1)
 
-    far = [(mx, my) for mx in range(nx) for my in range(0, ny, 2) if mx or my]
-    held = {(0, 0): brick}
-    for mask in far:
-        held[mask] = swap(brick, *mask)
-
+    weights = (w_in, b_in, w_mid, w_out)
+    work = [
+        pltpu.VMEM((6, 4, XL + 3, *TILE), f32),
+        pltpu.VMEM((2 * XL + 2, 32 * SUB, LANE), f32),
+        pltpu.VMEM((2 * XL + 3, SUB * SUB, LANE), f32),
+        pltpu.VMEM((hidden, 2 * LANE), bf16),
+        pltpu.VMEM((hidden, 2 * LANE), bf16),
+    ]
+    (inner,) = vmem_call(
+        inner_body, [((2 * XL + 3, SUB * SUB, LANE), f32)], displacement, moments, slab, *weights,
+        scratch=work[:2] + work[3:],
+        cost=pl.CostEstimate(flops=10**9, bytes_accessed=2 << 20, transcendentals=3 << 20),
+    )
     disp_out, vel_out, cbrick = vmem_call(
-        network_body,
-        [((6, XL, *TILE), f32), ((6, XL, *TILE), f32), ((5, 2, *TILE), f32)],
-        displacement, moments, velocity, slab, xup, xdn, yup, ydn, xyup, xydn, w_in, b_in, w_mid, w_out,
-        scratch=[
-            pltpu.VMEM((6, 4, XL + 3, *TILE), f32),
-            pltpu.VMEM((2 * XL + 2, 32 * SUB, LANE), f32),
-            pltpu.VMEM((2 * XL + 3, SUB * SUB, LANE), f32),
-            pltpu.VMEM((hidden, 2 * LANE), bf16),
-            pltpu.VMEM((hidden, 2 * LANE), bf16),
-        ],
+        outer_body,
+        [((6, XL, *TILE), f32), ((6, XL, *TILE), f32), ((18, *TILE), f32)],
+        displacement, moments, velocity, slab, xup, xdn, yup, ydn, xyup, xydn, *weights, inner,
+        scratch=work,
     )
     near_masks = [(0, 0)] + far
     late = lax.optimization_barrier((cbrick, *[held[m] for m in near_masks]))

time: 65.8 us -> 58 us (0.88)
  waiting for transfers between devices: 18.4 us -> 9.41 us
  Pallas kernels: 26.5 us -> 27.7 us
    ppermute x5, waiting for transfers between devices: 7.84 us -> 3.49 us  [shift(): return lax.ppermute(v, plane, pairs(lambda x, y: (x + dx, y + dy)))]
    ppermute x2, waiting for transfers between devices: 5.25 us -> 1.75 us  [along_z(): return lax.ppermute(v, 'gz', [(i, (i + step) % nz) for i in range(nz)])]
    pallas_call x4 -> x5, Pallas kernels: 26.5 us -> 27.7 us  [vmem_call(): pl.pallas_call(body, out_shape=tuple((jax.ShapeDtypeStruct(s, d) for s, d...]
    ppermute x14, waiting for transfers between devices: 5.28 us -> 4.17 us  [swap(): return lax.ppermute(v, plane, pairs(lambda x, y: (x ^ mx, y ^ my)))]
  transfers between devices with their start and end apart: 21 -> 21, of which waited for: 9 -> 11; matrix products, arithmetic and copies ran while one was open for 0% -> 1% of each run, Pallas kernels for 19% -> 24%
where the time goes in v1:
time: 58 us; the launch traced here: 57.7 us
  Pallas kernels  27.7 us (48%)
  starting transfers between devices  18.7 us (32%)
  waiting for transfers between devices  9.41 us (16%)
  local copies, waits for them, and re-layouts  0.99 us (2%)
  between operations  0.79 us (1%)
    pallas_call x5, Pallas kernels, vmem_call(): pl.pallas_call(body, out_shape=tuple((jax.ShapeDtypeStruct(s, d) for s, d...  27.7 us
    ppermute x14, starting transfers between devices, swap(): return lax.ppermute(v, plane, pairs(lambda x, y: (x ^ mx, y ^ my)))  8.58 us
    ppermute x2, starting transfers between devices, along_z(): return lax.ppermute(v, 'gz', [(i, (i + step) % nz) for i in range(nz)])  5.13 us
    ppermute x5, starting transfers between devices, shift(): return lax.ppermute(v, plane, pairs(lambda x, y: (x + dx, y + dy)))  5.02 us
    ppermute x14, waiting for transfers between devices, swap(): return lax.ppermute(v, plane, pairs(lambda x, y: (x ^ mx, y ^ my)))  4.17 us
    ppermute x5, waiting for transfers between devices, shift(): return lax.ppermute(v, plane, pairs(lambda x, y: (x + dx, y + dy)))  3.49 us
    ppermute x2, waiting for transfers between devices, along_z(): return lax.ppermute(v, 'gz', [(i, (i + step) % nz) for i in range(nz)])  1.75 us
  transfers between devices with their start and end apart: 21, of which 11 were waited for; matrix products, arithmetic and copies ran while one was open for 1% of the time, Pallas kernels for 24%

profile of v1, /device:TPU:0, one launch (start us, length us, event | category | flops | bytes accessed | tf_op | source)
XLA Modules:
  0.0 57.7 jit_solution(8005821462663312498)
XLA Ops:
  0.6 1.7 %shard_map.103 = (f32[14,8,128]{2,1,0:T(8,128)}, f32[4,8,8,128]{3,2,1,0:T(8,128)}) custom-call(f32[6,4,8,128]{3,2,1,0:T(8,128)} %disp.5, f32[6,4,8,128]{3,2,1,0:T(8,128)} %mom.5, s32[2,4,8,128]{3,2,1,0:T(8,128)} %bit_in.1), custom_call_target="tpu_custom_call" | custom-call | tf_op jit(solution)/shard_map/pallas_call | solution.py:57
  2.4 5.1 %collective-permute-start.1 = (f32[14,8,128]{2,1,0:T(8,128)}, f32[14,8,128]{2,1,0:T(8,128)S(1)}, u32[]{:S(2)}, u32[]{:S(2)}) collective-permute-start(f32[14,8,128]{2,1,0:T(8,128)} %get-tuple-element.17), channel_id=1, source_target_pairs={{0,3},{1,0},{2,1},{3,2},{4,7},{5,4},{6,5},{7,6},{8,11},{9,8},{10,9... | collective-permute-start | bytes 172040 | tf_op jit(solution)/shard_map/ppermute | solution.py:549
  7.5 0.0 collective-permute-start
  7.5 2.4 %collective-permute-start.9 = (f32[4,8,8,128]{3,2,1,0:T(8,128)}, f32[4,8,8,128]{3,2,1,0:T(8,128)S(1)}, u32[]{:S(2)}, u32[]{:S(2)}) collective-permute-start(f32[4,8,8,128]{3,2,1,0:T(8,128)} %get-tuple-element.26.refs_0_), channel_id=1, source_target_pairs={{0,24},{4,28},{8,16},{12,20},{16,8},{20,12},{24,0},{28,4},{1,25},{... | collective-permute-start | bytes 393224 | tf_op jit(solution)/shard_map/ppermute | solution.py:546
  10.0 0.5 collective-permute-start.8
  10.5 0.5 collective-permute-start.7
  11.0 0.1 copy.14
  11.1 0.0 copy-start.5
  11.1 0.0 copy-start.1
  11.2 0.7 %copy-done.5 = bf16[32,256]{1,0:T(8,128)(2,1)S(1)} copy-done((bf16[32,256]{1,0:T(8,128)(2,1)S(1)}, bf16[32,256]{1,0:T(8,128)(2,1)}, u32[]{:S(2)}) %copy-start.5) | copy-done | bytes 16408
  11.8 0.1 copy.13
  11.9 0.0 collective-permute-done.1.high
  12.0 1.7 %collective-permute-done.low = f32[14,8,128]{2,1,0:T(8,128)S(1)} collective-permute-done((f32[14,8,128]{2,1,0:T(8,128)}, f32[14,8,128]{2,1,0:T(8,128)S(1)}, u32[]{:S(2)}, u32[]{:S(2)}) %collective-permute-start) | collective-permute-done | bytes 57376 | tf_op jit(solution)/shard_map/ppermute | solution.py:549
  13.7 0.1 collective-permute-start.5
  13.8 2.5 %collective-permute-start.3 = (f32[6,8,128]{2,1,0:T(8,128)S(1)}, f32[6,8,128]{2,1,0:T(8,128)S(1)}, u32[]{:S(2)}, u32[]{:S(2)}) collective-permute-start(f32[6,8,128]{2,1,0:T(8,128)S(1)} %get-tuple-element.20), channel_id=1, source_target_pairs={{0,4},{4,8},{8,12},{12,0},{16,20},{20,24},{24,28},{28,16},{1,5},{5... | collective-permute-start | bytes 73736 | tf_op jit(solution)/shard_map/ppermute | solution.py:543
  16.4 1.6 %collective-permute-done.5.xyup = f32[6,8,128]{2,1,0:T(8,128)S(1)} collective-permute-done((f32[6,8,128]{2,1,0:T(8,128)S(1)}, f32[6,8,128]{2,1,0:T(8,128)S(1)}, u32[]{:S(2)}, u32[]{:S(2)}) %collective-permute-start.5) | collective-permute-done | bytes 24608 | tf_op jit(solution)/shard_map/ppermute | solution.py:543
  18.0 0.0 collective-permute-start.6
  18.0 0.3 collective-permute-done.3.yup
  18.3 1.3 %collective-permute-start.2 = (f32[2,12,8,128]{3,2,1,0:T(8,128)S(1)}, f32[2,12,8,128]{3,2,1,0:T(8,128)S(1)}, u32[]{:S(2)}, u32[]{:S(2)}) collective-permute-start(f32[2,12,8,128]{3,2,1,0:T(8,128)S(1)} %get-tuple-element.19), channel_id=1, source_target_pairs={{0,16},{4,20},{8,24},{12,28},{16,0},{20,4},{24,8},{28,12},{1,17},{... | collective-permute-start | bytes 294920 | tf_op jit(solution)/shard_map/ppermute | solution.py:543
  19.6 1.6 %collective-permute-done.6.xydn = f32[6,8,128]{2,1,0:T(8,128)S(1)} collective-permute-done((f32[6,8,128]{2,1,0:T(8,128)S(1)}, f32[6,8,128]{2,1,0:T(8,128)S(1)}, u32[]{:S(2)}, u32[]{:S(2)}) %collective-permute-start.6) | collective-permute-done | bytes 24608 | tf_op jit(solution)/shard_map/ppermute | solution.py:543
  21.2 1.1 %collective-permute-start.4 = (f32[6,8,128]{2,1,0:T(8,128)S(1)}, f32[6,8,128]{2,1,0:T(8,128)S(1)}, u32[]{:S(2)}, u32[]{:S(2)}) collective-permute-start(f32[6,8,128]{2,1,0:T(8,128)S(1)} %get-tuple-element.21), channel_id=1, source_target_pairs={{0,12},{4,0},{8,4},{12,8},{16,28},{20,16},{24,20},{28,24},{1,13},{... | collective-permute-start | bytes 73736 | tf_op jit(solution)/shard_map/ppermute | solution.py:543
  22.3 0.1 broadcast_in_dim.2.b_in
  22.4 0.0 copy-start.3
  22.4 4.9 %shard_map.105.inner = f32[11,64,128]{2,1,0:T(8,128)S(1)} custom-call(f32[6,4,8,128]{3,2,1,0:T(8,128)S(1)} %copy-done, f32[6,4,8,128]{3,2,1,0:T(8,128)S(1)} %copy-done.1, f32[14,8,128]{2,1,0:T(8,128)S(1)} %get-tuple-element.18.slab, bf16[256,32]{1,0:T(8,128)(2,1)S(1)} %fusion.1.w_in, f32[256,128]{1,0:T(8,128)S(1)} %broadcast_in_dim.2.b_in, ...), custom_call_target="tpu_custom_call" | custom-call | flops 1000000000 | bytes 2097152 | tf_op jit(solution)/shard_map/pallas_call | solution.py:57
  27.4 0.0 collective-permute-done.4.ydn
  27.4 0.0 collective-permute-done.2.xup.xdn
  27.4 8.7 %shard_map.106 = (f32[6,4,8,128]{3,2,1,0:T(8,128)}, f32[6,4,8,128]{3,2,1,0:T(8,128)}, f32[18,8,128]{2,1,0:T(8,128)S(1)}) custom-call(f32[6,4,8,128]{3,2,1,0:T(8,128)S(1)} %copy-done, f32[6,4,8,128]{3,2,1,0:T(8,128)S(1)} %copy-done.1, f32[6,4,8,128]{3,2,1,0:T(8,128)S(1)} %copy-done.3, f32[14,8,128]{2,1,0:T(8,128)S(1)} %get-tuple-element.18.slab, ...), custom_call_target="tpu_custom_call" | custom-call | tf_op jit(solution)/shard_map/pallas_call | solution.py:57
  36.0 0.0 collective-permute-done.9.refs_6_
  36.1 0.0 collective-permute-done.8.refs_4_
  36.1 0.0 collective-permute-done.7.refs_2_
  36.1 1.4 %collective-permute-start.19 = (f32[18,8,128]{2,1,0:T(8,128)S(1)}, f32[18,8,128]{2,1,0:T(8,128)S(1)}, u32[]{:S(2)}, u32[]{:S(2)}) collective-permute-start(f32[18,8,128]{2,1,0:T(8,128)S(1)} %get-tuple-element.30.refs_8_), channel_id=1, source_target_pairs={{0,24},{4,28},{8,16},{12,20},{16,8},{20,12},{24,0},{28,4},{1,25},{... | collective-permute-start | bytes 221192 | tf_op jit(solution)/shard_map/ppermute | solution.py:546
  37.5 1.6 %collective-permute-start.17 = (f32[18,8,128]{2,1,0:T(8,128)S(1)}, f32[18,8,128]{2,1,0:T(8,128)S(1)}, u32[]{:S(2)}, u32[]{:S(2)}) collective-permute-start(f32[18,8,128]{2,1,0:T(8,128)S(1)} %get-tuple-element.30.refs_8_), channel_id=1, source_target_pairs={{0,16},{4,20},{8,24},{12,28},{16,0},{20,4},{24,8},{28,12},{1,17},{... | collective-permute-start | bytes 221192 | tf_op jit(solution)/shard_map/ppermute | solution.py:546
  39.0 0.6 %collective-permute-start.15 = (f32[18,8,128]{2,1,0:T(8,128)S(1)}, f32[18,8,128]{2,1,0:T(8,128)S(1)}, u32[]{:S(2)}, u32[]{:S(2)}) collective-permute-start(f32[18,8,128]{2,1,0:T(8,128)S(1)} %get-tuple-element.30.refs_8_), channel_id=1, source_target_pairs={{0,8},{4,12},{8,0},{12,4},{16,24},{20,28},{24,16},{28,20},{1,9},{5... | collective-permute-start | bytes 221192 | tf_op jit(solution)/shard_map/ppermute | solution.py:546
  39.6 0.0 collective-permute-start.10
  39.6 0.5 collective-permute-start.11
  40.1 1.3 %collective-permute-done.19.refs_14_ = f32[18,8,128]{2,1,0:T(8,128)S(1)} collective-permute-done((f32[18,8,128]{2,1,0:T(8,128)S(1)}, f32[18,8,128]{2,1,0:T(8,128)S(1)}, u32[]{:S(2)}, u32[]{:S(2)}) %collective-permute-start.19) | collective-permute-done | bytes 73760 | tf_op jit(solution)/shard_map/ppermute | solution.py:546
  41.5 0.0 collective-permute-start.14
  41.5 1.2 %collective-permute-done.17.refs_12_ = f32[18,8,128]{2,1,0:T(8,128)S(1)} collective-permute-done((f32[18,8,128]{2,1,0:T(8,128)S(1)}, f32[18,8,128]{2,1,0:T(8,128)S(1)}, u32[]{:S(2)}, u32[]{:S(2)}) %collective-permute-start.17) | collective-permute-done | bytes 73760 | tf_op jit(solution)/shard_map/ppermute | solution.py:546
  42.7 0.0 collective-permute-start.12
  42.7 0.7 %collective-permute-done.15.refs_10_ = f32[18,8,128]{2,1,0:T(8,128)S(1)} collective-permute-done((f32[18,8,128]{2,1,0:T(8,128)S(1)}, f32[18,8,128]{2,1,0:T(8,128)S(1)}, u32[]{:S(2)}, u32[]{:S(2)}) %collective-permute-start.15) | collective-permute-done | bytes 73760 | tf_op jit(solution)/shard_map/ppermute | solution.py:546
  43.4 0.5 collective-permute-start.20
  43.9 0.1 collective-permute-start.18
  44.0 0.4 collective-permute-start.16
  44.4 0.3 collective-permute-done.13.refs_7_
  44.7 0.1 collective-permute-done.20.refs_15_
  44.8 0.3 collective-permute-done.18.refs_13_
  45.2 0.2 collective-permute-done.16.refs_11_
  45.3 12.4 %shard_map.107 = f32[6,4,8,128]{3,2,1,0:T(8,128)} custom-call(f32[4,8,8,128]{3,2,1,0:T(8,128)S(1)} %copy-done.2, f32[4,8,8,128]{3,2,1,0:T(8,128)S(1)} %collective-permute-done.10.refs_1_, f32[4,8,8,128]{3,2,1,0:T(8,128)S(1)} %collective-permute-done.7.refs_2_, f32[4,8,8,128]{3,2,1,0:T(8,128)S(1)} %collective-permute-done.11.refs_3_, ...), custom_call_target="tpu_custom_call" | custom-call | tf_op jit(solution)/shard_map/pallas_call | solution.py:57
  (22 shorter events, 0.1 us)
Async XLA Ops:
  0.6 10.4 %copy-start.4 = (bf16[256,256]{1,0:T(8,128)(2,1)S(1)}, bf16[256,256]{1,0:T(8,128)(2,1)}, u32[]{:S(2)}) copy-start(bf16[256,256]{1,0:T(8,128)(2,1)} %param.14) | copy-start | bytes 393220
  2.4 9.6 %collective-permute-start.1 = (f32[14,8,128]{2,1,0:T(8,128)}, f32[14,8,128]{2,1,0:T(8,128)S(1)}, u32[]{:S(2)}, u32[]{:S(2)}) collective-permute-start(f32[14,8,128]{2,1,0:T(8,128)} %get-tuple-element.17), channel_id=1, source_target_pairs={{0,3},{1,0},{2,1},{3,2},{4,7},{5,4},{6,5},{7,6},{8,11},{9,8},{10,9... | collective-permute-start | bytes 172040 | tf_op jit(solution)/shard_map/ppermute | solution.py:549
  7.5 6.2 %collective-permute-start = (f32[14,8,128]{2,1,0:T(8,128)}, f32[14,8,128]{2,1,0:T(8,128)S(1)}, u32[]{:S(2)}, u32[]{:S(2)}) collective-permute-start(f32[14,8,128]{2,1,0:T(8,128)} %get-tuple-element.17), channel_id=1, source_target_pairs={{0,1},{1,2},{2,3},{3,0},{4,5},{5,6},{6,7},{7,4},{8,9},{9,10},{10,1... | collective-permute-start | bytes 172040 | tf_op jit(solution)/shard_map/ppermute | solution.py:549
  7.5 28.5 %collective-permute-start.9 = (f32[4,8,8,128]{3,2,1,0:T(8,128)}, f32[4,8,8,128]{3,2,1,0:T(8,128)S(1)}, u32[]{:S(2)}, u32[]{:S(2)}) collective-permute-start(f32[4,8,8,128]{3,2,1,0:T(8,128)} %get-tuple-element.26.refs_0_), channel_id=1, source_target_pairs={{0,24},{4,28},{8,16},{12,20},{16,8},{20,12},{24,0},{28,4},{1,25},{... | collective-permute-start | bytes 393224 | tf_op jit(solution)/shard_map/ppermute | solution.py:546
  10.0 26.1 %collective-permute-start.8 = (f32[4,8,8,128]{3,2,1,0:T(8,128)}, f32[4,8,8,128]{3,2,1,0:T(8,128)S(1)}, u32[]{:S(2)}, u32[]{:S(2)}) collective-permute-start(f32[4,8,8,128]{3,2,1,0:T(8,128)} %get-tuple-element.26.refs_0_), channel_id=1, source_target_pairs={{0,16},{4,20},{8,24},{12,28},{16,0},{20,4},{24,8},{28,12},{1,17},{... | collective-permute-start | bytes 393224 | tf_op jit(solution)/shard_map/ppermute | solution.py:546
  10.5 25.6 %collective-permute-start.7 = (f32[4,8,8,128]{3,2,1,0:T(8,128)}, f32[4,8,8,128]{3,2,1,0:T(8,128)S(1)}, u32[]{:S(2)}, u32[]{:S(2)}) collective-permute-start(f32[4,8,8,128]{3,2,1,0:T(8,128)} %get-tuple-element.26.refs_0_), channel_id=1, source_target_pairs={{0,8},{4,12},{8,0},{12,4},{16,24},{20,28},{24,16},{28,20},{1,9},{5... | collective-permute-start | bytes 393224 | tf_op jit(solution)/shard_map/ppermute | solution.py:546
  11.1 0.7 %copy-start.5 = (bf16[32,256]{1,0:T(8,128)(2,1)S(1)}, bf16[32,256]{1,0:T(8,128)(2,1)}, u32[]{:S(2)}) copy-start(bf16[32,256]{1,0:T(8,128)(2,1)} %param.12) | copy-start | bytes 49156
  11.1 2.6 %copy-start.1 = (f32[6,4,8,128]{3,2,1,0:T(8,128)S(1)}, f32[6,4,8,128]{3,2,1,0:T(8,128)}, u32[]{:S(2)}) copy-start(f32[6,4,8,128]{3,2,1,0:T(8,128)} %mom.5) | copy-start | bytes 294916
  11.8 1.9 %copy-start = (f32[6,4,8,128]{3,2,1,0:T(8,128)S(1)}, f32[6,4,8,128]{3,2,1,0:T(8,128)}, u32[]{:S(2)}) copy-start(f32[6,4,8,128]{3,2,1,0:T(8,128)} %disp.5) | copy-start | bytes 294916
  13.7 4.2 %collective-permute-start.5 = (f32[6,8,128]{2,1,0:T(8,128)S(1)}, f32[6,8,128]{2,1,0:T(8,128)S(1)}, u32[]{:S(2)}, u32[]{:S(2)}) collective-permute-start(f32[6,8,128]{2,1,0:T(8,128)S(1)} %get-tuple-element.20), channel_id=1, source_target_pairs={{0,20},{4,24},{8,28},{12,16},{16,4},{20,8},{24,12},{28,0},{1,21},{... | collective-permute-start | bytes 73736 | tf_op jit(solution)/shard_map/ppermute | solution.py:543
  13.8 4.5 %collective-permute-start.3 = (f32[6,8,128]{2,1,0:T(8,128)S(1)}, f32[6,8,128]{2,1,0:T(8,128)S(1)}, u32[]{:S(2)}, u32[]{:S(2)}) collective-permute-start(f32[6,8,128]{2,1,0:T(8,128)S(1)} %get-tuple-element.20), channel_id=1, source_target_pairs={{0,4},{4,8},{8,12},{12,0},{16,20},{20,24},{24,28},{28,16},{1,5},{5... | collective-permute-start | bytes 73736 | tf_op jit(solution)/shard_map/ppermute | solution.py:543
  18.0 1.6 %copy-start.7 = (f32[256]{0:T(256)S(1)}, f32[256]{0:T(256)}, u32[]{:S(2)}) copy-start(f32[256]{0:T(256)} %param.13) | copy-start | bytes 3076
  18.0 3.3 %collective-permute-start.6 = (f32[6,8,128]{2,1,0:T(8,128)S(1)}, f32[6,8,128]{2,1,0:T(8,128)S(1)}, u32[]{:S(2)}, u32[]{:S(2)}) collective-permute-start(f32[6,8,128]{2,1,0:T(8,128)S(1)} %get-tuple-element.21), channel_id=1, source_target_pairs={{0,28},{4,16},{8,20},{12,24},{16,12},{20,0},{24,4},{28,8},{1,29},{... | collective-permute-start | bytes 73736 | tf_op jit(solution)/shard_map/ppermute | solution.py:543
  18.3 1.3 %copy-start.6 = (bf16[256,4]{0,1:T(4,128)(2,1)S(1)}, bf16[256,4]{0,1:T(4,128)(2,1)}, u32[]{:S(2)}) copy-start(bf16[256,4]{0,1:T(4,128)(2,1)} %param.15) | copy-start | bytes 6148
  18.3 9.1 %collective-permute-start.2 = (f32[2,12,8,128]{3,2,1,0:T(8,128)S(1)}, f32[2,12,8,128]{3,2,1,0:T(8,128)S(1)}, u32[]{:S(2)}, u32[]{:S(2)}) collective-permute-start(f32[2,12,8,128]{3,2,1,0:T(8,128)S(1)} %get-tuple-element.19), channel_id=1, source_target_pairs={{0,16},{4,20},{8,24},{12,28},{16,0},{20,4},{24,8},{28,12},{1,17},{... | collective-permute-start | bytes 294920 | tf_op jit(solution)/shard_map/ppermute | solution.py:543
  21.2 6.2 %collective-permute-start.4 = (f32[6,8,128]{2,1,0:T(8,128)S(1)}, f32[6,8,128]{2,1,0:T(8,128)S(1)}, u32[]{:S(2)}, u32[]{:S(2)}) collective-permute-start(f32[6,8,128]{2,1,0:T(8,128)S(1)} %get-tuple-element.21), channel_id=1, source_target_pairs={{0,12},{4,0},{8,4},{12,8},{16,28},{20,16},{24,20},{28,24},{1,13},{... | collective-permute-start | bytes 73736 | tf_op jit(solution)/shard_map/ppermute | solution.py:543
  22.4 5.0 %copy-start.3 = (f32[6,4,8,128]{3,2,1,0:T(8,128)S(1)}, f32[6,4,8,128]{3,2,1,0:T(8,128)}, u32[]{:S(2)}) copy-start(f32[6,4,8,128]{3,2,1,0:T(8,128)} %vel.1) | copy-start | bytes 294916
  27.3 12.3 %copy-start.2 = (f32[4,8,8,128]{3,2,1,0:T(8,128)S(1)}, f32[4,8,8,128]{3,2,1,0:T(8,128)}, u32[]{:S(2)}) copy-start(f32[4,8,8,128]{3,2,1,0:T(8,128)} %get-tuple-element.26.refs_0_) | copy-start | bytes 393220
  36.1 5.4 %collective-permute-start.19 = (f32[18,8,128]{2,1,0:T(8,128)S(1)}, f32[18,8,128]{2,1,0:T(8,128)S(1)}, u32[]{:S(2)}, u32[]{:S(2)}) collective-permute-start(f32[18,8,128]{2,1,0:T(8,128)S(1)} %get-tuple-element.30.refs_8_), channel_id=1, source_target_pairs={{0,24},{4,28},{8,16},{12,20},{16,8},{20,12},{24,0},{28,4},{1,25},{... | collective-permute-start | bytes 221192 | tf_op jit(solution)/shard_map/ppermute | solution.py:546
  37.5 5.2 %collective-permute-start.17 = (f32[18,8,128]{2,1,0:T(8,128)S(1)}, f32[18,8,128]{2,1,0:T(8,128)S(1)}, u32[]{:S(2)}, u32[]{:S(2)}) collective-permute-start(f32[18,8,128]{2,1,0:T(8,128)S(1)} %get-tuple-element.30.refs_8_), channel_id=1, source_target_pairs={{0,16},{4,20},{8,24},{12,28},{16,0},{20,4},{24,8},{28,12},{1,17},{... | collective-permute-start | bytes 221192 | tf_op jit(solution)/shard_map/ppermute | solution.py:546
  39.0 4.4 %collective-permute-start.15 = (f32[18,8,128]{2,1,0:T(8,128)S(1)}, f32[18,8,128]{2,1,0:T(8,128)S(1)}, u32[]{:S(2)}, u32[]{:S(2)}) collective-permute-start(f32[18,8,128]{2,1,0:T(8,128)S(1)} %get-tuple-element.30.refs_8_), channel_id=1, source_target_pairs={{0,8},{4,12},{8,0},{12,4},{16,24},{20,28},{24,16},{28,20},{1,9},{5... | collective-permute-start | bytes 221192 | tf_op jit(solution)/shard_map/ppermute | solution.py:546
  39.6 4.3 %collective-permute-start.10 = (f32[4,8,8,128]{3,2,1,0:T(8,128)S(1)}, f32[4,8,8,128]{3,2,1,0:T(8,128)S(1)}, u32[]{:S(2)}, u32[]{:S(2)}) collective-permute-start(f32[4,8,8,128]{3,2,1,0:T(8,128)S(1)} %copy-done.2), channel_id=1, source_target_pairs={{0,4},{4,0},{8,12},{12,8},{16,20},{20,16},{24,28},{28,24},{1,5},{5... | collective-permute-start | bytes 393224 | tf_op jit(solution)/shard_map/ppermute | solution.py:546
  39.6 4.4 %collective-permute-start.11 = (f32[4,8,8,128]{3,2,1,0:T(8,128)S(1)}, f32[4,8,8,128]{3,2,1,0:T(8,128)S(1)}, u32[]{:S(2)}, u32[]{:S(2)}) collective-permute-start(f32[4,8,8,128]{3,2,1,0:T(8,128)S(1)} %collective-permute-done.7.refs_2_), channel_id=1, source_target_pairs={{0,4},{4,0},{8,12},{12,8},{16,20},{20,16},{24,28},{28,24},{1,5},{5... | collective-permute-start | bytes 393224 | tf_op jit(solution)/shard_map/ppermute | solution.py:546
  41.5 1.9 %collective-permute-start.14 = (f32[18,8,128]{2,1,0:T(8,128)S(1)}, f32[18,8,128]{2,1,0:T(8,128)S(1)}, u32[]{:S(2)}, u32[]{:S(2)}) collective-permute-start(f32[18,8,128]{2,1,0:T(8,128)S(1)} %get-tuple-element.30.refs_8_), channel_id=1, source_target_pairs={{0,4},{4,0},{8,12},{12,8},{16,20},{20,16},{24,28},{28,24},{1,5},{5... | collective-permute-start | bytes 221192 | tf_op jit(solution)/shard_map/ppermute | solution.py:546
  42.7 1.7 %collective-permute-start.12 = (f32[4,8,8,128]{3,2,1,0:T(8,128)S(1)}, f32[4,8,8,128]{3,2,1,0:T(8,128)S(1)}, u32[]{:S(2)}, u32[]{:S(2)}) collective-permute-start(f32[4,8,8,128]{3,2,1,0:T(8,128)S(1)} %collective-permute-done.8.refs_4_), channel_id=1, source_target_pairs={{0,4},{4,0},{8,12},{12,8},{16,20},{20,16},{24,28},{28,24},{1,5},{5... | collective-permute-start | bytes 393224 | tf_op jit(solution)/shard_map/ppermute | solution.py:546
  43.4 1.3 %collective-permute-start.13 = (f32[4,8,8,128]{3,2,1,0:T(8,128)S(1)}, f32[4,8,8,128]{3,2,1,0:T(8,128)S(1)}, u32[]{:S(2)}, u32[]{:S(2)}) collective-permute-start(f32[4,8,8,128]{3,2,1,0:T(8,128)S(1)} %collective-permute-done.9.refs_6_), channel_id=1, source_target_pairs={{0,4},{4,0},{8,12},{12,8},{16,20},{20,16},{24,28},{28,24},{1,5},{5... | collective-permute-start | bytes 393224 | tf_op jit(solution)/shard_map/ppermute | solution.py:546
  43.4 1.4 %collective-permute-start.20 = (f32[18,8,128]{2,1,0:T(8,128)S(1)}, f32[18,8,128]{2,1,0:T(8,128)S(1)}, u32[]{:S(2)}, u32[]{:S(2)}) collective-permute-start(f32[18,8,128]{2,1,0:T(8,128)S(1)} %collective-permute-done.19.refs_14_), channel_id=1, source_target_pairs={{0,4},{4,0},{8,12},{12,8},{16,20},{20,16},{24,28},{28,24},{1,5},{5... | collective-permute-start | bytes 221192 | tf_op jit(solution)/shard_map/ppermute | solution.py:546
  43.9 1.3 %collective-permute-start.18 = (f32[18,8,128]{2,1,0:T(8,128)S(1)}, f32[18,8,128]{2,1,0:T(8,128)S(1)}, u32[]{:S(2)}, u32[]{:S(2)}) collective-permute-start(f32[18,8,128]{2,1,0:T(8,128)S(1)} %collective-permute-done.17.refs_12_), channel_id=1, source_target_pairs={{0,4},{4,0},{8,12},{12,8},{16,20},{20,16},{24,28},{28,24},{1,5},{5... | collective-permute-start | bytes 221192 | tf_op jit(solution)/shard_map/ppermute | solution.py:546
  44.0 1.4 %collective-permute-start.16 = (f32[18,8,128]{2,1,0:T(8,128)S(1)}, f32[18,8,128]{2,1,0:T(8,128)S(1)}, u32[]{:S(2)}, u32[]{:S(2)}) collective-permute-start(f32[18,8,128]{2,1,0:T(8,128)S(1)} %collective-permute-done.15.refs_10_), channel_id=1, source_target_pairs={{0,4},{4,0},{8,12},{12,8},{16,20},{20,16},{24,28},{28,24},{1,5},{5... | collective-permute-start | bytes 221192 | tf_op jit(solution)/shard_map/ppermute | solution.py:546

commit v2 on v1

--- a/solution.py
+++ b/solution.py
@@ -259,8 +259,8 @@
 
 
 def outer_body(
-    disp, mom, vel, slab, xup, xdn, yup, ydn, xyup, xydn, w_in, b_in, w_mid, w_out, inner,
-    disp_out, vel_out, cbrick, near, table, heads, one, two,
+    disp, mom, slab, xup, xdn, yup, ydn, xyup, xydn, w_in, b_in, w_mid, w_out, inner,
+    cbrick, force, near, table, heads, one, two,
 ):
     e0 = odd_mask(0)
     slots = XL + 1
@@ -280,9 +280,7 @@
             coupling.append(1.0 + 0.5 * jnp.tanh(heads[at, 3 * SUB : 4 * SUB, :]))
             if slot < XL:
                 for k in range(3):
-                    v = vel[3 * p + k, slot] + lattice_step * heads[at, k * SUB : (k + 1) * SUB, :]
-                    vel_out[3 * p + k, slot] = v
-                    disp_out[3 * p + k, slot] = disp[3 * p + k, slot] + lattice_step * v
+                    force[3 * p + k, slot] = heads[at, k * SUB : (k + 1) * SUB, :]
         for xh in range(2):
             even, odd = coupling[2 * xh], coupling[2 * xh + 1]
             cbrick[2 * xh + p] = jnp.where(e0, odd, even)
@@ -291,6 +289,12 @@
         for k in range(4):
             h = slab[6 + 3 * p + k if k < 3 else 12 + p]
             cbrick[10 + 4 * p + k] = jnp.where(e0, lanes(h, 64), h)
+
+
+def move_body(disp, vel, force, disp_out, vel_out):
+    v = vel[...] + lattice_step * force[...]
+    vel_out[...] = v
+    disp_out[...] = disp[...] + lattice_step * v
 
 
 def even_fit(func, terms):
@@ -485,6 +489,33 @@
                     for k in range(3):
                         state[p, par, k, r, j] = new[k]
 
+    def last_turn(p, par, bit, half_turns):
+        opp = 1 - par
+        first = 2 * ix
+        before = jnp.where(ix == 0, xh_all - 1, first - 1)
+        after = jnp.where(ix == nx - 1, 0, first + 2)
+        near_x = (before, first, first + 1, after)
+        for r in range(ny):
+            e = row_mask(r, par)
+            fields = [[], []]
+            for k in range(3):
+                head = (p, opp, k)
+                c = [mc[*head, r, x] for x in near_x]
+                for n in (1, 2):
+                    x = near_x[n]
+                    seam = pltpu.roll(mh[*head, r, x // 4], (LANE - SLAB * (x % 4)) % LANE, 1)
+                    up = lanes(jnp.where(lane == 0, seam, c[n]), -1)
+                    down = lanes(jnp.where(lane == LANE - 1, seam, c[n]), 1)
+                    shell = c[n] + jnp.where(e, c[n + 1], c[n - 1]) + (up + down)
+                    shell += y_next(mc, head, r, x) + y_last(mc, head, r, x)
+                    fields[n - 1].append(cc[p, par, r, x] * nc[par, k, r, x] + shell)
+            for n in (1, 2):
+                x = near_x[n]
+                own = [mc[p, par, k, r, x] for k in range(3)]
+                new = rotated(own, fields[n - 1], half_turns, mc[p, par, 3, r, x] == bit)
+                for k in range(3):
+                    mc[p, par, k, r, x] = new[k]
+
     unit = second_shell * half_step / (2.0 * np.pi)
 
     def sweep(p, sector, half_turns):
@@ -512,7 +543,8 @@
     near_total(1)
     lax.fori_loop(0, 7, middle, 0)
     near_total(0)
-    lax.fori_loop(0, 4, descend, 0)
+    lax.fori_loop(0, 3, descend, 0)
+    last_turn(0, 0, 0.0, unit)
 
     for p in range(2):
         for k in range(3):
@@ -596,11 +628,14 @@
         scratch=work[:2] + work[3:],
         cost=pl.CostEstimate(flops=10**9, bytes_accessed=2 << 20, transcendentals=3 << 20),
     )
-    disp_out, vel_out, cbrick = vmem_call(
+    cbrick, force = vmem_call(
         outer_body,
-        [((6, XL, *TILE), f32), ((6, XL, *TILE), f32), ((18, *TILE), f32)],
-        displacement, moments, velocity, slab, xup, xdn, yup, ydn, xyup, xydn, *weights, inner,
+        [((18, *TILE), f32), ((6, XL, *TILE), f32)],
+        displacement, moments, slab, xup, xdn, yup, ydn, xyup, xydn, *weights, inner,
         scratch=work,
+    )
+    disp_out, vel_out = vmem_call(
+        move_body, [((6, XL, *TILE), f32)] * 2, displacement, velocity, force,
     )
     near_masks = [(0, 0)] + far
     late = lax.optimization_barrier((cbrick, *[held[m] for m in near_masks]))

time: 58 us -> 56.3 us (0.971)
  waiting for transfers between devices: 9.41 us -> 7.01 us
  local copies, waits for them, and re-layouts: 0.99 us -> 1.76 us
    ppermute x2, waiting for transfers between devices: 1.75 us -> 0.01 us  [along_z(): return lax.ppermute(v, 'gz', [(i, (i + step) % nz) for i in range(nz)])]
    ppermute x14, starting transfers between devices: 8.58 us -> 10 us  [swap(): return lax.ppermute(v, plane, pairs(lambda x, y: (x ^ mx, y ^ my)))]
    ppermute x5, starting transfers between devices: 5.02 us -> 3.73 us  [shift(): return lax.ppermute(v, plane, pairs(lambda x, y: (x + dx, y + dy)))]
    ppermute x14, waiting for transfers between devices: 4.17 us -> 3.13 us  [swap(): return lax.ppermute(v, plane, pairs(lambda x, y: (x ^ mx, y ^ my)))]
    unnamed x17, local copies, waits for them, and re-layouts: 0.8 us -> 1.57 us
    pallas_call x5 -> x6, Pallas kernels: 27.7 us -> 27.5 us  [vmem_call(): pl.pallas_call(body, out_shape=tuple((jax.ShapeDtypeStruct(s, d) for s, d...]
  transfers between devices with their start and end apart: 21 -> 21, of which waited for: 11 -> 5; matrix products, arithmetic and copies ran while one was open for 1% -> 1% of each run, Pallas kernels for 24% -> 24%
where the time goes in v2:
time: 56.3 us; the launch traced here: 56.1 us
  Pallas kernels  27.5 us (49%)
  starting transfers between devices  18.9 us (34%)
  waiting for transfers between devices  7.01 us (12%)
  local copies, waits for them, and re-layouts  1.76 us (3%)
  between operations  0.81 us (1%)
    pallas_call x6, Pallas kernels, vmem_call(): pl.pallas_call(body, out_shape=tuple((jax.ShapeDtypeStruct(s, d) for s, d...  27.5 us
    ppermute x14, starting transfers between devices, swap(): return lax.ppermute(v, plane, pairs(lambda x, y: (x ^ mx, y ^ my)))  10 us
    ppermute x2, starting transfers between devices, along_z(): return lax.ppermute(v, 'gz', [(i, (i + step) % nz) for i in range(nz)])  5.2 us
    ppermute x5, waiting for transfers between devices, shift(): return lax.ppermute(v, plane, pairs(lambda x, y: (x + dx, y + dy)))  3.87 us
    ppermute x5, starting transfers between devices, shift(): return lax.ppermute(v, plane, pairs(lambda x, y: (x + dx, y + dy)))  3.73 us
    ppermute x14, waiting for transfers between devices, swap(): return lax.ppermute(v, plane, pairs(lambda x, y: (x ^ mx, y ^ my)))  3.13 us
    unnamed x17, local copies, waits for them, and re-layouts  1.57 us
  transfers between devices with their start and end apart: 21, of which 5 were waited for; matrix products, arithmetic and copies ran while one was open for 1% of the time, Pallas kernels for 24%

profile of v2, /device:TPU:0, one launch (start us, length us, event | category | flops | bytes accessed | tf_op | source)
XLA Modules:
  0.0 56.1 jit_solution(13262003349091561649)
XLA Ops:
  0.6 1.7 %shard_map.103 = (f32[14,8,128]{2,1,0:T(8,128)}, f32[4,8,8,128]{3,2,1,0:T(8,128)}) custom-call(f32[6,4,8,128]{3,2,1,0:T(8,128)} %disp.7, f32[6,4,8,128]{3,2,1,0:T(8,128)} %mom.5, s32[2,4,8,128]{3,2,1,0:T(8,128)} %bit_in.1), custom_call_target="tpu_custom_call" | custom-call | tf_op jit(solution)/shard_map/pallas_call | solution.py:57
  2.4 3.1 %collective-permute-start = (f32[14,8,128]{2,1,0:T(8,128)}, f32[14,8,128]{2,1,0:T(8,128)S(1)}, u32[]{:S(2)}, u32[]{:S(2)}) collective-permute-start(f32[14,8,128]{2,1,0:T(8,128)} %get-tuple-element.18), channel_id=1, source_target_pairs={{0,1},{1,2},{2,3},{3,0},{4,5},{5,6},{6,7},{7,4},{8,9},{9,10},{10,1... | collective-permute-start | bytes 172040 | tf_op jit(solution)/shard_map/ppermute | solution.py:581
  5.5 2.1 %collective-permute-start.1 = (f32[14,8,128]{2,1,0:T(8,128)}, f32[14,8,128]{2,1,0:T(8,128)S(1)}, u32[]{:S(2)}, u32[]{:S(2)}) collective-permute-start(f32[14,8,128]{2,1,0:T(8,128)} %get-tuple-element.18), channel_id=1, source_target_pairs={{0,3},{1,0},{2,1},{3,2},{4,7},{5,4},{6,5},{7,6},{8,11},{9,8},{10,9... | collective-permute-start | bytes 172040 | tf_op jit(solution)/shard_map/ppermute | solution.py:581
  7.6 1.6 %collective-permute-start.7 = (f32[4,8,8,128]{3,2,1,0:T(8,128)}, f32[4,8,8,128]{3,2,1,0:T(8,128)S(1)}, u32[]{:S(2)}, u32[]{:S(2)}) collective-permute-start(f32[4,8,8,128]{3,2,1,0:T(8,128)} %get-tuple-element.28.refs_0_), channel_id=1, source_target_pairs={{0,8},{4,12},{8,0},{12,4},{16,24},{20,28},{24,16},{28,20},{1,9},{5... | collective-permute-start | bytes 393224 | tf_op jit(solution)/shard_map/ppermute | solution.py:578
  9.2 1.5 %collective-permute-start.8 = (f32[4,8,8,128]{3,2,1,0:T(8,128)}, f32[4,8,8,128]{3,2,1,0:T(8,128)S(1)}, u32[]{:S(2)}, u32[]{:S(2)}) collective-permute-start(f32[4,8,8,128]{3,2,1,0:T(8,128)} %get-tuple-element.28.refs_0_), channel_id=1, source_target_pairs={{0,16},{4,20},{8,24},{12,28},{16,0},{20,4},{24,8},{28,12},{1,17},{... | collective-permute-start | bytes 393224 | tf_op jit(solution)/shard_map/ppermute | solution.py:578
  10.8 0.3 collective-permute-start.9
  11.1 0.1 copy.14
  11.2 0.0 copy-start.5
  11.2 0.0 copy-start.1
  11.2 0.7 %copy-done.5 = bf16[32,256]{1,0:T(8,128)(2,1)S(1)} copy-done((bf16[32,256]{1,0:T(8,128)(2,1)S(1)}, bf16[32,256]{1,0:T(8,128)(2,1)}, u32[]{:S(2)}) %copy-start.5) | copy-done | bytes 16408
  11.9 0.1 copy.13
  12.0 0.0 collective-permute-done.1.high
  12.0 0.1 copy-done.1
  12.1 0.7 %copy-done = f32[6,4,8,128]{3,2,1,0:T(8,128)S(1)} copy-done((f32[6,4,8,128]{3,2,1,0:T(8,128)S(1)}, f32[6,4,8,128]{3,2,1,0:T(8,128)}, u32[]{:S(2)}) %copy-start) | copy-done | bytes 98328
  12.8 0.1 collective-permute-start.3
  12.9 1.7 %collective-permute-start.4 = (f32[6,8,128]{2,1,0:T(8,128)S(1)}, f32[6,8,128]{2,1,0:T(8,128)S(1)}, u32[]{:S(2)}, u32[]{:S(2)}) collective-permute-start(f32[6,8,128]{2,1,0:T(8,128)S(1)} %get-tuple-element.22), channel_id=1, source_target_pairs={{0,12},{4,0},{8,4},{12,8},{16,28},{20,16},{24,20},{28,24},{1,13},{... | collective-permute-start | bytes 73736 | tf_op jit(solution)/shard_map/ppermute | solution.py:575
  14.7 0.0 copy-start.7
  14.7 1.5 %collective-permute-done.3.yup = f32[6,8,128]{2,1,0:T(8,128)S(1)} collective-permute-done((f32[6,8,128]{2,1,0:T(8,128)S(1)}, f32[6,8,128]{2,1,0:T(8,128)S(1)}, u32[]{:S(2)}, u32[]{:S(2)}) %collective-permute-start.3) | collective-permute-done | bytes 24608 | tf_op jit(solution)/shard_map/ppermute | solution.py:575
  16.1 0.6 %collective-permute-start.5 = (f32[6,8,128]{2,1,0:T(8,128)S(1)}, f32[6,8,128]{2,1,0:T(8,128)S(1)}, u32[]{:S(2)}, u32[]{:S(2)}) collective-permute-start(f32[6,8,128]{2,1,0:T(8,128)S(1)} %get-tuple-element.21), channel_id=1, source_target_pairs={{0,20},{4,24},{8,28},{12,16},{16,4},{20,8},{24,12},{28,0},{1,21},{... | collective-permute-start | bytes 73736 | tf_op jit(solution)/shard_map/ppermute | solution.py:575
  16.7 0.0 collective-permute-done.4.ydn
  16.7 1.2 %collective-permute-start.2 = (f32[2,12,8,128]{3,2,1,0:T(8,128)S(1)}, f32[2,12,8,128]{3,2,1,0:T(8,128)S(1)}, u32[]{:S(2)}, u32[]{:S(2)}) collective-permute-start(f32[2,12,8,128]{3,2,1,0:T(8,128)S(1)} %get-tuple-element.20), channel_id=1, source_target_pairs={{0,16},{4,20},{8,24},{12,28},{16,0},{20,4},{24,8},{28,12},{1,17},{... | collective-permute-start | bytes 294920 | tf_op jit(solution)/shard_map/ppermute | solution.py:575
  17.9 2.4 %collective-permute-done.5.xyup = f32[6,8,128]{2,1,0:T(8,128)S(1)} collective-permute-done((f32[6,8,128]{2,1,0:T(8,128)S(1)}, f32[6,8,128]{2,1,0:T(8,128)S(1)}, u32[]{:S(2)}, u32[]{:S(2)}) %collective-permute-start.5) | collective-permute-done | bytes 24608 | tf_op jit(solution)/shard_map/ppermute | solution.py:575
  20.3 0.2 collective-permute-start.6
  20.5 0.1 broadcast_in_dim.2.b_in
  20.6 4.9 %shard_map.105.inner = f32[11,64,128]{2,1,0:T(8,128)S(1)} custom-call(f32[6,4,8,128]{3,2,1,0:T(8,128)S(1)} %copy-done, f32[6,4,8,128]{3,2,1,0:T(8,128)S(1)} %copy-done.1, f32[14,8,128]{2,1,0:T(8,128)S(1)} %get-tuple-element.19.slab, bf16[256,32]{1,0:T(8,128)(2,1)S(1)} %fusion.1.w_in, f32[256,128]{1,0:T(8,128)S(1)} %broadcast_in_dim.2.b_in, ...), custom_call_target="tpu_custom_call" | custom-call | flops 1000000000 | bytes 2097152 | tf_op jit(solution)/shard_map/pallas_call | solution.py:57
  25.5 0.0 copy-start.3
  25.5 0.0 collective-permute-done.2.xup.xdn
  25.6 8.0 %shard_map.106 = (f32[18,8,128]{2,1,0:T(8,128)S(1)}, f32[6,4,8,128]{3,2,1,0:T(8,128)S(1)}) custom-call(f32[6,4,8,128]{3,2,1,0:T(8,128)S(1)} %copy-done, f32[6,4,8,128]{3,2,1,0:T(8,128)S(1)} %copy-done.1, f32[14,8,128]{2,1,0:T(8,128)S(1)} %get-tuple-element.19.slab, f32[2,12,8,128]{3,2,1,0:T(8,128)S(1)} %collective-permute-done.2.xup.xdn, ...), custom_call_target="tpu_custom_call" | custom-call | tf_op jit(solution)/shard_map/pallas_call | solution.py:57
  33.6 0.0 collective-permute-done.8.refs_4_
  33.6 0.0 collective-permute-done.9.refs_6_
  33.6 1.6 %collective-permute-start.15 = (f32[18,8,128]{2,1,0:T(8,128)S(1)}, f32[18,8,128]{2,1,0:T(8,128)S(1)}, u32[]{:S(2)}, u32[]{:S(2)}) collective-permute-start(f32[18,8,128]{2,1,0:T(8,128)S(1)} %get-tuple-element.32.refs_8_), channel_id=1, source_target_pairs={{0,8},{4,12},{8,0},{12,4},{16,24},{20,28},{24,16},{28,20},{1,9},{5... | collective-permute-start | bytes 221192 | tf_op jit(solution)/shard_map/ppermute | solution.py:578
  35.3 1.5 %collective-permute-start.17 = (f32[18,8,128]{2,1,0:T(8,128)S(1)}, f32[18,8,128]{2,1,0:T(8,128)S(1)}, u32[]{:S(2)}, u32[]{:S(2)}) collective-permute-start(f32[18,8,128]{2,1,0:T(8,128)S(1)} %get-tuple-element.32.refs_8_), channel_id=1, source_target_pairs={{0,16},{4,20},{8,24},{12,28},{16,0},{20,4},{24,8},{28,12},{1,17},{... | collective-permute-start | bytes 221192 | tf_op jit(solution)/shard_map/ppermute | solution.py:578
  36.8 0.4 collective-permute-start.19
  37.2 0.9 %collective-permute-start.10 = (f32[4,8,8,128]{3,2,1,0:T(8,128)S(1)}, f32[4,8,8,128]{3,2,1,0:T(8,128)S(1)}, u32[]{:S(2)}, u32[]{:S(2)}) collective-permute-start(f32[4,8,8,128]{3,2,1,0:T(8,128)S(1)} %copy-done.2), channel_id=1, source_target_pairs={{0,4},{4,0},{8,12},{12,8},{16,20},{20,16},{24,28},{28,24},{1,5},{5... | collective-permute-start | bytes 393224 | tf_op jit(solution)/shard_map/ppermute | solution.py:578
  38.0 0.0 collective-permute-start.11
  38.1 0.0 collective-permute-done.15.refs_10_
  38.1 0.9 %collective-permute-start.14 = (f32[18,8,128]{2,1,0:T(8,128)S(1)}, f32[18,8,128]{2,1,0:T(8,128)S(1)}, u32[]{:S(2)}, u32[]{:S(2)}) collective-permute-start(f32[18,8,128]{2,1,0:T(8,128)S(1)} %get-tuple-element.32.refs_8_), channel_id=1, source_target_pairs={{0,4},{4,0},{8,12},{12,8},{16,20},{20,16},{24,28},{28,24},{1,5},{5... | collective-permute-start | bytes 221192 | tf_op jit(solution)/shard_map/ppermute | solution.py:578
  38.9 1.1 %collective-permute-done.17.refs_12_ = f32[18,8,128]{2,1,0:T(8,128)S(1)} collective-permute-done((f32[18,8,128]{2,1,0:T(8,128)S(1)}, f32[18,8,128]{2,1,0:T(8,128)S(1)}, u32[]{:S(2)}, u32[]{:S(2)}) %collective-permute-start.17) | collective-permute-done | bytes 73760 | tf_op jit(solution)/shard_map/ppermute | solution.py:578
  40.0 0.2 collective-permute-start.12
  40.2 1.8 %collective-permute-done.19.refs_14_ = f32[18,8,128]{2,1,0:T(8,128)S(1)} collective-permute-done((f32[18,8,128]{2,1,0:T(8,128)S(1)}, f32[18,8,128]{2,1,0:T(8,128)S(1)}, u32[]{:S(2)}, u32[]{:S(2)}) %collective-permute-start.19) | collective-permute-done | bytes 73760 | tf_op jit(solution)/shard_map/ppermute | solution.py:578
  42.0 0.5 collective-permute-start.16
  42.6 0.1 collective-permute-start.18
  42.6 0.4 collective-permute-start.20
  43.1 0.7 %shard_map.107 = (f32[6,4,8,128]{3,2,1,0:T(8,128)}, f32[6,4,8,128]{3,2,1,0:T(8,128)}) custom-call(f32[6,4,8,128]{3,2,1,0:T(8,128)S(1)} %copy-done, f32[6,4,8,128]{3,2,1,0:T(8,128)S(1)} %copy-done.3, f32[6,4,8,128]{3,2,1,0:T(8,128)S(1)} %get-tuple-element.23.force), custom_call_target="tpu_custom_call" | custom-call | tf_op jit(solution)/shard_map/pallas_call | solution.py:57
  43.8 0.0 collective-permute-done.12.refs_5_
  43.8 0.0 collective-permute-done.18.refs_13_
  43.8 0.2 collective-permute-done.20.refs_15_
  44.0 12.1 %shard_map.108 = f32[6,4,8,128]{3,2,1,0:T(8,128)} custom-call(f32[4,8,8,128]{3,2,1,0:T(8,128)S(1)} %copy-done.2, f32[4,8,8,128]{3,2,1,0:T(8,128)S(1)} %collective-permute-done.10.refs_1_, f32[4,8,8,128]{3,2,1,0:T(8,128)S(1)} %collective-permute-done.7.refs_2_, f32[4,8,8,128]{3,2,1,0:T(8,128)S(1)} %collective-permute-done.11.refs_3_, ...), custom_call_target="tpu_custom_call" | custom-call | tf_op jit(solution)/shard_map/pallas_call | solution.py:57
  (23 shorter events, 0.1 us)
Async XLA Ops:
  0.6 10.4 %copy-start.4 = (bf16[256,256]{1,0:T(8,128)(2,1)S(1)}, bf16[256,256]{1,0:T(8,128)(2,1)}, u32[]{:S(2)}) copy-start(bf16[256,256]{1,0:T(8,128)(2,1)} %param.14) | copy-start | bytes 393220
  2.4 9.6 %collective-permute-start = (f32[14,8,128]{2,1,0:T(8,128)}, f32[14,8,128]{2,1,0:T(8,128)S(1)}, u32[]{:S(2)}, u32[]{:S(2)}) collective-permute-start(f32[14,8,128]{2,1,0:T(8,128)} %get-tuple-element.18), channel_id=1, source_target_pairs={{0,1},{1,2},{2,3},{3,0},{4,5},{5,6},{6,7},{7,4},{8,9},{9,10},{10,1... | collective-permute-start | bytes 172040 | tf_op jit(solution)/shard_map/ppermute | solution.py:581
  5.5 6.5 %collective-permute-start.1 = (f32[14,8,128]{2,1,0:T(8,128)}, f32[14,8,128]{2,1,0:T(8,128)S(1)}, u32[]{:S(2)}, u32[]{:S(2)}) collective-permute-start(f32[14,8,128]{2,1,0:T(8,128)} %get-tuple-element.18), channel_id=1, source_target_pairs={{0,3},{1,0},{2,1},{3,2},{4,7},{5,4},{6,5},{7,6},{8,11},{9,8},{10,9... | collective-permute-start | bytes 172040 | tf_op jit(solution)/shard_map/ppermute | solution.py:581
  7.6 26.0 %collective-permute-start.7 = (f32[4,8,8,128]{3,2,1,0:T(8,128)}, f32[4,8,8,128]{3,2,1,0:T(8,128)S(1)}, u32[]{:S(2)}, u32[]{:S(2)}) collective-permute-start(f32[4,8,8,128]{3,2,1,0:T(8,128)} %get-tuple-element.28.refs_0_), channel_id=1, source_target_pairs={{0,8},{4,12},{8,0},{12,4},{16,24},{20,28},{24,16},{28,20},{1,9},{5... | collective-permute-start | bytes 393224 | tf_op jit(solution)/shard_map/ppermute | solution.py:578
  9.2 24.4 %collective-permute-start.8 = (f32[4,8,8,128]{3,2,1,0:T(8,128)}, f32[4,8,8,128]{3,2,1,0:T(8,128)S(1)}, u32[]{:S(2)}, u32[]{:S(2)}) collective-permute-start(f32[4,8,8,128]{3,2,1,0:T(8,128)} %get-tuple-element.28.refs_0_), channel_id=1, source_target_pairs={{0,16},{4,20},{8,24},{12,28},{16,0},{20,4},{24,8},{28,12},{1,17},{... | collective-permute-start | bytes 393224 | tf_op jit(solution)/shard_map/ppermute | solution.py:578
  10.8 22.9 %collective-permute-start.9 = (f32[4,8,8,128]{3,2,1,0:T(8,128)}, f32[4,8,8,128]{3,2,1,0:T(8,128)S(1)}, u32[]{:S(2)}, u32[]{:S(2)}) collective-permute-start(f32[4,8,8,128]{3,2,1,0:T(8,128)} %get-tuple-element.28.refs_0_), channel_id=1, source_target_pairs={{0,24},{4,28},{8,16},{12,20},{16,8},{20,12},{24,0},{28,4},{1,25},{... | collective-permute-start | bytes 393224 | tf_op jit(solution)/shard_map/ppermute | solution.py:578
  11.2 0.7 %copy-start.5 = (bf16[32,256]{1,0:T(8,128)(2,1)S(1)}, bf16[32,256]{1,0:T(8,128)(2,1)}, u32[]{:S(2)}) copy-start(bf16[32,256]{1,0:T(8,128)(2,1)} %param.12) | copy-start | bytes 49156
  11.2 0.9 %copy-start.1 = (f32[6,4,8,128]{3,2,1,0:T(8,128)S(1)}, f32[6,4,8,128]{3,2,1,0:T(8,128)}, u32[]{:S(2)}) copy-start(f32[6,4,8,128]{3,2,1,0:T(8,128)} %mom.5) | copy-start | bytes 294916
  11.9 0.9 %copy-start = (f32[6,4,8,128]{3,2,1,0:T(8,128)S(1)}, f32[6,4,8,128]{3,2,1,0:T(8,128)}, u32[]{:S(2)}) copy-start(f32[6,4,8,128]{3,2,1,0:T(8,128)} %disp.7) | copy-start | bytes 294916
  12.8 3.3 %collective-permute-start.3 = (f32[6,8,128]{2,1,0:T(8,128)S(1)}, f32[6,8,128]{2,1,0:T(8,128)S(1)}, u32[]{:S(2)}, u32[]{:S(2)}) collective-permute-start(f32[6,8,128]{2,1,0:T(8,128)S(1)} %get-tuple-element.21), channel_id=1, source_target_pairs={{0,4},{4,8},{8,12},{12,0},{16,20},{20,24},{24,28},{28,16},{1,5},{5... | collective-permute-start | bytes 73736 | tf_op jit(solution)/shard_map/ppermute | solution.py:575
  12.9 3.8 %collective-permute-start.4 = (f32[6,8,128]{2,1,0:T(8,128)S(1)}, f32[6,8,128]{2,1,0:T(8,128)S(1)}, u32[]{:S(2)}, u32[]{:S(2)}) collective-permute-start(f32[6,8,128]{2,1,0:T(8,128)S(1)} %get-tuple-element.22), channel_id=1, source_target_pairs={{0,12},{4,0},{8,4},{12,8},{16,28},{20,16},{24,20},{28,24},{1,13},{... | collective-permute-start | bytes 73736 | tf_op jit(solution)/shard_map/ppermute | solution.py:575
  14.7 3.2 %copy-start.7 = (f32[256]{0:T(256)S(1)}, f32[256]{0:T(256)}, u32[]{:S(2)}) copy-start(f32[256]{0:T(256)} %param.13) | copy-start | bytes 3076
  16.1 4.2 %collective-permute-start.5 = (f32[6,8,128]{2,1,0:T(8,128)S(1)}, f32[6,8,128]{2,1,0:T(8,128)S(1)}, u32[]{:S(2)}, u32[]{:S(2)}) collective-permute-start(f32[6,8,128]{2,1,0:T(8,128)S(1)} %get-tuple-element.21), channel_id=1, source_target_pairs={{0,20},{4,24},{8,28},{12,16},{16,4},{20,8},{24,12},{28,0},{1,21},{... | collective-permute-start | bytes 73736 | tf_op jit(solution)/shard_map/ppermute | solution.py:575
  16.7 1.2 %copy-start.6 = (bf16[256,4]{0,1:T(4,128)(2,1)S(1)}, bf16[256,4]{0,1:T(4,128)(2,1)}, u32[]{:S(2)}) copy-start(bf16[256,4]{0,1:T(4,128)(2,1)} %param.15) | copy-start | bytes 6148
  16.7 8.8 %collective-permute-start.2 = (f32[2,12,8,128]{3,2,1,0:T(8,128)S(1)}, f32[2,12,8,128]{3,2,1,0:T(8,128)S(1)}, u32[]{:S(2)}, u32[]{:S(2)}) collective-permute-start(f32[2,12,8,128]{3,2,1,0:T(8,128)S(1)} %get-tuple-element.20), channel_id=1, source_target_pairs={{0,16},{4,20},{8,24},{12,28},{16,0},{20,4},{24,8},{28,12},{1,17},{... | collective-permute-start | bytes 294920 | tf_op jit(solution)/shard_map/ppermute | solution.py:575
  20.3 5.2 %collective-permute-start.6 = (f32[6,8,128]{2,1,0:T(8,128)S(1)}, f32[6,8,128]{2,1,0:T(8,128)S(1)}, u32[]{:S(2)}, u32[]{:S(2)}) collective-permute-start(f32[6,8,128]{2,1,0:T(8,128)S(1)} %get-tuple-element.22), channel_id=1, source_target_pairs={{0,28},{4,16},{8,20},{12,24},{16,12},{20,0},{24,4},{28,8},{1,29},{... | collective-permute-start | bytes 73736 | tf_op jit(solution)/shard_map/ppermute | solution.py:575
  25.5 11.7 %copy-start.2 = (f32[4,8,8,128]{3,2,1,0:T(8,128)S(1)}, f32[4,8,8,128]{3,2,1,0:T(8,128)}, u32[]{:S(2)}) copy-start(f32[4,8,8,128]{3,2,1,0:T(8,128)} %get-tuple-element.28.refs_0_) | copy-start | bytes 393220
  25.5 17.5 %copy-start.3 = (f32[6,4,8,128]{3,2,1,0:T(8,128)S(1)}, f32[6,4,8,128]{3,2,1,0:T(8,128)}, u32[]{:S(2)}) copy-start(f32[6,4,8,128]{3,2,1,0:T(8,128)} %vel.1) | copy-start | bytes 294916
  33.6 4.5 %collective-permute-start.15 = (f32[18,8,128]{2,1,0:T(8,128)S(1)}, f32[18,8,128]{2,1,0:T(8,128)S(1)}, u32[]{:S(2)}, u32[]{:S(2)}) collective-permute-start(f32[18,8,128]{2,1,0:T(8,128)S(1)} %get-tuple-element.32.refs_8_), channel_id=1, source_target_pairs={{0,8},{4,12},{8,0},{12,4},{16,24},{20,28},{24,16},{28,20},{1,9},{5... | collective-permute-start | bytes 221192 | tf_op jit(solution)/shard_map/ppermute | solution.py:578
  35.3 4.8 %collective-permute-start.17 = (f32[18,8,128]{2,1,0:T(8,128)S(1)}, f32[18,8,128]{2,1,0:T(8,128)S(1)}, u32[]{:S(2)}, u32[]{:S(2)}) collective-permute-start(f32[18,8,128]{2,1,0:T(8,128)S(1)} %get-tuple-element.32.refs_8_), channel_id=1, source_target_pairs={{0,16},{4,20},{8,24},{12,28},{16,0},{20,4},{24,8},{28,12},{1,17},{... | collective-permute-start | bytes 221192 | tf_op jit(solution)/shard_map/ppermute | solution.py:578
  36.8 5.3 %collective-permute-start.19 = (f32[18,8,128]{2,1,0:T(8,128)S(1)}, f32[18,8,128]{2,1,0:T(8,128)S(1)}, u32[]{:S(2)}, u32[]{:S(2)}) collective-permute-start(f32[18,8,128]{2,1,0:T(8,128)S(1)} %get-tuple-element.32.refs_8_), channel_id=1, source_target_pairs={{0,24},{4,28},{8,16},{12,20},{16,8},{20,12},{24,0},{28,4},{1,25},{... | collective-permute-start | bytes 221192 | tf_op jit(solution)/shard_map/ppermute | solution.py:578
  37.2 5.4 %collective-permute-start.10 = (f32[4,8,8,128]{3,2,1,0:T(8,128)S(1)}, f32[4,8,8,128]{3,2,1,0:T(8,128)S(1)}, u32[]{:S(2)}, u32[]{:S(2)}) collective-permute-start(f32[4,8,8,128]{3,2,1,0:T(8,128)S(1)} %copy-done.2), channel_id=1, source_target_pairs={{0,4},{4,0},{8,12},{12,8},{16,20},{20,16},{24,28},{28,24},{1,5},{5... | collective-permute-start | bytes 393224 | tf_op jit(solution)/shard_map/ppermute | solution.py:578
  38.0 4.6 %collective-permute-start.11 = (f32[4,8,8,128]{3,2,1,0:T(8,128)S(1)}, f32[4,8,8,128]{3,2,1,0:T(8,128)S(1)}, u32[]{:S(2)}, u32[]{:S(2)}) collective-permute-start(f32[4,8,8,128]{3,2,1,0:T(8,128)S(1)} %collective-permute-done.7.refs_2_), channel_id=1, source_target_pairs={{0,4},{4,0},{8,12},{12,8},{16,20},{20,16},{24,28},{28,24},{1,5},{5... | collective-permute-start | bytes 393224 | tf_op jit(solution)/shard_map/ppermute | solution.py:578
  38.1 3.9 %collective-permute-start.14 = (f32[18,8,128]{2,1,0:T(8,128)S(1)}, f32[18,8,128]{2,1,0:T(8,128)S(1)}, u32[]{:S(2)}, u32[]{:S(2)}) collective-permute-start(f32[18,8,128]{2,1,0:T(8,128)S(1)} %get-tuple-element.32.refs_8_), channel_id=1, source_target_pairs={{0,4},{4,0},{8,12},{12,8},{16,20},{20,16},{24,28},{28,24},{1,5},{5... | collective-permute-start | bytes 221192 | tf_op jit(solution)/shard_map/ppermute | solution.py:578
  40.0 3.8 %collective-permute-start.12 = (f32[4,8,8,128]{3,2,1,0:T(8,128)S(1)}, f32[4,8,8,128]{3,2,1,0:T(8,128)S(1)}, u32[]{:S(2)}, u32[]{:S(2)}) collective-permute-start(f32[4,8,8,128]{3,2,1,0:T(8,128)S(1)} %collective-permute-done.8.refs_4_), channel_id=1, source_target_pairs={{0,4},{4,0},{8,12},{12,8},{16,20},{20,16},{24,28},{28,24},{1,5},{5... | collective-permute-start | bytes 393224 | tf_op jit(solution)/shard_map/ppermute | solution.py:578
  42.0 1.7 %collective-permute-start.13 = (f32[4,8,8,128]{3,2,1,0:T(8,128)S(1)}, f32[4,8,8,128]{3,2,1,0:T(8,128)S(1)}, u32[]{:S(2)}, u32[]{:S(2)}) collective-permute-start(f32[4,8,8,128]{3,2,1,0:T(8,128)S(1)} %collective-permute-done.9.refs_6_), channel_id=1, source_target_pairs={{0,4},{4,0},{8,12},{12,8},{16,20},{20,16},{24,28},{28,24},{1,5},{5... | collective-permute-start | bytes 393224 | tf_op jit(solution)/shard_map/ppermute | solution.py:578
  42.0 1.7 %collective-permute-start.16 = (f32[18,8,128]{2,1,0:T(8,128)S(1)}, f32[18,8,128]{2,1,0:T(8,128)S(1)}, u32[]{:S(2)}, u32[]{:S(2)}) collective-permute-start(f32[18,8,128]{2,1,0:T(8,128)S(1)} %collective-permute-done.15.refs_10_), channel_id=1, source_target_pairs={{0,4},{4,0},{8,12},{12,8},{16,20},{20,16},{24,28},{28,24},{1,5},{5... | collective-permute-start | bytes 221192 | tf_op jit(solution)/shard_map/ppermute | solution.py:578
  42.6 1.3 %collective-permute-start.18 = (f32[18,8,128]{2,1,0:T(8,128)S(1)}, f32[18,8,128]{2,1,0:T(8,128)S(1)}, u32[]{:S(2)}, u32[]{:S(2)}) collective-permute-start(f32[18,8,128]{2,1,0:T(8,128)S(1)} %collective-permute-done.17.refs_12_), channel_id=1, source_target_pairs={{0,4},{4,0},{8,12},{12,8},{16,20},{20,16},{24,28},{28,24},{1,5},{5... | collective-permute-start | bytes 221192 | tf_op jit(solution)/shard_map/ppermute | solution.py:578
  42.6 1.4 %collective-permute-start.20 = (f32[18,8,128]{2,1,0:T(8,128)S(1)}, f32[18,8,128]{2,1,0:T(8,128)S(1)}, u32[]{:S(2)}, u32[]{:S(2)}) collective-permute-start(f32[18,8,128]{2,1,0:T(8,128)S(1)} %collective-permute-done.19.refs_14_), channel_id=1, source_target_pairs={{0,4},{4,0},{8,12},{12,8},{16,20},{20,16},{24,28},{28,24},{1,5},{5... | collective-permute-start | bytes 221192 | tf_op jit(solution)/shard_map/ppermute | solution.py:578

commit v3 on v2

--- a/solution.py
+++ b/solution.py
@@ -119,57 +119,66 @@
     lane, sub = iota(1), iota(0)
     block = lane_block()
     edge_x = XL - 1 if p == 0 else 0
-    for i in range(6):
-        src = disp if i < 3 else mom
-        k = i % 3
-        c = [src[3 * q + k, x] for x in range(XL)]
-        h = slab[(0 if i < 3 else 6) + 3 * q + k]
-        fc, fh = (xf[2 * i], xf[2 * i + 1]) if halo else (None, None)
-
-        def wide(row):
-            return jnp.broadcast_to(row, TILE)
-
-        for dy in range(2):
-            if dy:
-                step = 1 if p == 0 else -1
-                put = sub == (0 if p == 0 else SUB - 1)
-                c = [rows(c[x], step) for x in range(XL)]
-                h = rows(h, step)
-                if halo:
-                    c = [jnp.where(put, wide(yr[i, x : x + 1, :]), c[x]) for x in range(XL)]
-                    h = jnp.where(put, wide(yr[i, XL : XL + 1, :]), h)
-                    fc = jnp.where(put, wide(xyr[i, edge_x : edge_x + 1, :]), rows(fc, step))
-                    fh = jnp.where(put, wide(xyr[i, XL : XL + 1, :]), rows(fh, step))
-            for dz in range(2):
-                if dz == 0:
-                    cs, hs, fcs, fhs = c, h, fc, fh
-                else:
+
+    def component(k, carry):
+        for half in range(2):
+            i = 3 * half + k
+            src = mom if half else disp
+            c = [src[3 * q + k, x] for x in range(XL)]
+            h = slab[6 * half + 3 * q + k]
+            fc, fh = (xf[2 * i], xf[2 * i + 1]) if halo else (None, None)
+
+            def wide(row):
+                return jnp.broadcast_to(row, TILE)
+
+            for dy in range(2):
+                if dy:
                     step = 1 if p == 0 else -1
-                    seam = LANE - 1 if p == 0 else 0
-                    at_seam = lane == seam
-                    at_seams = (lane & (SLAB - 1)) == (SLAB - 1 if p == 0 else 0)
-                    cs = [
-                        lanes(jnp.where(at_seam, lanes(h, -SLAB * ORDER[x]), c[x]), step)
-                        for x in range(XL)
-                    ]
+                    put = sub == (0 if p == 0 else SUB - 1)
+                    c = [rows(c[x], step) for x in range(XL)]
+                    h = rows(h, step)
                     if halo:
-                        hs = lanes(jnp.where(at_seams, merge_blocks([c[x] for x in ORDER]), h), step)
-                        fcs = lanes(jnp.where(at_seam, lanes(fh, -SLAB * ORDER[edge_x]), fc), step)
-                        fhs = lanes(jnp.where(at_seams, lanes(fc, SLAB * ORDER[edge_x]), fh), step)
-                at = 2 * dy + dz
-                for x in range(XL):
-                    near[i, at, x + 1 - p] = cs[x]
-                if not halo:
-                    continue
-                near[i, at, XL * p] = fcs
-                near[i, at, XL + 1] = hs
-                if p == 0:
-                    moved = jnp.where(block == 0, lanes(fhs, SLAB), lanes(hs, 2 * SLAB))
-                    moved = jnp.where(block == 1, lanes(hs, -SLAB), moved)
-                else:
-                    moved = jnp.where(block == 3, lanes(fhs, -SLAB), lanes(hs, 2 * SLAB))
-                    moved = jnp.where(block == 2, lanes(hs, SLAB), moved)
-                near[i, at, XL + 2] = moved
+                        c = [jnp.where(put, wide(yr[i, x : x + 1, :]), c[x]) for x in range(XL)]
+                        h = jnp.where(put, wide(yr[i, XL : XL + 1, :]), h)
+                        fc = jnp.where(put, wide(xyr[i, edge_x : edge_x + 1, :]), rows(fc, step))
+                        fh = jnp.where(put, wide(xyr[i, XL : XL + 1, :]), rows(fh, step))
+                for dz in range(2):
+                    if dz == 0:
+                        cs, hs, fcs, fhs = c, h, fc, fh
+                    else:
+                        step = 1 if p == 0 else -1
+                        seam = LANE - 1 if p == 0 else 0
+                        at_seam = lane == seam
+                        at_seams = (lane & (SLAB - 1)) == (SLAB - 1 if p == 0 else 0)
+                        cs = [
+                            lanes(jnp.where(at_seam, lanes(h, -SLAB * ORDER[x]), c[x]), step)
+                            for x in range(XL)
+                        ]
+                        if halo:
+                            hs = lanes(jnp.where(at_seams, merge_blocks([c[x] for x in ORDER]), h), step)
+                            fcs = lanes(jnp.where(at_seam, lanes(fh, -SLAB * ORDER[edge_x]), fc), step)
+                            fhs = lanes(jnp.where(at_seams, lanes(fc, SLAB * ORDER[edge_x]), fh), step)
+                    at = 2 * dy + dz
+                    for x in range(XL):
+                        near[i, at, x + 1 - p] = cs[x]
+                    if not halo:
+                        continue
+                    near[i, at, XL * p] = fcs
+                    near[i, at, XL + 1] = hs
+                    if p == 0:
+                        moved = jnp.where(block == 0, lanes(fhs, SLAB), lanes(hs, 2 * SLAB))
+                        moved = jnp.where(block == 1, lanes(hs, -SLAB), moved)
+                    else:
+                        moved = jnp.where(block == 3, lanes(fhs, -SLAB), lanes(hs, 2 * SLAB))
+                        moved = jnp.where(block == 2, lanes(hs, SLAB), moved)
+                    near[i, at, XL + 2] = moved
+        return carry
+
+    if halo:
+        lax.fori_loop(0, 3, component, 0)
+    else:
+        for k in range(3):
+            component(k, 0)
 
 
 def feature_rows(p, disp, mom, slab, near, table, slots):
@@ -420,7 +429,8 @@
         q = 1 - p
         y_move = y_last if p == 0 else y_next
         z_move = z_last if p == 0 else z_next
-        for k in range(3):
+
+        def component(k, carry):
             for r in range(ny):
                 e = row_mask(r, 0)
                 for ref, to, size in ((mc, tc, xh_all), (mh, th, groups)):
@@ -453,6 +463,9 @@
                             whole, split = split, whole
                         to[0, k, r, j] = jnp.where(e, whole, split)
                         to[1, k, r, j] = jnp.where(e, split, whole)
+            return carry
+
+        lax.fori_loop(0, 3, component, 0)
 
     def turn(p, par, bit, half_turns):
         opp = 1 - par

time: 56.3 us -> 52.4 us (0.931)
  Pallas kernels: 27.5 us -> 23.7 us
    pallas_call x6, Pallas kernels: 27.5 us -> 23.7 us  [vmem_call(): pl.pallas_call(body, out_shape=tuple((jax.ShapeDtypeStruct(s, d) for s, d...]
  transfers between devices with their start and end apart: 21 -> 21, of which waited for: 5 -> 5; matrix products, arithmetic and copies ran while one was open for 1% -> 1% of each run, Pallas kernels for 24% -> 21%
where the time goes in v3:
time: 52.4 us; the launch traced here: 52.2 us
  Pallas kernels  23.7 us (45%)
  starting transfers between devices  18.6 us (35%)
  waiting for transfers between devices  7.32 us (14%)
  local copies, waits for them, and re-layouts  1.76 us (3%)
  between operations  0.81 us (2%)
    pallas_call x6, Pallas kernels, vmem_call(): pl.pallas_call(body, out_shape=tuple((jax.ShapeDtypeStruct(s, d) for s, d...  23.7 us
    ppermute x14, starting transfers between devices, swap(): return lax.ppermute(v, plane, pairs(lambda x, y: (x ^ mx, y ^ my)))  9.69 us
    ppermute x2, starting transfers between devices, along_z(): return lax.ppermute(v, 'gz', [(i, (i + step) % nz) for i in range(nz)])  5.2 us
    ppermute x5, waiting for transfers between devices, shift(): return lax.ppermute(v, plane, pairs(lambda x, y: (x + dx, y + dy)))  3.87 us
    ppermute x5, starting transfers between devices, shift(): return lax.ppermute(v, plane, pairs(lambda x, y: (x + dx, y + dy)))  3.73 us
    ppermute x14, waiting for transfers between devices, swap(): return lax.ppermute(v, plane, pairs(lambda x, y: (x ^ mx, y ^ my)))  3.44 us
    unnamed x17, local copies, waits for them, and re-layouts  1.57 us
  transfers between devices with their start and end apart: 21, of which 5 were waited for; matrix products, arithmetic and copies ran while one was open for 1% of the time, Pallas kernels for 21%

profile of v3, /device:TPU:0, one launch (start us, length us, event | category | flops | bytes accessed | tf_op | source)
XLA Modules:
  0.0 52.2 jit_solution(2308154919193421881)
XLA Ops:
  0.6 1.7 %shard_map.103 = (f32[14,8,128]{2,1,0:T(8,128)}, f32[4,8,8,128]{3,2,1,0:T(8,128)}) custom-call(f32[6,4,8,128]{3,2,1,0:T(8,128)} %disp.7, f32[6,4,8,128]{3,2,1,0:T(8,128)} %mom.5, s32[2,4,8,128]{3,2,1,0:T(8,128)} %bit_in.1), custom_call_target="tpu_custom_call" | custom-call | tf_op jit(solution)/shard_map/pallas_call | solution.py:57
  2.4 3.1 %collective-permute-start = (f32[14,8,128]{2,1,0:T(8,128)}, f32[14,8,128]{2,1,0:T(8,128)S(1)}, u32[]{:S(2)}, u32[]{:S(2)}) collective-permute-start(f32[14,8,128]{2,1,0:T(8,128)} %get-tuple-element.18), channel_id=1, source_target_pairs={{0,1},{1,2},{2,3},{3,0},{4,5},{5,6},{6,7},{7,4},{8,9},{9,10},{10,1... | collective-permute-start | bytes 172040 | tf_op jit(solution)/shard_map/ppermute | solution.py:594
  5.5 2.1 %collective-permute-start.1 = (f32[14,8,128]{2,1,0:T(8,128)}, f32[14,8,128]{2,1,0:T(8,128)S(1)}, u32[]{:S(2)}, u32[]{:S(2)}) collective-permute-start(f32[14,8,128]{2,1,0:T(8,128)} %get-tuple-element.18), channel_id=1, source_target_pairs={{0,3},{1,0},{2,1},{3,2},{4,7},{5,4},{6,5},{7,6},{8,11},{9,8},{10,9... | collective-permute-start | bytes 172040 | tf_op jit(solution)/shard_map/ppermute | solution.py:594
  7.6 1.6 %collective-permute-start.7 = (f32[4,8,8,128]{3,2,1,0:T(8,128)}, f32[4,8,8,128]{3,2,1,0:T(8,128)S(1)}, u32[]{:S(2)}, u32[]{:S(2)}) collective-permute-start(f32[4,8,8,128]{3,2,1,0:T(8,128)} %get-tuple-element.28.refs_0_), channel_id=1, source_target_pairs={{0,8},{4,12},{8,0},{12,4},{16,24},{20,28},{24,16},{28,20},{1,9},{5... | collective-permute-start | bytes 393224 | tf_op jit(solution)/shard_map/ppermute | solution.py:591
  9.2 1.5 %collective-permute-start.8 = (f32[4,8,8,128]{3,2,1,0:T(8,128)}, f32[4,8,8,128]{3,2,1,0:T(8,128)S(1)}, u32[]{:S(2)}, u32[]{:S(2)}) collective-permute-start(f32[4,8,8,128]{3,2,1,0:T(8,128)} %get-tuple-element.28.refs_0_), channel_id=1, source_target_pairs={{0,16},{4,20},{8,24},{12,28},{16,0},{20,4},{24,8},{28,12},{1,17},{... | collective-permute-start | bytes 393224 | tf_op jit(solution)/shard_map/ppermute | solution.py:591
  10.8 0.3 collective-permute-start.9
  11.1 0.1 copy.14
  11.2 0.0 copy-start.5
  11.2 0.0 copy-start.1
  11.2 0.7 %copy-done.5 = bf16[32,256]{1,0:T(8,128)(2,1)S(1)} copy-done((bf16[32,256]{1,0:T(8,128)(2,1)S(1)}, bf16[32,256]{1,0:T(8,128)(2,1)}, u32[]{:S(2)}) %copy-start.5) | copy-done | bytes 16408
  11.9 0.1 copy.13
  12.0 0.0 collective-permute-done.1.high
  12.0 0.1 copy-done.1
  12.1 0.7 %copy-done = f32[6,4,8,128]{3,2,1,0:T(8,128)S(1)} copy-done((f32[6,4,8,128]{3,2,1,0:T(8,128)S(1)}, f32[6,4,8,128]{3,2,1,0:T(8,128)}, u32[]{:S(2)}) %copy-start) | copy-done | bytes 98328
  12.8 0.1 collective-permute-start.3
  12.9 1.7 %collective-permute-start.4 = (f32[6,8,128]{2,1,0:T(8,128)S(1)}, f32[6,8,128]{2,1,0:T(8,128)S(1)}, u32[]{:S(2)}, u32[]{:S(2)}) collective-permute-start(f32[6,8,128]{2,1,0:T(8,128)S(1)} %get-tuple-element.22), channel_id=1, source_target_pairs={{0,12},{4,0},{8,4},{12,8},{16,28},{20,16},{24,20},{28,24},{1,13},{... | collective-permute-start | bytes 73736 | tf_op jit(solution)/shard_map/ppermute | solution.py:588
  14.7 0.0 copy-start.7
  14.7 1.5 %collective-permute-done.3.yup = f32[6,8,128]{2,1,0:T(8,128)S(1)} collective-permute-done((f32[6,8,128]{2,1,0:T(8,128)S(1)}, f32[6,8,128]{2,1,0:T(8,128)S(1)}, u32[]{:S(2)}, u32[]{:S(2)}) %collective-permute-start.3) | collective-permute-done | bytes 24608 | tf_op jit(solution)/shard_map/ppermute | solution.py:588
  16.1 0.6 %collective-permute-start.5 = (f32[6,8,128]{2,1,0:T(8,128)S(1)}, f32[6,8,128]{2,1,0:T(8,128)S(1)}, u32[]{:S(2)}, u32[]{:S(2)}) collective-permute-start(f32[6,8,128]{2,1,0:T(8,128)S(1)} %get-tuple-element.21), channel_id=1, source_target_pairs={{0,20},{4,24},{8,28},{12,16},{16,4},{20,8},{24,12},{28,0},{1,21},{... | collective-permute-start | bytes 73736 | tf_op jit(solution)/shard_map/ppermute | solution.py:588
  16.7 0.0 collective-permute-done.4.ydn
  16.7 1.2 %collective-permute-start.2 = (f32[2,12,8,128]{3,2,1,0:T(8,128)S(1)}, f32[2,12,8,128]{3,2,1,0:T(8,128)S(1)}, u32[]{:S(2)}, u32[]{:S(2)}) collective-permute-start(f32[2,12,8,128]{3,2,1,0:T(8,128)S(1)} %get-tuple-element.20), channel_id=1, source_target_pairs={{0,16},{4,20},{8,24},{12,28},{16,0},{20,4},{24,8},{28,12},{1,17},{... | collective-permute-start | bytes 294920 | tf_op jit(solution)/shard_map/ppermute | solution.py:588
  17.9 2.4 %collective-permute-done.5.xyup = f32[6,8,128]{2,1,0:T(8,128)S(1)} collective-permute-done((f32[6,8,128]{2,1,0:T(8,128)S(1)}, f32[6,8,128]{2,1,0:T(8,128)S(1)}, u32[]{:S(2)}, u32[]{:S(2)}) %collective-permute-start.5) | collective-permute-done | bytes 24608 | tf_op jit(solution)/shard_map/ppermute | solution.py:588
  20.3 0.2 collective-permute-start.6
  20.5 0.1 broadcast_in_dim.2.b_in
  20.6 4.9 %shard_map.105.inner = f32[11,64,128]{2,1,0:T(8,128)S(1)} custom-call(f32[6,4,8,128]{3,2,1,0:T(8,128)S(1)} %copy-done, f32[6,4,8,128]{3,2,1,0:T(8,128)S(1)} %copy-done.1, f32[14,8,128]{2,1,0:T(8,128)S(1)} %get-tuple-element.19.slab, bf16[256,32]{1,0:T(8,128)(2,1)S(1)} %fusion.1.w_in, f32[256,128]{1,0:T(8,128)S(1)} %broadcast_in_dim.2.b_in, ...), custom_call_target="tpu_custom_call" | custom-call | flops 1000000000 | bytes 2097152 | tf_op jit(solution)/shard_map/pallas_call | solution.py:57
  25.5 0.0 copy-start.3
  25.5 0.0 collective-permute-done.2.xup.xdn
  25.5 5.4 %shard_map.106 = (f32[18,8,128]{2,1,0:T(8,128)S(1)}, f32[6,4,8,128]{3,2,1,0:T(8,128)S(1)}) custom-call(f32[6,4,8,128]{3,2,1,0:T(8,128)S(1)} %copy-done, f32[6,4,8,128]{3,2,1,0:T(8,128)S(1)} %copy-done.1, f32[14,8,128]{2,1,0:T(8,128)S(1)} %get-tuple-element.19.slab, f32[2,12,8,128]{3,2,1,0:T(8,128)S(1)} %collective-permute-done.2.xup.xdn, ...), custom_call_target="tpu_custom_call" | custom-call | tf_op jit(solution)/shard_map/pallas_call | solution.py:57
  31.0 0.0 collective-permute-done.7.refs_2_
  31.0 0.0 collective-permute-done.8.refs_4_
  31.0 1.6 %collective-permute-start.15 = (f32[18,8,128]{2,1,0:T(8,128)S(1)}, f32[18,8,128]{2,1,0:T(8,128)S(1)}, u32[]{:S(2)}, u32[]{:S(2)}) collective-permute-start(f32[18,8,128]{2,1,0:T(8,128)S(1)} %get-tuple-element.32.refs_8_), channel_id=1, source_target_pairs={{0,8},{4,12},{8,0},{12,4},{16,24},{20,28},{24,16},{28,20},{1,9},{5... | collective-permute-start | bytes 221192 | tf_op jit(solution)/shard_map/ppermute | solution.py:591
  32.6 1.5 %collective-permute-start.17 = (f32[18,8,128]{2,1,0:T(8,128)S(1)}, f32[18,8,128]{2,1,0:T(8,128)S(1)}, u32[]{:S(2)}, u32[]{:S(2)}) collective-permute-start(f32[18,8,128]{2,1,0:T(8,128)S(1)} %get-tuple-element.32.refs_8_), channel_id=1, source_target_pairs={{0,16},{4,20},{8,24},{12,28},{16,0},{20,4},{24,8},{28,12},{1,17},{... | collective-permute-start | bytes 221192 | tf_op jit(solution)/shard_map/ppermute | solution.py:591
  34.1 0.4 collective-permute-start.19
  34.5 0.9 %collective-permute-start.10 = (f32[4,8,8,128]{3,2,1,0:T(8,128)S(1)}, f32[4,8,8,128]{3,2,1,0:T(8,128)S(1)}, u32[]{:S(2)}, u32[]{:S(2)}) collective-permute-start(f32[4,8,8,128]{3,2,1,0:T(8,128)S(1)} %copy-done.2), channel_id=1, source_target_pairs={{0,4},{4,0},{8,12},{12,8},{16,20},{20,16},{24,28},{28,24},{1,5},{5... | collective-permute-start | bytes 393224 | tf_op jit(solution)/shard_map/ppermute | solution.py:591
  35.4 0.0 collective-permute-start.11
  35.4 0.0 collective-permute-done.15.refs_10_
  35.5 0.6 %collective-permute-start.14 = (f32[18,8,128]{2,1,0:T(8,128)S(1)}, f32[18,8,128]{2,1,0:T(8,128)S(1)}, u32[]{:S(2)}, u32[]{:S(2)}) collective-permute-start(f32[18,8,128]{2,1,0:T(8,128)S(1)} %get-tuple-element.32.refs_8_), channel_id=1, source_target_pairs={{0,4},{4,0},{8,12},{12,8},{16,20},{20,16},{24,28},{28,24},{1,5},{5... | collective-permute-start | bytes 221192 | tf_op jit(solution)/shard_map/ppermute | solution.py:591
  36.0 1.4 %collective-permute-done.17.refs_12_ = f32[18,8,128]{2,1,0:T(8,128)S(1)} collective-permute-done((f32[18,8,128]{2,1,0:T(8,128)S(1)}, f32[18,8,128]{2,1,0:T(8,128)S(1)}, u32[]{:S(2)}, u32[]{:S(2)}) %collective-permute-start.17) | collective-permute-done | bytes 73760 | tf_op jit(solution)/shard_map/ppermute | solution.py:591
  37.4 0.2 collective-permute-start.12
  37.6 1.8 %collective-permute-done.19.refs_14_ = f32[18,8,128]{2,1,0:T(8,128)S(1)} collective-permute-done((f32[18,8,128]{2,1,0:T(8,128)S(1)}, f32[18,8,128]{2,1,0:T(8,128)S(1)}, u32[]{:S(2)}, u32[]{:S(2)}) %collective-permute-start.19) | collective-permute-done | bytes 73760 | tf_op jit(solution)/shard_map/ppermute | solution.py:591
  39.4 0.0 collective-permute-start.13
  39.4 0.5 collective-permute-start.16
  39.9 0.1 collective-permute-start.18
  40.0 0.4 collective-permute-start.20
  40.4 0.7 %shard_map.107 = (f32[6,4,8,128]{3,2,1,0:T(8,128)}, f32[6,4,8,128]{3,2,1,0:T(8,128)}) custom-call(f32[6,4,8,128]{3,2,1,0:T(8,128)S(1)} %copy-done, f32[6,4,8,128]{3,2,1,0:T(8,128)S(1)} %copy-done.3, f32[6,4,8,128]{3,2,1,0:T(8,128)S(1)} %get-tuple-element.23.force), custom_call_target="tpu_custom_call" | custom-call | tf_op jit(solution)/shard_map/pallas_call | solution.py:57
  41.1 0.0 collective-permute-done.18.refs_13_
  41.2 0.2 collective-permute-done.20.refs_15_
  41.3 10.9 %shard_map.108 = f32[6,4,8,128]{3,2,1,0:T(8,128)} custom-call(f32[4,8,8,128]{3,2,1,0:T(8,128)S(1)} %copy-done.2, f32[4,8,8,128]{3,2,1,0:T(8,128)S(1)} %collective-permute-done.10.refs_1_, f32[4,8,8,128]{3,2,1,0:T(8,128)S(1)} %collective-permute-done.7.refs_2_, f32[4,8,8,128]{3,2,1,0:T(8,128)S(1)} %collective-permute-done.11.refs_3_, ...), custom_call_target="tpu_custom_call" | custom-call | tf_op jit(solution)/shard_map/pallas_call | solution.py:57
  (23 shorter events, 0.1 us)
Async XLA Ops:
  0.6 10.4 %copy-start.4 = (bf16[256,256]{1,0:T(8,128)(2,1)S(1)}, bf16[256,256]{1,0:T(8,128)(2,1)}, u32[]{:S(2)}) copy-start(bf16[256,256]{1,0:T(8,128)(2,1)} %param.14) | copy-start | bytes 393220
  2.4 9.6 %collective-permute-start = (f32[14,8,128]{2,1,0:T(8,128)}, f32[14,8,128]{2,1,0:T(8,128)S(1)}, u32[]{:S(2)}, u32[]{:S(2)}) collective-permute-start(f32[14,8,128]{2,1,0:T(8,128)} %get-tuple-element.18), channel_id=1, source_target_pairs={{0,1},{1,2},{2,3},{3,0},{4,5},{5,6},{6,7},{7,4},{8,9},{9,10},{10,1... | collective-permute-start | bytes 172040 | tf_op jit(solution)/shard_map/ppermute | solution.py:594
  5.5 6.5 %collective-permute-start.1 = (f32[14,8,128]{2,1,0:T(8,128)}, f32[14,8,128]{2,1,0:T(8,128)S(1)}, u32[]{:S(2)}, u32[]{:S(2)}) collective-permute-start(f32[14,8,128]{2,1,0:T(8,128)} %get-tuple-element.18), channel_id=1, source_target_pairs={{0,3},{1,0},{2,1},{3,2},{4,7},{5,4},{6,5},{7,6},{8,11},{9,8},{10,9... | collective-permute-start | bytes 172040 | tf_op jit(solution)/shard_map/ppermute | solution.py:594
  7.6 23.4 %collective-permute-start.7 = (f32[4,8,8,128]{3,2,1,0:T(8,128)}, f32[4,8,8,128]{3,2,1,0:T(8,128)S(1)}, u32[]{:S(2)}, u32[]{:S(2)}) collective-permute-start(f32[4,8,8,128]{3,2,1,0:T(8,128)} %get-tuple-element.28.refs_0_), channel_id=1, source_target_pairs={{0,8},{4,12},{8,0},{12,4},{16,24},{20,28},{24,16},{28,20},{1,9},{5... | collective-permute-start | bytes 393224 | tf_op jit(solution)/shard_map/ppermute | solution.py:591
  9.2 21.7 %collective-permute-start.8 = (f32[4,8,8,128]{3,2,1,0:T(8,128)}, f32[4,8,8,128]{3,2,1,0:T(8,128)S(1)}, u32[]{:S(2)}, u32[]{:S(2)}) collective-permute-start(f32[4,8,8,128]{3,2,1,0:T(8,128)} %get-tuple-element.28.refs_0_), channel_id=1, source_target_pairs={{0,16},{4,20},{8,24},{12,28},{16,0},{20,4},{24,8},{28,12},{1,17},{... | collective-permute-start | bytes 393224 | tf_op jit(solution)/shard_map/ppermute | solution.py:591
  10.8 20.2 %collective-permute-start.9 = (f32[4,8,8,128]{3,2,1,0:T(8,128)}, f32[4,8,8,128]{3,2,1,0:T(8,128)S(1)}, u32[]{:S(2)}, u32[]{:S(2)}) collective-permute-start(f32[4,8,8,128]{3,2,1,0:T(8,128)} %get-tuple-element.28.refs_0_), channel_id=1, source_target_pairs={{0,24},{4,28},{8,16},{12,20},{16,8},{20,12},{24,0},{28,4},{1,25},{... | collective-permute-start | bytes 393224 | tf_op jit(solution)/shard_map/ppermute | solution.py:591
  11.2 0.7 %copy-start.5 = (bf16[32,256]{1,0:T(8,128)(2,1)S(1)}, bf16[32,256]{1,0:T(8,128)(2,1)}, u32[]{:S(2)}) copy-start(bf16[32,256]{1,0:T(8,128)(2,1)} %param.12) | copy-start | bytes 49156
  11.2 0.9 %copy-start.1 = (f32[6,4,8,128]{3,2,1,0:T(8,128)S(1)}, f32[6,4,8,128]{3,2,1,0:T(8,128)}, u32[]{:S(2)}) copy-start(f32[6,4,8,128]{3,2,1,0:T(8,128)} %mom.5) | copy-start | bytes 294916
  11.9 0.9 %copy-start = (f32[6,4,8,128]{3,2,1,0:T(8,128)S(1)}, f32[6,4,8,128]{3,2,1,0:T(8,128)}, u32[]{:S(2)}) copy-start(f32[6,4,8,128]{3,2,1,0:T(8,128)} %disp.7) | copy-start | bytes 294916
  12.8 3.3 %collective-permute-start.3 = (f32[6,8,128]{2,1,0:T(8,128)S(1)}, f32[6,8,128]{2,1,0:T(8,128)S(1)}, u32[]{:S(2)}, u32[]{:S(2)}) collective-permute-start(f32[6,8,128]{2,1,0:T(8,128)S(1)} %get-tuple-element.21), channel_id=1, source_target_pairs={{0,4},{4,8},{8,12},{12,0},{16,20},{20,24},{24,28},{28,16},{1,5},{5... | collective-permute-start | bytes 73736 | tf_op jit(solution)/shard_map/ppermute | solution.py:588
  12.9 3.8 %collective-permute-start.4 = (f32[6,8,128]{2,1,0:T(8,128)S(1)}, f32[6,8,128]{2,1,0:T(8,128)S(1)}, u32[]{:S(2)}, u32[]{:S(2)}) collective-permute-start(f32[6,8,128]{2,1,0:T(8,128)S(1)} %get-tuple-element.22), channel_id=1, source_target_pairs={{0,12},{4,0},{8,4},{12,8},{16,28},{20,16},{24,20},{28,24},{1,13},{... | collective-permute-start | bytes 73736 | tf_op jit(solution)/shard_map/ppermute | solution.py:588
  14.7 3.2 %copy-start.7 = (f32[256]{0:T(256)S(1)}, f32[256]{0:T(256)}, u32[]{:S(2)}) copy-start(f32[256]{0:T(256)} %param.13) | copy-start | bytes 3076
  16.1 4.2 %collective-permute-start.5 = (f32[6,8,128]{2,1,0:T(8,128)S(1)}, f32[6,8,128]{2,1,0:T(8,128)S(1)}, u32[]{:S(2)}, u32[]{:S(2)}) collective-permute-start(f32[6,8,128]{2,1,0:T(8,128)S(1)} %get-tuple-element.21), channel_id=1, source_target_pairs={{0,20},{4,24},{8,28},{12,16},{16,4},{20,8},{24,12},{28,0},{1,21},{... | collective-permute-start | bytes 73736 | tf_op jit(solution)/shard_map/ppermute | solution.py:588
  16.7 1.2 %copy-start.6 = (bf16[256,4]{0,1:T(4,128)(2,1)S(1)}, bf16[256,4]{0,1:T(4,128)(2,1)}, u32[]{:S(2)}) copy-start(bf16[256,4]{0,1:T(4,128)(2,1)} %param.15) | copy-start | bytes 6148
  16.7 8.8 %collective-permute-start.2 = (f32[2,12,8,128]{3,2,1,0:T(8,128)S(1)}, f32[2,12,8,128]{3,2,1,0:T(8,128)S(1)}, u32[]{:S(2)}, u32[]{:S(2)}) collective-permute-start(f32[2,12,8,128]{3,2,1,0:T(8,128)S(1)} %get-tuple-element.20), channel_id=1, source_target_pairs={{0,16},{4,20},{8,24},{12,28},{16,0},{20,4},{24,8},{28,12},{1,17},{... | collective-permute-start | bytes 294920 | tf_op jit(solution)/shard_map/ppermute | solution.py:588
  20.3 5.2 %collective-permute-start.6 = (f32[6,8,128]{2,1,0:T(8,128)S(1)}, f32[6,8,128]{2,1,0:T(8,128)S(1)}, u32[]{:S(2)}, u32[]{:S(2)}) collective-permute-start(f32[6,8,128]{2,1,0:T(8,128)S(1)} %get-tuple-element.22), channel_id=1, source_target_pairs={{0,28},{4,16},{8,20},{12,24},{16,12},{20,0},{24,4},{28,8},{1,29},{... | collective-permute-start | bytes 73736 | tf_op jit(solution)/shard_map/ppermute | solution.py:588
  25.5 9.0 %copy-start.2 = (f32[4,8,8,128]{3,2,1,0:T(8,128)S(1)}, f32[4,8,8,128]{3,2,1,0:T(8,128)}, u32[]{:S(2)}) copy-start(f32[4,8,8,128]{3,2,1,0:T(8,128)} %get-tuple-element.28.refs_0_) | copy-start | bytes 393220
  25.5 14.9 %copy-start.3 = (f32[6,4,8,128]{3,2,1,0:T(8,128)S(1)}, f32[6,4,8,128]{3,2,1,0:T(8,128)}, u32[]{:S(2)}) copy-start(f32[6,4,8,128]{3,2,1,0:T(8,128)} %vel.1) | copy-start | bytes 294916
  31.0 4.5 %collective-permute-start.15 = (f32[18,8,128]{2,1,0:T(8,128)S(1)}, f32[18,8,128]{2,1,0:T(8,128)S(1)}, u32[]{:S(2)}, u32[]{:S(2)}) collective-permute-start(f32[18,8,128]{2,1,0:T(8,128)S(1)} %get-tuple-element.32.refs_8_), channel_id=1, source_target_pairs={{0,8},{4,12},{8,0},{12,4},{16,24},{20,28},{24,16},{28,20},{1,9},{5... | collective-permute-start | bytes 221192 | tf_op jit(solution)/shard_map/ppermute | solution.py:591
  32.6 4.8 %collective-permute-start.17 = (f32[18,8,128]{2,1,0:T(8,128)S(1)}, f32[18,8,128]{2,1,0:T(8,128)S(1)}, u32[]{:S(2)}, u32[]{:S(2)}) collective-permute-start(f32[18,8,128]{2,1,0:T(8,128)S(1)} %get-tuple-element.32.refs_8_), channel_id=1, source_target_pairs={{0,16},{4,20},{8,24},{12,28},{16,0},{20,4},{24,8},{28,12},{1,17},{... | collective-permute-start | bytes 221192 | tf_op jit(solution)/shard_map/ppermute | solution.py:591
  34.1 5.3 %collective-permute-start.19 = (f32[18,8,128]{2,1,0:T(8,128)S(1)}, f32[18,8,128]{2,1,0:T(8,128)S(1)}, u32[]{:S(2)}, u32[]{:S(2)}) collective-permute-start(f32[18,8,128]{2,1,0:T(8,128)S(1)} %get-tuple-element.32.refs_8_), channel_id=1, source_target_pairs={{0,24},{4,28},{8,16},{12,20},{16,8},{20,12},{24,0},{28,4},{1,25},{... | collective-permute-start | bytes 221192 | tf_op jit(solution)/shard_map/ppermute | solution.py:591
  34.5 5.4 %collective-permute-start.10 = (f32[4,8,8,128]{3,2,1,0:T(8,128)S(1)}, f32[4,8,8,128]{3,2,1,0:T(8,128)S(1)}, u32[]{:S(2)}, u32[]{:S(2)}) collective-permute-start(f32[4,8,8,128]{3,2,1,0:T(8,128)S(1)} %copy-done.2), channel_id=1, source_target_pairs={{0,4},{4,0},{8,12},{12,8},{16,20},{20,16},{24,28},{28,24},{1,5},{5... | collective-permute-start | bytes 393224 | tf_op jit(solution)/shard_map/ppermute | solution.py:591
  35.4 4.6 %collective-permute-start.11 = (f32[4,8,8,128]{3,2,1,0:T(8,128)S(1)}, f32[4,8,8,128]{3,2,1,0:T(8,128)S(1)}, u32[]{:S(2)}, u32[]{:S(2)}) collective-permute-start(f32[4,8,8,128]{3,2,1,0:T(8,128)S(1)} %collective-permute-done.7.refs_2_), channel_id=1, source_target_pairs={{0,4},{4,0},{8,12},{12,8},{16,20},{20,16},{24,28},{28,24},{1,5},{5... | collective-permute-start | bytes 393224 | tf_op jit(solution)/shard_map/ppermute | solution.py:591
  35.5 3.9 %collective-permute-start.14 = (f32[18,8,128]{2,1,0:T(8,128)S(1)}, f32[18,8,128]{2,1,0:T(8,128)S(1)}, u32[]{:S(2)}, u32[]{:S(2)}) collective-permute-start(f32[18,8,128]{2,1,0:T(8,128)S(1)} %get-tuple-element.32.refs_8_), channel_id=1, source_target_pairs={{0,4},{4,0},{8,12},{12,8},{16,20},{20,16},{24,28},{28,24},{1,5},{5... | collective-permute-start | bytes 221192 | tf_op jit(solution)/shard_map/ppermute | solution.py:591
  37.4 3.7 %collective-permute-start.12 = (f32[4,8,8,128]{3,2,1,0:T(8,128)S(1)}, f32[4,8,8,128]{3,2,1,0:T(8,128)S(1)}, u32[]{:S(2)}, u32[]{:S(2)}) collective-permute-start(f32[4,8,8,128]{3,2,1,0:T(8,128)S(1)} %collective-permute-done.8.refs_4_), channel_id=1, source_target_pairs={{0,4},{4,0},{8,12},{12,8},{16,20},{20,16},{24,28},{28,24},{1,5},{5... | collective-permute-start | bytes 393224 | tf_op jit(solution)/shard_map/ppermute | solution.py:591
  39.4 1.7 %collective-permute-start.13 = (f32[4,8,8,128]{3,2,1,0:T(8,128)S(1)}, f32[4,8,8,128]{3,2,1,0:T(8,128)S(1)}, u32[]{:S(2)}, u32[]{:S(2)}) collective-permute-start(f32[4,8,8,128]{3,2,1,0:T(8,128)S(1)} %collective-permute-done.9.refs_6_), channel_id=1, source_target_pairs={{0,4},{4,0},{8,12},{12,8},{16,20},{20,16},{24,28},{28,24},{1,5},{5... | collective-permute-start | bytes 393224 | tf_op jit(solution)/shard_map/ppermute | solution.py:591
  39.4 1.7 %collective-permute-start.16 = (f32[18,8,128]{2,1,0:T(8,128)S(1)}, f32[18,8,128]{2,1,0:T(8,128)S(1)}, u32[]{:S(2)}, u32[]{:S(2)}) collective-permute-start(f32[18,8,128]{2,1,0:T(8,128)S(1)} %collective-permute-done.15.refs_10_), channel_id=1, source_target_pairs={{0,4},{4,0},{8,12},{12,8},{16,20},{20,16},{24,28},{28,24},{1,5},{5... | collective-permute-start | bytes 221192 | tf_op jit(solution)/shard_map/ppermute | solution.py:591
  39.9 1.3 %collective-permute-start.18 = (f32[18,8,128]{2,1,0:T(8,128)S(1)}, f32[18,8,128]{2,1,0:T(8,128)S(1)}, u32[]{:S(2)}, u32[]{:S(2)}) collective-permute-start(f32[18,8,128]{2,1,0:T(8,128)S(1)} %collective-permute-done.17.refs_12_), channel_id=1, source_target_pairs={{0,4},{4,0},{8,12},{12,8},{16,20},{20,16},{24,28},{28,24},{1,5},{5... | collective-permute-start | bytes 221192 | tf_op jit(solution)/shard_map/ppermute | solution.py:591
  40.0 1.4 %collective-permute-start.20 = (f32[18,8,128]{2,1,0:T(8,128)S(1)}, f32[18,8,128]{2,1,0:T(8,128)S(1)}, u32[]{:S(2)}, u32[]{:S(2)}) collective-permute-start(f32[18,8,128]{2,1,0:T(8,128)S(1)} %collective-permute-done.19.refs_14_), channel_id=1, source_target_pairs={{0,4},{4,0},{8,12},{12,8},{16,20},{20,16},{24,28},{28,24},{1,5},{5... | collective-permute-start | bytes 221192 | tf_op jit(solution)/shard_map/ppermute | solution.py:591

commit v4 on v3

--- a/solution.py
+++ b/solution.py
@@ -65,14 +65,14 @@
     )(*args)
 
 
-def pack_body(disp_in, mom_in, bit_in, out, brick, disp, mom, bit, sems):
+def pack_body(disp_in, mom_in, bit_in, w_in, out, brick, disp, mom, w, bit, sems):
     copies = [
         pltpu.make_async_copy(source, target, sems.at[n])
-        for n, (source, target) in enumerate(((disp_in, disp), (mom_in, mom), (bit_in, bit)))
+        for n, (source, target) in enumerate(((disp_in, disp), (mom_in, mom), (bit_in, bit), (w_in, w)))
     ]
     for copy in copies:
         copy.start()
-    for copy in copies:
+    for copy in copies[:3]:
         copy.wait()
     for i in range(14):
         if i < 6:
@@ -90,6 +90,7 @@
                 even, odd = tiles[2 * xh], tiles[2 * xh + 1]
                 brick[xh, 4 * p + k] = jnp.where(e0, odd, even)
                 brick[2 + xh, 4 * p + k] = jnp.where(e0, even, odd)
+    copies[3].wait()
 
 
 def halo_body(disp, mom, low, high, slab, faces, yup, ydn):
@@ -594,23 +595,23 @@
         return lax.ppermute(v, "gz", [(i, (i + step) % nz) for i in range(nz)])
 
     w_in = (weight_in.T.astype(f32) * 0.5).astype(bf16)
-    w_mid = (weight_mid.T.astype(f32) * 0.5).astype(bf16)
     w_out = jnp.pad(weight_out.T, ((0, SUB - 4), (0, 0)))
     hidden = weight_mid.shape[0]
     b_in = jnp.broadcast_to((0.5 * bias_in)[:, None], (hidden, LANE))
 
-    packed, brick = vmem_call(
-        pack_body, [((14, *TILE), f32), ((4, 8, *TILE), f32)], displacement, moments, sector_bit,
+    packed, brick, disp_here, mom_here, w_here = vmem_call(
+        pack_body,
+        [((14, *TILE), f32), ((4, 8, *TILE), f32)] + [(displacement.shape, f32)] * 2
+        + [(weight_mid.shape, bf16)],
+        *[pltpu.with_memory_space_constraint(x, pltpu.HBM) for x in (displacement, moments, sector_bit, weight_mid)],
         space=pltpu.HBM,
-        grant=60 << 20,
         scratch=[
-            pltpu.VMEM(displacement.shape, f32),
-            pltpu.VMEM(moments.shape, f32),
             pltpu.VMEM(sector_bit.shape, sector_bit.dtype),
-            pltpu.SemaphoreType.DMA((3,)),
+            pltpu.SemaphoreType.DMA((4,)),
         ],
     )
-    low, high = along_z(packed, 1), along_z(packed, -1)
+    low = along_z(packed, 1)
+    high = along_z(packed, -1)
     far = [(mx, my) for mx in range(nx) for my in range(0, ny, 2) if mx or my]
     held = {(0, 0): brick}
     for mask in far:
@@ -618,7 +619,7 @@
     slab, faces, yup, ydn = vmem_call(
         halo_body,
         [((14, *TILE), f32), ((2, 12, *TILE), f32)] + [((6, *TILE), f32)] * 2,
-        displacement, moments, low, high,
+        disp_here, mom_here, low, high,
     )
     if nx == 2:
         faces = shift(faces, 1, 0)
@@ -628,6 +629,7 @@
     xyup, xydn = shift(yup, 1, 1), shift(ydn, -1, -1)
     yup, ydn = shift(yup, 0, 1), shift(ydn, 0, -1)
 
+    w_mid = (w_here.T.astype(f32) * 0.5).astype(bf16)
     weights = (w_in, b_in, w_mid, w_out)
     work = [
         pltpu.VMEM((6, 4, XL + 3, *TILE), f32),
@@ -637,18 +639,18 @@
         pltpu.VMEM((hidden, 2 * LANE), bf16),
     ]
     (inner,) = vmem_call(
-        inner_body, [((2 * XL + 3, SUB * SUB, LANE), f32)], displacement, moments, slab, *weights,
+        inner_body, [((2 * XL + 3, SUB * SUB, LANE), f32)], disp_here, mom_here, slab, *weights,
         scratch=work[:2] + work[3:],
         cost=pl.CostEstimate(flops=10**9, bytes_accessed=2 << 20, transcendentals=3 << 20),
     )
     cbrick, force = vmem_call(
         outer_body,
         [((18, *TILE), f32), ((6, XL, *TILE), f32)],
-        displacement, moments, slab, xup, xdn, yup, ydn, xyup, xydn, *weights, inner,
+        disp_here, mom_here, slab, xup, xdn, yup, ydn, xyup, xydn, *weights, inner,
         scratch=work,
     )
     disp_out, vel_out = vmem_call(
-        move_body, [((6, XL, *TILE), f32)] * 2, displacement, velocity, force,
+        move_body, [((6, XL, *TILE), f32)] * 2, disp_here, velocity, force,
     )
     near_masks = [(0, 0)] + far
     late = lax.optimization_barrier((cbrick, *[held[m] for m in near_masks]))

time: 52.4 us -> 52.3 us (level)
  waiting for transfers between devices: 7.32 us -> 8.54 us
  local copies, waits for them, and re-layouts: 1.76 us -> 0.98 us
  Pallas kernels: 23.7 us -> 23 us
    ppermute x2, waiting for transfers between devices: 0.01 us -> 1.55 us  [along_z(): return lax.ppermute(v, 'gz', [(i, (i + step) % nz) for i in range(nz)])]
    ppermute x5, starting transfers between devices: 3.73 us -> 5.02 us  [shift(): return lax.ppermute(v, plane, pairs(lambda x, y: (x + dx, y + dy)))]
    ppermute x14, starting transfers between devices: 9.69 us -> 8.58 us  [swap(): return lax.ppermute(v, plane, pairs(lambda x, y: (x ^ mx, y ^ my)))]
    unnamed x17 -> x8, local copies, waits for them, and re-layouts: 1.57 us -> 0.69 us
    pallas_call x6, Pallas kernels: 23.7 us -> 23 us  [vmem_call(): pl.pallas_call(body, out_shape=tuple((jax.ShapeDtypeStruct(s, d) for s, d...]
  transfers between devices with their start and end apart: 21 -> 21, of which waited for: 5 -> 8; matrix products, arithmetic and copies ran while one was open for 1% -> 1% of each run, Pallas kernels for 21% -> 21%
where the time goes in v4:
time: 52.3 us; the launch traced here: 52.1 us
  Pallas kernels  23 us (44%)
  starting transfers between devices  18.7 us (36%)
  waiting for transfers between devices  8.54 us (16%)
  local copies, waits for them, and re-layouts  0.98 us (2%)
  between operations  0.77 us (1%)
    pallas_call x6, Pallas kernels, vmem_call(): pl.pallas_call(body, out_shape=tuple((jax.ShapeDtypeStruct(s, d) for s, d...  23 us
    ppermute x14, starting transfers between devices, swap(): return lax.ppermute(v, plane, pairs(lambda x, y: (x ^ mx, y ^ my)))  8.58 us
    ppermute x2, starting transfers between devices, along_z(): return lax.ppermute(v, 'gz', [(i, (i + step) % nz) for i in range(nz)])  5.13 us
    ppermute x5, starting transfers between devices, shift(): return lax.ppermute(v, plane, pairs(lambda x, y: (x + dx, y + dy)))  5.02 us
    ppermute x14, waiting for transfers between devices, swap(): return lax.ppermute(v, plane, pairs(lambda x, y: (x ^ mx, y ^ my)))  3.5 us
    ppermute x5, waiting for transfers between devices, shift(): return lax.ppermute(v, plane, pairs(lambda x, y: (x + dx, y + dy)))  3.49 us
    ppermute x2, waiting for transfers between devices, along_z(): return lax.ppermute(v, 'gz', [(i, (i + step) % nz) for i in range(nz)])  1.55 us
  transfers between devices with their start and end apart: 21, of which 8 were waited for; matrix products, arithmetic and copies ran while one was open for 1% of the time, Pallas kernels for 21%

profile of v4, /device:TPU:0, one launch (start us, length us, event | category | flops | bytes accessed | tf_op | source)
XLA Modules:
  0.0 52.1 jit_solution(15794348908856113244)
XLA Ops:
  0.6 1.1 %shard_map.103 = (f32[14,8,128]{2,1,0:T(8,128)S(1)}, f32[4,8,8,128]{3,2,1,0:T(8,128)S(1)}, f32[6,4,8,128]{3,2,1,0:T(8,128)S(1)}, f32[6,4,8,128]{3,2,1,0:T(8,128)S(1)}, bf16[256,256]{1,0:T(8,128)(2,1)S(1)}) custom-call(f32[6,4,8,128]{3,2,1,0:T(8,128)} %disp_in.1, f32[6,4,8,128]{3,2,1,0:T(8,128)} %mom_in.1, s32[2,4,8,128]{3,2,1,0:T(8,128)} %bit_in.1, ...), custom_call_target="tpu_custom_call" | custom-call | tf_op jit(solution)/shard_map/pallas_call | solution.py:57
  1.7 5.1 %collective-permute-start.1 = (f32[14,8,128]{2,1,0:T(8,128)S(1)}, f32[14,8,128]{2,1,0:T(8,128)S(1)}, u32[]{:S(2)}, u32[]{:S(2)}) collective-permute-start(f32[14,8,128]{2,1,0:T(8,128)S(1)} %get-tuple-element.23), channel_id=1, source_target_pairs={{0,3},{1,0},{2,1},{3,2},{4,7},{5,4},{6,5},{7,6},{8,11},{9,8},{10,9... | collective-permute-start | bytes 172040 | tf_op jit(solution)/shard_map/ppermute | solution.py:595
  6.9 0.0 collective-permute-start
  6.9 2.4 %collective-permute-start.9 = (f32[4,8,8,128]{3,2,1,0:T(8,128)S(1)}, f32[4,8,8,128]{3,2,1,0:T(8,128)S(1)}, u32[]{:S(2)}, u32[]{:S(2)}) collective-permute-start(f32[4,8,8,128]{3,2,1,0:T(8,128)S(1)} %get-tuple-element.34.refs_0_), channel_id=1, source_target_pairs={{0,24},{4,28},{8,16},{12,20},{16,8},{20,12},{24,0},{28,4},{1,25},{... | collective-permute-start | bytes 393224 | tf_op jit(solution)/shard_map/ppermute | solution.py:592
  9.3 0.5 collective-permute-start.8
  9.8 0.5 %collective-permute-start.7 = (f32[4,8,8,128]{3,2,1,0:T(8,128)S(1)}, f32[4,8,8,128]{3,2,1,0:T(8,128)S(1)}, u32[]{:S(2)}, u32[]{:S(2)}) collective-permute-start(f32[4,8,8,128]{3,2,1,0:T(8,128)S(1)} %get-tuple-element.34.refs_0_), channel_id=1, source_target_pairs={{0,8},{4,12},{8,0},{12,4},{16,24},{20,28},{24,16},{28,20},{1,9},{5... | collective-permute-start | bytes 393224 | tf_op jit(solution)/shard_map/ppermute | solution.py:592
  10.4 0.1 copy.14
  10.5 0.0 copy-start.1
  10.5 0.7 %copy-done.1 = bf16[32,256]{1,0:T(8,128)(2,1)S(1)} copy-done((bf16[32,256]{1,0:T(8,128)(2,1)S(1)}, bf16[32,256]{1,0:T(8,128)(2,1)}, u32[]{:S(2)}) %copy-start.1) | copy-done | bytes 16408
  11.2 0.1 copy.13
  11.3 0.0 collective-permute-done.1.high
  11.3 1.5 %collective-permute-done.low = f32[14,8,128]{2,1,0:T(8,128)S(1)} collective-permute-done((f32[14,8,128]{2,1,0:T(8,128)S(1)}, f32[14,8,128]{2,1,0:T(8,128)S(1)}, u32[]{:S(2)}, u32[]{:S(2)}) %collective-permute-start) | collective-permute-done | bytes 57376 | tf_op jit(solution)/shard_map/ppermute | solution.py:595
  12.9 0.1 collective-permute-start.5
  12.9 2.5 %collective-permute-start.3 = (f32[6,8,128]{2,1,0:T(8,128)S(1)}, f32[6,8,128]{2,1,0:T(8,128)S(1)}, u32[]{:S(2)}, u32[]{:S(2)}) collective-permute-start(f32[6,8,128]{2,1,0:T(8,128)S(1)} %get-tuple-element.26), channel_id=1, source_target_pairs={{0,4},{4,8},{8,12},{12,0},{16,20},{20,24},{24,28},{28,16},{1,5},{5... | collective-permute-start | bytes 73736 | tf_op jit(solution)/shard_map/ppermute | solution.py:589
  15.5 1.6 %collective-permute-done.5.xyup = f32[6,8,128]{2,1,0:T(8,128)S(1)} collective-permute-done((f32[6,8,128]{2,1,0:T(8,128)S(1)}, f32[6,8,128]{2,1,0:T(8,128)S(1)}, u32[]{:S(2)}, u32[]{:S(2)}) %collective-permute-start.5) | collective-permute-done | bytes 24608 | tf_op jit(solution)/shard_map/ppermute | solution.py:589
  17.1 0.0 collective-permute-start.6
  17.1 0.3 collective-permute-done.3.yup
  17.4 1.3 %collective-permute-start.2 = (f32[2,12,8,128]{3,2,1,0:T(8,128)S(1)}, f32[2,12,8,128]{3,2,1,0:T(8,128)S(1)}, u32[]{:S(2)}, u32[]{:S(2)}) collective-permute-start(f32[2,12,8,128]{3,2,1,0:T(8,128)S(1)} %get-tuple-element.25), channel_id=1, source_target_pairs={{0,16},{4,20},{8,24},{12,28},{16,0},{20,4},{24,8},{28,12},{1,17},{... | collective-permute-start | bytes 294920 | tf_op jit(solution)/shard_map/ppermute | solution.py:589
  18.7 1.6 %collective-permute-done.6.xydn = f32[6,8,128]{2,1,0:T(8,128)S(1)} collective-permute-done((f32[6,8,128]{2,1,0:T(8,128)S(1)}, f32[6,8,128]{2,1,0:T(8,128)S(1)}, u32[]{:S(2)}, u32[]{:S(2)}) %collective-permute-start.6) | collective-permute-done | bytes 24608 | tf_op jit(solution)/shard_map/ppermute | solution.py:589
  20.3 1.1 %collective-permute-start.4 = (f32[6,8,128]{2,1,0:T(8,128)S(1)}, f32[6,8,128]{2,1,0:T(8,128)S(1)}, u32[]{:S(2)}, u32[]{:S(2)}) collective-permute-start(f32[6,8,128]{2,1,0:T(8,128)S(1)} %get-tuple-element.27), channel_id=1, source_target_pairs={{0,12},{4,0},{8,4},{12,8},{16,28},{20,16},{24,20},{28,24},{1,13},{... | collective-permute-start | bytes 73736 | tf_op jit(solution)/shard_map/ppermute | solution.py:589
  21.4 0.1 broadcast_in_dim.2.b_in
  21.5 4.9 %shard_map.105.inner = f32[11,64,128]{2,1,0:T(8,128)S(1)} custom-call(f32[6,4,8,128]{3,2,1,0:T(8,128)S(1)} %get-tuple-element.21.disp, f32[6,4,8,128]{3,2,1,0:T(8,128)S(1)} %get-tuple-element.22.mom, f32[14,8,128]{2,1,0:T(8,128)S(1)} %get-tuple-element.24.slab, bf16[256,32]{1,0:T(8,128)(2,1)S(1)} %fusion.1.w_in, f32[256,128]{1,0:T(8,128)S(1)} %broadcast_in_dim.2.b_in, ...), custom_call_target="tpu_custom_call" | custom-call | flops 1000000000 | bytes 2097152 | tf_op jit(solution)/shard_map/pallas_call | solution.py:57
  26.4 0.0 copy-start
  26.4 0.0 collective-permute-done.4.ydn
  26.5 0.0 collective-permute-done.2.xup.xdn
  26.5 5.4 %shard_map.106 = (f32[18,8,128]{2,1,0:T(8,128)S(1)}, f32[6,4,8,128]{3,2,1,0:T(8,128)S(1)}) custom-call(f32[6,4,8,128]{3,2,1,0:T(8,128)S(1)} %get-tuple-element.21.disp, f32[6,4,8,128]{3,2,1,0:T(8,128)S(1)} %get-tuple-element.22.mom, f32[14,8,128]{2,1,0:T(8,128)S(1)} %get-tuple-element.24.slab, f32[2,12,8,128]{3,2,1,0:T(8,128)S(1)} %collective-permute-done.2.xup.xdn, ...), custom_call_target="tpu_custom_call" | custom-call | tf_op jit(solution)/shard_map/pallas_call | solution.py:57
  31.9 0.0 collective-permute-done.8.refs_4_
  31.9 0.0 collective-permute-done.7.refs_2_
  31.9 1.4 %collective-permute-start.19 = (f32[18,8,128]{2,1,0:T(8,128)S(1)}, f32[18,8,128]{2,1,0:T(8,128)S(1)}, u32[]{:S(2)}, u32[]{:S(2)}) collective-permute-start(f32[18,8,128]{2,1,0:T(8,128)S(1)} %get-tuple-element.38.refs_8_), channel_id=1, source_target_pairs={{0,24},{4,28},{8,16},{12,20},{16,8},{20,12},{24,0},{28,4},{1,25},{... | collective-permute-start | bytes 221192 | tf_op jit(solution)/shard_map/ppermute | solution.py:592
  33.3 1.6 %collective-permute-start.17 = (f32[18,8,128]{2,1,0:T(8,128)S(1)}, f32[18,8,128]{2,1,0:T(8,128)S(1)}, u32[]{:S(2)}, u32[]{:S(2)}) collective-permute-start(f32[18,8,128]{2,1,0:T(8,128)S(1)} %get-tuple-element.38.refs_8_), channel_id=1, source_target_pairs={{0,16},{4,20},{8,24},{12,28},{16,0},{20,4},{24,8},{28,12},{1,17},{... | collective-permute-start | bytes 221192 | tf_op jit(solution)/shard_map/ppermute | solution.py:592
  34.9 0.6 %collective-permute-start.15 = (f32[18,8,128]{2,1,0:T(8,128)S(1)}, f32[18,8,128]{2,1,0:T(8,128)S(1)}, u32[]{:S(2)}, u32[]{:S(2)}) collective-permute-start(f32[18,8,128]{2,1,0:T(8,128)S(1)} %get-tuple-element.38.refs_8_), channel_id=1, source_target_pairs={{0,8},{4,12},{8,0},{12,4},{16,24},{20,28},{24,16},{28,20},{1,9},{5... | collective-permute-start | bytes 221192 | tf_op jit(solution)/shard_map/ppermute | solution.py:592
  35.5 0.5 collective-permute-start.11
  36.0 1.4 %collective-permute-done.19.refs_14_ = f32[18,8,128]{2,1,0:T(8,128)S(1)} collective-permute-done((f32[18,8,128]{2,1,0:T(8,128)S(1)}, f32[18,8,128]{2,1,0:T(8,128)S(1)}, u32[]{:S(2)}, u32[]{:S(2)}) %collective-permute-start.19) | collective-permute-done | bytes 73760 | tf_op jit(solution)/shard_map/ppermute | solution.py:592
  37.3 1.2 %collective-permute-done.17.refs_12_ = f32[18,8,128]{2,1,0:T(8,128)S(1)} collective-permute-done((f32[18,8,128]{2,1,0:T(8,128)S(1)}, f32[18,8,128]{2,1,0:T(8,128)S(1)}, u32[]{:S(2)}, u32[]{:S(2)}) %collective-permute-start.17) | collective-permute-done | bytes 73760 | tf_op jit(solution)/shard_map/ppermute | solution.py:592
  38.5 0.7 %collective-permute-done.15.refs_10_ = f32[18,8,128]{2,1,0:T(8,128)S(1)} collective-permute-done((f32[18,8,128]{2,1,0:T(8,128)S(1)}, f32[18,8,128]{2,1,0:T(8,128)S(1)}, u32[]{:S(2)}, u32[]{:S(2)}) %collective-permute-start.15) | collective-permute-done | bytes 73760 | tf_op jit(solution)/shard_map/ppermute | solution.py:592
  39.3 0.0 collective-permute-start.13
  39.3 0.0 collective-permute-done.14.refs_9_
  39.3 0.5 collective-permute-start.20
  39.8 0.0 collective-permute-done.10.refs_1_
  39.8 0.1 collective-permute-start.18
  39.8 0.0 collective-permute-done.11.refs_3_
  39.8 0.4 collective-permute-start.16
  40.3 0.7 %shard_map.107 = (f32[6,4,8,128]{3,2,1,0:T(8,128)}, f32[6,4,8,128]{3,2,1,0:T(8,128)}) custom-call(f32[6,4,8,128]{3,2,1,0:T(8,128)S(1)} %get-tuple-element.21.disp, f32[6,4,8,128]{3,2,1,0:T(8,128)S(1)} %copy-done, f32[6,4,8,128]{3,2,1,0:T(8,128)S(1)} %get-tuple-element.29.force), custom_call_target="tpu_custom_call" | custom-call | tf_op jit(solution)/shard_map/pallas_call | solution.py:57
  41.0 0.0 collective-permute-done.13.refs_7_
  41.0 0.0 collective-permute-done.20.refs_15_
  41.0 0.0 collective-permute-done.18.refs_13_
  41.0 0.2 collective-permute-done.16.refs_11_
  41.2 10.9 %shard_map.108 = f32[6,4,8,128]{3,2,1,0:T(8,128)} custom-call(f32[4,8,8,128]{3,2,1,0:T(8,128)S(1)} %get-tuple-element.34.refs_0_, f32[4,8,8,128]{3,2,1,0:T(8,128)S(1)} %collective-permute-done.10.refs_1_, f32[4,8,8,128]{3,2,1,0:T(8,128)S(1)} %collective-permute-done.7.refs_2_, f32[4,8,8,128]{3,2,1,0:T(8,128)S(1)} %collective-permute-done.11.refs_3_, ...), custom_call_target="tpu_custom_call" | custom-call | tf_op jit(solution)/shard_map/pallas_call | solution.py:57
  (15 shorter events, 0.1 us)
Async XLA Ops:
  1.7 9.6 %collective-permute-start.1 = (f32[14,8,128]{2,1,0:T(8,128)S(1)}, f32[14,8,128]{2,1,0:T(8,128)S(1)}, u32[]{:S(2)}, u32[]{:S(2)}) collective-permute-start(f32[14,8,128]{2,1,0:T(8,128)S(1)} %get-tuple-element.23), channel_id=1, source_target_pairs={{0,3},{1,0},{2,1},{3,2},{4,7},{5,4},{6,5},{7,6},{8,11},{9,8},{10,9... | collective-permute-start | bytes 172040 | tf_op jit(solution)/shard_map/ppermute | solution.py:595
  6.9 6.0 %collective-permute-start = (f32[14,8,128]{2,1,0:T(8,128)S(1)}, f32[14,8,128]{2,1,0:T(8,128)S(1)}, u32[]{:S(2)}, u32[]{:S(2)}) collective-permute-start(f32[14,8,128]{2,1,0:T(8,128)S(1)} %get-tuple-element.23), channel_id=1, source_target_pairs={{0,1},{1,2},{2,3},{3,0},{4,5},{5,6},{6,7},{7,4},{8,9},{9,10},{10,1... | collective-permute-start | bytes 172040 | tf_op jit(solution)/shard_map/ppermute | solution.py:595
  6.9 25.0 %collective-permute-start.9 = (f32[4,8,8,128]{3,2,1,0:T(8,128)S(1)}, f32[4,8,8,128]{3,2,1,0:T(8,128)S(1)}, u32[]{:S(2)}, u32[]{:S(2)}) collective-permute-start(f32[4,8,8,128]{3,2,1,0:T(8,128)S(1)} %get-tuple-element.34.refs_0_), channel_id=1, source_target_pairs={{0,24},{4,28},{8,16},{12,20},{16,8},{20,12},{24,0},{28,4},{1,25},{... | collective-permute-start | bytes 393224 | tf_op jit(solution)/shard_map/ppermute | solution.py:592
  9.3 22.6 %collective-permute-start.8 = (f32[4,8,8,128]{3,2,1,0:T(8,128)S(1)}, f32[4,8,8,128]{3,2,1,0:T(8,128)S(1)}, u32[]{:S(2)}, u32[]{:S(2)}) collective-permute-start(f32[4,8,8,128]{3,2,1,0:T(8,128)S(1)} %get-tuple-element.34.refs_0_), channel_id=1, source_target_pairs={{0,16},{4,20},{8,24},{12,28},{16,0},{20,4},{24,8},{28,12},{1,17},{... | collective-permute-start | bytes 393224 | tf_op jit(solution)/shard_map/ppermute | solution.py:592
  9.8 22.1 %collective-permute-start.7 = (f32[4,8,8,128]{3,2,1,0:T(8,128)S(1)}, f32[4,8,8,128]{3,2,1,0:T(8,128)S(1)}, u32[]{:S(2)}, u32[]{:S(2)}) collective-permute-start(f32[4,8,8,128]{3,2,1,0:T(8,128)S(1)} %get-tuple-element.34.refs_0_), channel_id=1, source_target_pairs={{0,8},{4,12},{8,0},{12,4},{16,24},{20,28},{24,16},{28,20},{1,9},{5... | collective-permute-start | bytes 393224 | tf_op jit(solution)/shard_map/ppermute | solution.py:592
  10.5 0.7 %copy-start.1 = (bf16[32,256]{1,0:T(8,128)(2,1)S(1)}, bf16[32,256]{1,0:T(8,128)(2,1)}, u32[]{:S(2)}) copy-start(bf16[32,256]{1,0:T(8,128)(2,1)} %param.12) | copy-start | bytes 49156
  12.9 4.2 %collective-permute-start.5 = (f32[6,8,128]{2,1,0:T(8,128)S(1)}, f32[6,8,128]{2,1,0:T(8,128)S(1)}, u32[]{:S(2)}, u32[]{:S(2)}) collective-permute-start(f32[6,8,128]{2,1,0:T(8,128)S(1)} %get-tuple-element.26), channel_id=1, source_target_pairs={{0,20},{4,24},{8,28},{12,16},{16,4},{20,8},{24,12},{28,0},{1,21},{... | collective-permute-start | bytes 73736 | tf_op jit(solution)/shard_map/ppermute | solution.py:589
  12.9 4.5 %collective-permute-start.3 = (f32[6,8,128]{2,1,0:T(8,128)S(1)}, f32[6,8,128]{2,1,0:T(8,128)S(1)}, u32[]{:S(2)}, u32[]{:S(2)}) collective-permute-start(f32[6,8,128]{2,1,0:T(8,128)S(1)} %get-tuple-element.26), channel_id=1, source_target_pairs={{0,4},{4,8},{8,12},{12,0},{16,20},{20,24},{24,28},{28,16},{1,5},{5... | collective-permute-start | bytes 73736 | tf_op jit(solution)/shard_map/ppermute | solution.py:589
  17.1 1.6 %copy-start.3 = (f32[256]{0:T(256)S(1)}, f32[256]{0:T(256)}, u32[]{:S(2)}) copy-start(f32[256]{0:T(256)} %param.13) | copy-start | bytes 3076
  17.1 3.3 %collective-permute-start.6 = (f32[6,8,128]{2,1,0:T(8,128)S(1)}, f32[6,8,128]{2,1,0:T(8,128)S(1)}, u32[]{:S(2)}, u32[]{:S(2)}) collective-permute-start(f32[6,8,128]{2,1,0:T(8,128)S(1)} %get-tuple-element.27), channel_id=1, source_target_pairs={{0,28},{4,16},{8,20},{12,24},{16,12},{20,0},{24,4},{28,8},{1,29},{... | collective-permute-start | bytes 73736 | tf_op jit(solution)/shard_map/ppermute | solution.py:589
  17.4 1.3 %copy-start.2 = (bf16[256,4]{0,1:T(4,128)(2,1)S(1)}, bf16[256,4]{0,1:T(4,128)(2,1)}, u32[]{:S(2)}) copy-start(bf16[256,4]{0,1:T(4,128)(2,1)} %param.15) | copy-start | bytes 6148
  17.4 9.1 %collective-permute-start.2 = (f32[2,12,8,128]{3,2,1,0:T(8,128)S(1)}, f32[2,12,8,128]{3,2,1,0:T(8,128)S(1)}, u32[]{:S(2)}, u32[]{:S(2)}) collective-permute-start(f32[2,12,8,128]{3,2,1,0:T(8,128)S(1)} %get-tuple-element.25), channel_id=1, source_target_pairs={{0,16},{4,20},{8,24},{12,28},{16,0},{20,4},{24,8},{28,12},{1,17},{... | collective-permute-start | bytes 294920 | tf_op jit(solution)/shard_map/ppermute | solution.py:589
  20.3 6.1 %collective-permute-start.4 = (f32[6,8,128]{2,1,0:T(8,128)S(1)}, f32[6,8,128]{2,1,0:T(8,128)S(1)}, u32[]{:S(2)}, u32[]{:S(2)}) collective-permute-start(f32[6,8,128]{2,1,0:T(8,128)S(1)} %get-tuple-element.27), channel_id=1, source_target_pairs={{0,12},{4,0},{8,4},{12,8},{16,28},{20,16},{24,20},{28,24},{1,13},{... | collective-permute-start | bytes 73736 | tf_op jit(solution)/shard_map/ppermute | solution.py:589
  26.4 13.9 %copy-start = (f32[6,4,8,128]{3,2,1,0:T(8,128)S(1)}, f32[6,4,8,128]{3,2,1,0:T(8,128)}, u32[]{:S(2)}) copy-start(f32[6,4,8,128]{3,2,1,0:T(8,128)} %vel.1) | copy-start | bytes 294916
  31.9 5.4 %collective-permute-start.19 = (f32[18,8,128]{2,1,0:T(8,128)S(1)}, f32[18,8,128]{2,1,0:T(8,128)S(1)}, u32[]{:S(2)}, u32[]{:S(2)}) collective-permute-start(f32[18,8,128]{2,1,0:T(8,128)S(1)} %get-tuple-element.38.refs_8_), channel_id=1, source_target_pairs={{0,24},{4,28},{8,16},{12,20},{16,8},{20,12},{24,0},{28,4},{1,25},{... | collective-permute-start | bytes 221192 | tf_op jit(solution)/shard_map/ppermute | solution.py:592
  33.3 5.2 %collective-permute-start.17 = (f32[18,8,128]{2,1,0:T(8,128)S(1)}, f32[18,8,128]{2,1,0:T(8,128)S(1)}, u32[]{:S(2)}, u32[]{:S(2)}) collective-permute-start(f32[18,8,128]{2,1,0:T(8,128)S(1)} %get-tuple-element.38.refs_8_), channel_id=1, source_target_pairs={{0,16},{4,20},{8,24},{12,28},{16,0},{20,4},{24,8},{28,12},{1,17},{... | collective-permute-start | bytes 221192 | tf_op jit(solution)/shard_map/ppermute | solution.py:592
  34.9 4.4 %collective-permute-start.15 = (f32[18,8,128]{2,1,0:T(8,128)S(1)}, f32[18,8,128]{2,1,0:T(8,128)S(1)}, u32[]{:S(2)}, u32[]{:S(2)}) collective-permute-start(f32[18,8,128]{2,1,0:T(8,128)S(1)} %get-tuple-element.38.refs_8_), channel_id=1, source_target_pairs={{0,8},{4,12},{8,0},{12,4},{16,24},{20,28},{24,16},{28,20},{1,9},{5... | collective-permute-start | bytes 221192 | tf_op jit(solution)/shard_map/ppermute | solution.py:592
  35.5 4.3 %collective-permute-start.10 = (f32[4,8,8,128]{3,2,1,0:T(8,128)S(1)}, f32[4,8,8,128]{3,2,1,0:T(8,128)S(1)}, u32[]{:S(2)}, u32[]{:S(2)}) collective-permute-start(f32[4,8,8,128]{3,2,1,0:T(8,128)S(1)} %get-tuple-element.34.refs_0_), channel_id=1, source_target_pairs={{0,4},{4,0},{8,12},{12,8},{16,20},{20,16},{24,28},{28,24},{1,5},{5... | collective-permute-start | bytes 393224 | tf_op jit(solution)/shard_map/ppermute | solution.py:592
  35.5 4.4 %collective-permute-start.11 = (f32[4,8,8,128]{3,2,1,0:T(8,128)S(1)}, f32[4,8,8,128]{3,2,1,0:T(8,128)S(1)}, u32[]{:S(2)}, u32[]{:S(2)}) collective-permute-start(f32[4,8,8,128]{3,2,1,0:T(8,128)S(1)} %collective-permute-done.7.refs_2_), channel_id=1, source_target_pairs={{0,4},{4,0},{8,12},{12,8},{16,20},{20,16},{24,28},{28,24},{1,5},{5... | collective-permute-start | bytes 393224 | tf_op jit(solution)/shard_map/ppermute | solution.py:592
  37.3 1.9 %collective-permute-start.14 = (f32[18,8,128]{2,1,0:T(8,128)S(1)}, f32[18,8,128]{2,1,0:T(8,128)S(1)}, u32[]{:S(2)}, u32[]{:S(2)}) collective-permute-start(f32[18,8,128]{2,1,0:T(8,128)S(1)} %get-tuple-element.38.refs_8_), channel_id=1, source_target_pairs={{0,4},{4,0},{8,12},{12,8},{16,20},{20,16},{24,28},{28,24},{1,5},{5... | collective-permute-start | bytes 221192 | tf_op jit(solution)/shard_map/ppermute | solution.py:592
  38.5 2.5 %collective-permute-start.12 = (f32[4,8,8,128]{3,2,1,0:T(8,128)S(1)}, f32[4,8,8,128]{3,2,1,0:T(8,128)S(1)}, u32[]{:S(2)}, u32[]{:S(2)}) collective-permute-start(f32[4,8,8,128]{3,2,1,0:T(8,128)S(1)} %collective-permute-done.8.refs_4_), channel_id=1, source_target_pairs={{0,4},{4,0},{8,12},{12,8},{16,20},{20,16},{24,28},{28,24},{1,5},{5... | collective-permute-start | bytes 393224 | tf_op jit(solution)/shard_map/ppermute | solution.py:592
  39.3 1.7 %collective-permute-start.13 = (f32[4,8,8,128]{3,2,1,0:T(8,128)S(1)}, f32[4,8,8,128]{3,2,1,0:T(8,128)S(1)}, u32[]{:S(2)}, u32[]{:S(2)}) collective-permute-start(f32[4,8,8,128]{3,2,1,0:T(8,128)S(1)} %collective-permute-done.9.refs_6_), channel_id=1, source_target_pairs={{0,4},{4,0},{8,12},{12,8},{16,20},{20,16},{24,28},{28,24},{1,5},{5... | collective-permute-start | bytes 393224 | tf_op jit(solution)/shard_map/ppermute | solution.py:592
  39.3 1.7 %collective-permute-start.20 = (f32[18,8,128]{2,1,0:T(8,128)S(1)}, f32[18,8,128]{2,1,0:T(8,128)S(1)}, u32[]{:S(2)}, u32[]{:S(2)}) collective-permute-start(f32[18,8,128]{2,1,0:T(8,128)S(1)} %collective-permute-done.19.refs_14_), channel_id=1, source_target_pairs={{0,4},{4,0},{8,12},{12,8},{16,20},{20,16},{24,28},{28,24},{1,5},{5... | collective-permute-start | bytes 221192 | tf_op jit(solution)/shard_map/ppermute | solution.py:592
  39.8 1.3 %collective-permute-start.18 = (f32[18,8,128]{2,1,0:T(8,128)S(1)}, f32[18,8,128]{2,1,0:T(8,128)S(1)}, u32[]{:S(2)}, u32[]{:S(2)}) collective-permute-start(f32[18,8,128]{2,1,0:T(8,128)S(1)} %collective-permute-done.17.refs_12_), channel_id=1, source_target_pairs={{0,4},{4,0},{8,12},{12,8},{16,20},{20,16},{24,28},{28,24},{1,5},{5... | collective-permute-start | bytes 221192 | tf_op jit(solution)/shard_map/ppermute | solution.py:592
  39.8 1.4 %collective-permute-start.16 = (f32[18,8,128]{2,1,0:T(8,128)S(1)}, f32[18,8,128]{2,1,0:T(8,128)S(1)}, u32[]{:S(2)}, u32[]{:S(2)}) collective-permute-start(f32[18,8,128]{2,1,0:T(8,128)S(1)} %collective-permute-done.15.refs_10_), channel_id=1, source_target_pairs={{0,4},{4,0},{8,12},{12,8},{16,20},{20,16},{24,28},{28,24},{1,5},{5... | collective-permute-start | bytes 221192 | tf_op jit(solution)/shard_map/ppermute | solution.py:592

commit v5 on v4

--- a/solution.py
+++ b/solution.py
@@ -265,7 +265,7 @@
         inner = range(1, XL) if p == 0 else range(XL - 1)
         feature_rows(p, disp, mom, slab, near, table.at[pl.ds((XL + 1) * p, XL + 1)], inner)
     total = 2 * (XL - 1) * (SUB - 1)
-    perceptron(table, heads, w_in, b_in, w_mid, w_out, one, two, inner_row, total, 4)
+    perceptron(table, heads, w_in, b_in, w_mid, w_out, one, two, inner_row, total, 8)
 
 
 def outer_body(
@@ -275,14 +275,15 @@
     e0 = odd_mask(0)
     slots = XL + 1
     for n in range(2 * slots):
-        heads[n] = inner[n]
+        if n % slots != XL and n not in (0, slots + XL - 1):
+            heads[n] = inner[n]
     for p in range(2):
         args = (xup.at[0], yup, xyup) if p == 0 else (xdn.at[xdn.shape[0] - 1], ydn, xydn)
         near_tiles(p, disp, mom, slab, args, near)
         part = table.at[pl.ds(slots * p, slots)]
         feature_rows(p, disp, mom, slab, near, part, range(slots))
     total = 2 * (2 * SUB + XL - 1)
-    perceptron(table, heads, w_in, b_in, w_mid, w_out, one, two, outer_row, total, 3)
+    perceptron(table, heads, w_in, b_in, w_mid, w_out, one, two, outer_row, total, 7)
     for p in range(2):
         coupling = []
         for slot in range(slots):

time: 52.3 us -> 51.5 us (0.985)
  Pallas kernels: 23 us -> 22.2 us
    pallas_call x6, Pallas kernels: 23 us -> 22.2 us  [vmem_call(): pl.pallas_call(body, out_shape=tuple((jax.ShapeDtypeStruct(s, d) for s, d...]
  transfers between devices with their start and end apart: 21 -> 21, of which waited for: 8 -> 8; matrix products, arithmetic and copies ran while one was open for 1% -> 1% of each run, Pallas kernels for 21% -> 20%
where the time goes in v5:
time: 51.5 us; the launch traced here: 51.3 us
  Pallas kernels  22.2 us (43%)
  starting transfers between devices  18.7 us (36%)
  waiting for transfers between devices  8.54 us (17%)
  local copies, waits for them, and re-layouts  0.98 us (2%)
  between operations  0.79 us (2%)
    pallas_call x6, Pallas kernels, vmem_call(): pl.pallas_call(body, out_shape=tuple((jax.ShapeDtypeStruct(s, d) for s, d...  22.2 us
    ppermute x14, starting transfers between devices, swap(): return lax.ppermute(v, plane, pairs(lambda x, y: (x ^ mx, y ^ my)))  8.58 us
    ppermute x2, starting transfers between devices, along_z(): return lax.ppermute(v, 'gz', [(i, (i + step) % nz) for i in range(nz)])  5.13 us
    ppermute x5, starting transfers between devices, shift(): return lax.ppermute(v, plane, pairs(lambda x, y: (x + dx, y + dy)))  5.02 us
    ppermute x14, waiting for transfers between devices, swap(): return lax.ppermute(v, plane, pairs(lambda x, y: (x ^ mx, y ^ my)))  3.5 us
    ppermute x5, waiting for transfers between devices, shift(): return lax.ppermute(v, plane, pairs(lambda x, y: (x + dx, y + dy)))  3.49 us
    ppermute x2, waiting for transfers between devices, along_z(): return lax.ppermute(v, 'gz', [(i, (i + step) % nz) for i in range(nz)])  1.55 us
  transfers between devices with their start and end apart: 21, of which 8 were waited for; matrix products, arithmetic and copies ran while one was open for 1% of the time, Pallas kernels for 20%

profile of v5, /device:TPU:0, one launch (start us, length us, event | category | flops | bytes accessed | tf_op | source)
XLA Modules:
  0.0 51.3 jit_solution(13659311080973423992)
XLA Ops:
  0.6 1.1 %shard_map.103 = (f32[14,8,128]{2,1,0:T(8,128)S(1)}, f32[4,8,8,128]{3,2,1,0:T(8,128)S(1)}, f32[6,4,8,128]{3,2,1,0:T(8,128)S(1)}, f32[6,4,8,128]{3,2,1,0:T(8,128)S(1)}, bf16[256,256]{1,0:T(8,128)(2,1)S(1)}) custom-call(f32[6,4,8,128]{3,2,1,0:T(8,128)} %disp_in.1, f32[6,4,8,128]{3,2,1,0:T(8,128)} %mom_in.1, s32[2,4,8,128]{3,2,1,0:T(8,128)} %bit_in.1, ...), custom_call_target="tpu_custom_call" | custom-call | tf_op jit(solution)/shard_map/pallas_call | solution.py:57
  1.7 5.1 %collective-permute-start.1 = (f32[14,8,128]{2,1,0:T(8,128)S(1)}, f32[14,8,128]{2,1,0:T(8,128)S(1)}, u32[]{:S(2)}, u32[]{:S(2)}) collective-permute-start(f32[14,8,128]{2,1,0:T(8,128)S(1)} %get-tuple-element.23), channel_id=1, source_target_pairs={{0,3},{1,0},{2,1},{3,2},{4,7},{5,4},{6,5},{7,6},{8,11},{9,8},{10,9... | collective-permute-start | bytes 172040 | tf_op jit(solution)/shard_map/ppermute | solution.py:596
  6.9 0.0 collective-permute-start
  6.9 2.4 %collective-permute-start.9 = (f32[4,8,8,128]{3,2,1,0:T(8,128)S(1)}, f32[4,8,8,128]{3,2,1,0:T(8,128)S(1)}, u32[]{:S(2)}, u32[]{:S(2)}) collective-permute-start(f32[4,8,8,128]{3,2,1,0:T(8,128)S(1)} %get-tuple-element.34.refs_0_), channel_id=1, source_target_pairs={{0,24},{4,28},{8,16},{12,20},{16,8},{20,12},{24,0},{28,4},{1,25},{... | collective-permute-start | bytes 393224 | tf_op jit(solution)/shard_map/ppermute | solution.py:593
  9.3 0.5 collective-permute-start.8
  9.8 0.5 %collective-permute-start.7 = (f32[4,8,8,128]{3,2,1,0:T(8,128)S(1)}, f32[4,8,8,128]{3,2,1,0:T(8,128)S(1)}, u32[]{:S(2)}, u32[]{:S(2)}) collective-permute-start(f32[4,8,8,128]{3,2,1,0:T(8,128)S(1)} %get-tuple-element.34.refs_0_), channel_id=1, source_target_pairs={{0,8},{4,12},{8,0},{12,4},{16,24},{20,28},{24,16},{28,20},{1,9},{5... | collective-permute-start | bytes 393224 | tf_op jit(solution)/shard_map/ppermute | solution.py:593
  10.4 0.1 copy.14
  10.5 0.0 copy-start.1
  10.5 0.7 %copy-done.1 = bf16[32,256]{1,0:T(8,128)(2,1)S(1)} copy-done((bf16[32,256]{1,0:T(8,128)(2,1)S(1)}, bf16[32,256]{1,0:T(8,128)(2,1)}, u32[]{:S(2)}) %copy-start.1) | copy-done | bytes 16408
  11.2 0.1 copy.13
  11.3 0.0 collective-permute-done.1.high
  11.3 1.5 %collective-permute-done.low = f32[14,8,128]{2,1,0:T(8,128)S(1)} collective-permute-done((f32[14,8,128]{2,1,0:T(8,128)S(1)}, f32[14,8,128]{2,1,0:T(8,128)S(1)}, u32[]{:S(2)}, u32[]{:S(2)}) %collective-permute-start) | collective-permute-done | bytes 57376 | tf_op jit(solution)/shard_map/ppermute | solution.py:596
  12.9 0.1 collective-permute-start.5
  12.9 2.5 %collective-permute-start.3 = (f32[6,8,128]{2,1,0:T(8,128)S(1)}, f32[6,8,128]{2,1,0:T(8,128)S(1)}, u32[]{:S(2)}, u32[]{:S(2)}) collective-permute-start(f32[6,8,128]{2,1,0:T(8,128)S(1)} %get-tuple-element.26), channel_id=1, source_target_pairs={{0,4},{4,8},{8,12},{12,0},{16,20},{20,24},{24,28},{28,16},{1,5},{5... | collective-permute-start | bytes 73736 | tf_op jit(solution)/shard_map/ppermute | solution.py:590
  15.5 1.6 %collective-permute-done.5.xyup = f32[6,8,128]{2,1,0:T(8,128)S(1)} collective-permute-done((f32[6,8,128]{2,1,0:T(8,128)S(1)}, f32[6,8,128]{2,1,0:T(8,128)S(1)}, u32[]{:S(2)}, u32[]{:S(2)}) %collective-permute-start.5) | collective-permute-done | bytes 24608 | tf_op jit(solution)/shard_map/ppermute | solution.py:590
  17.1 0.0 collective-permute-start.6
  17.1 0.3 collective-permute-done.3.yup
  17.4 1.3 %collective-permute-start.2 = (f32[2,12,8,128]{3,2,1,0:T(8,128)S(1)}, f32[2,12,8,128]{3,2,1,0:T(8,128)S(1)}, u32[]{:S(2)}, u32[]{:S(2)}) collective-permute-start(f32[2,12,8,128]{3,2,1,0:T(8,128)S(1)} %get-tuple-element.25), channel_id=1, source_target_pairs={{0,16},{4,20},{8,24},{12,28},{16,0},{20,4},{24,8},{28,12},{1,17},{... | collective-permute-start | bytes 294920 | tf_op jit(solution)/shard_map/ppermute | solution.py:590
  18.7 1.6 %collective-permute-done.6.xydn = f32[6,8,128]{2,1,0:T(8,128)S(1)} collective-permute-done((f32[6,8,128]{2,1,0:T(8,128)S(1)}, f32[6,8,128]{2,1,0:T(8,128)S(1)}, u32[]{:S(2)}, u32[]{:S(2)}) %collective-permute-start.6) | collective-permute-done | bytes 24608 | tf_op jit(solution)/shard_map/ppermute | solution.py:590
  20.3 1.1 %collective-permute-start.4 = (f32[6,8,128]{2,1,0:T(8,128)S(1)}, f32[6,8,128]{2,1,0:T(8,128)S(1)}, u32[]{:S(2)}, u32[]{:S(2)}) collective-permute-start(f32[6,8,128]{2,1,0:T(8,128)S(1)} %get-tuple-element.27), channel_id=1, source_target_pairs={{0,12},{4,0},{8,4},{12,8},{16,28},{20,16},{24,20},{28,24},{1,13},{... | collective-permute-start | bytes 73736 | tf_op jit(solution)/shard_map/ppermute | solution.py:590
  21.4 0.1 broadcast_in_dim.2.b_in
  21.5 4.4 %shard_map.105.inner = f32[11,64,128]{2,1,0:T(8,128)S(1)} custom-call(f32[6,4,8,128]{3,2,1,0:T(8,128)S(1)} %get-tuple-element.21.disp, f32[6,4,8,128]{3,2,1,0:T(8,128)S(1)} %get-tuple-element.22.mom, f32[14,8,128]{2,1,0:T(8,128)S(1)} %get-tuple-element.24.slab, bf16[256,32]{1,0:T(8,128)(2,1)S(1)} %fusion.1.w_in, f32[256,128]{1,0:T(8,128)S(1)} %broadcast_in_dim.2.b_in, ...), custom_call_target="tpu_custom_call" | custom-call | flops 1000000000 | bytes 2097152 | tf_op jit(solution)/shard_map/pallas_call | solution.py:57
  26.0 0.0 copy-start
  26.0 0.0 collective-permute-done.4.ydn
  26.0 0.0 collective-permute-done.2.xup.xdn
  26.0 5.1 %shard_map.106 = (f32[18,8,128]{2,1,0:T(8,128)S(1)}, f32[6,4,8,128]{3,2,1,0:T(8,128)S(1)}) custom-call(f32[6,4,8,128]{3,2,1,0:T(8,128)S(1)} %get-tuple-element.21.disp, f32[6,4,8,128]{3,2,1,0:T(8,128)S(1)} %get-tuple-element.22.mom, f32[14,8,128]{2,1,0:T(8,128)S(1)} %get-tuple-element.24.slab, f32[2,12,8,128]{3,2,1,0:T(8,128)S(1)} %collective-permute-done.2.xup.xdn, ...), custom_call_target="tpu_custom_call" | custom-call | tf_op jit(solution)/shard_map/pallas_call | solution.py:57
  31.1 0.0 collective-permute-done.9.refs_6_
  31.1 0.0 collective-permute-done.8.refs_4_
  31.1 0.0 collective-permute-done.7.refs_2_
  31.1 1.4 %collective-permute-start.19 = (f32[18,8,128]{2,1,0:T(8,128)S(1)}, f32[18,8,128]{2,1,0:T(8,128)S(1)}, u32[]{:S(2)}, u32[]{:S(2)}) collective-permute-start(f32[18,8,128]{2,1,0:T(8,128)S(1)} %get-tuple-element.38.refs_8_), channel_id=1, source_target_pairs={{0,24},{4,28},{8,16},{12,20},{16,8},{20,12},{24,0},{28,4},{1,25},{... | collective-permute-start | bytes 221192 | tf_op jit(solution)/shard_map/ppermute | solution.py:593
  32.5 1.6 %collective-permute-start.17 = (f32[18,8,128]{2,1,0:T(8,128)S(1)}, f32[18,8,128]{2,1,0:T(8,128)S(1)}, u32[]{:S(2)}, u32[]{:S(2)}) collective-permute-start(f32[18,8,128]{2,1,0:T(8,128)S(1)} %get-tuple-element.38.refs_8_), channel_id=1, source_target_pairs={{0,16},{4,20},{8,24},{12,28},{16,0},{20,4},{24,8},{28,12},{1,17},{... | collective-permute-start | bytes 221192 | tf_op jit(solution)/shard_map/ppermute | solution.py:593
  34.1 0.6 %collective-permute-start.15 = (f32[18,8,128]{2,1,0:T(8,128)S(1)}, f32[18,8,128]{2,1,0:T(8,128)S(1)}, u32[]{:S(2)}, u32[]{:S(2)}) collective-permute-start(f32[18,8,128]{2,1,0:T(8,128)S(1)} %get-tuple-element.38.refs_8_), channel_id=1, source_target_pairs={{0,8},{4,12},{8,0},{12,4},{16,24},{20,28},{24,16},{28,20},{1,9},{5... | collective-permute-start | bytes 221192 | tf_op jit(solution)/shard_map/ppermute | solution.py:593
  34.7 0.0 collective-permute-start.10
  34.7 0.5 collective-permute-start.11
  35.2 1.4 %collective-permute-done.19.refs_14_ = f32[18,8,128]{2,1,0:T(8,128)S(1)} collective-permute-done((f32[18,8,128]{2,1,0:T(8,128)S(1)}, f32[18,8,128]{2,1,0:T(8,128)S(1)}, u32[]{:S(2)}, u32[]{:S(2)}) %collective-permute-start.19) | collective-permute-done | bytes 73760 | tf_op jit(solution)/shard_map/ppermute | solution.py:593
  36.5 1.2 %collective-permute-done.17.refs_12_ = f32[18,8,128]{2,1,0:T(8,128)S(1)} collective-permute-done((f32[18,8,128]{2,1,0:T(8,128)S(1)}, f32[18,8,128]{2,1,0:T(8,128)S(1)}, u32[]{:S(2)}, u32[]{:S(2)}) %collective-permute-start.17) | collective-permute-done | bytes 73760 | tf_op jit(solution)/shard_map/ppermute | solution.py:593
  37.7 0.0 collective-permute-start.12
  37.7 0.7 %collective-permute-done.15.refs_10_ = f32[18,8,128]{2,1,0:T(8,128)S(1)} collective-permute-done((f32[18,8,128]{2,1,0:T(8,128)S(1)}, f32[18,8,128]{2,1,0:T(8,128)S(1)}, u32[]{:S(2)}, u32[]{:S(2)}) %collective-permute-start.15) | collective-permute-done | bytes 73760 | tf_op jit(solution)/shard_map/ppermute | solution.py:593
  38.5 0.0 collective-permute-start.13
  38.5 0.0 collective-permute-done.14.refs_9_
  38.5 0.5 collective-permute-start.20
  39.0 0.0 collective-permute-done.10.refs_1_
  39.0 0.1 collective-permute-start.18
  39.1 0.4 collective-permute-start.16
  39.5 0.7 %shard_map.107 = (f32[6,4,8,128]{3,2,1,0:T(8,128)}, f32[6,4,8,128]{3,2,1,0:T(8,128)}) custom-call(f32[6,4,8,128]{3,2,1,0:T(8,128)S(1)} %get-tuple-element.21.disp, f32[6,4,8,128]{3,2,1,0:T(8,128)S(1)} %copy-done, f32[6,4,8,128]{3,2,1,0:T(8,128)S(1)} %get-tuple-element.29.force), custom_call_target="tpu_custom_call" | custom-call | tf_op jit(solution)/shard_map/pallas_call | solution.py:57
  40.2 0.0 collective-permute-done.18.refs_13_
  40.2 0.2 collective-permute-done.16.refs_11_
  40.4 10.9 %shard_map.108 = f32[6,4,8,128]{3,2,1,0:T(8,128)} custom-call(f32[4,8,8,128]{3,2,1,0:T(8,128)S(1)} %get-tuple-element.34.refs_0_, f32[4,8,8,128]{3,2,1,0:T(8,128)S(1)} %collective-permute-done.10.refs_1_, f32[4,8,8,128]{3,2,1,0:T(8,128)S(1)} %collective-permute-done.7.refs_2_, f32[4,8,8,128]{3,2,1,0:T(8,128)S(1)} %collective-permute-done.11.refs_3_, ...), custom_call_target="tpu_custom_call" | custom-call | tf_op jit(solution)/shard_map/pallas_call | solution.py:57
  (15 shorter events, 0.1 us)
Async XLA Ops:
  1.7 9.6 %collective-permute-start.1 = (f32[14,8,128]{2,1,0:T(8,128)S(1)}, f32[14,8,128]{2,1,0:T(8,128)S(1)}, u32[]{:S(2)}, u32[]{:S(2)}) collective-permute-start(f32[14,8,128]{2,1,0:T(8,128)S(1)} %get-tuple-element.23), channel_id=1, source_target_pairs={{0,3},{1,0},{2,1},{3,2},{4,7},{5,4},{6,5},{7,6},{8,11},{9,8},{10,9... | collective-permute-start | bytes 172040 | tf_op jit(solution)/shard_map/ppermute | solution.py:596
  6.9 6.0 %collective-permute-start = (f32[14,8,128]{2,1,0:T(8,128)S(1)}, f32[14,8,128]{2,1,0:T(8,128)S(1)}, u32[]{:S(2)}, u32[]{:S(2)}) collective-permute-start(f32[14,8,128]{2,1,0:T(8,128)S(1)} %get-tuple-element.23), channel_id=1, source_target_pairs={{0,1},{1,2},{2,3},{3,0},{4,5},{5,6},{6,7},{7,4},{8,9},{9,10},{10,1... | collective-permute-start | bytes 172040 | tf_op jit(solution)/shard_map/ppermute | solution.py:596
  6.9 24.2 %collective-permute-start.9 = (f32[4,8,8,128]{3,2,1,0:T(8,128)S(1)}, f32[4,8,8,128]{3,2,1,0:T(8,128)S(1)}, u32[]{:S(2)}, u32[]{:S(2)}) collective-permute-start(f32[4,8,8,128]{3,2,1,0:T(8,128)S(1)} %get-tuple-element.34.refs_0_), channel_id=1, source_target_pairs={{0,24},{4,28},{8,16},{12,20},{16,8},{20,12},{24,0},{28,4},{1,25},{... | collective-permute-start | bytes 393224 | tf_op jit(solution)/shard_map/ppermute | solution.py:593
  9.3 21.8 %collective-permute-start.8 = (f32[4,8,8,128]{3,2,1,0:T(8,128)S(1)}, f32[4,8,8,128]{3,2,1,0:T(8,128)S(1)}, u32[]{:S(2)}, u32[]{:S(2)}) collective-permute-start(f32[4,8,8,128]{3,2,1,0:T(8,128)S(1)} %get-tuple-element.34.refs_0_), channel_id=1, source_target_pairs={{0,16},{4,20},{8,24},{12,28},{16,0},{20,4},{24,8},{28,12},{1,17},{... | collective-permute-start | bytes 393224 | tf_op jit(solution)/shard_map/ppermute | solution.py:593
  9.8 21.3 %collective-permute-start.7 = (f32[4,8,8,128]{3,2,1,0:T(8,128)S(1)}, f32[4,8,8,128]{3,2,1,0:T(8,128)S(1)}, u32[]{:S(2)}, u32[]{:S(2)}) collective-permute-start(f32[4,8,8,128]{3,2,1,0:T(8,128)S(1)} %get-tuple-element.34.refs_0_), channel_id=1, source_target_pairs={{0,8},{4,12},{8,0},{12,4},{16,24},{20,28},{24,16},{28,20},{1,9},{5... | collective-permute-start | bytes 393224 | tf_op jit(solution)/shard_map/ppermute | solution.py:593
  10.5 0.7 %copy-start.1 = (bf16[32,256]{1,0:T(8,128)(2,1)S(1)}, bf16[32,256]{1,0:T(8,128)(2,1)}, u32[]{:S(2)}) copy-start(bf16[32,256]{1,0:T(8,128)(2,1)} %param.12) | copy-start | bytes 49156
  12.9 4.2 %collective-permute-start.5 = (f32[6,8,128]{2,1,0:T(8,128)S(1)}, f32[6,8,128]{2,1,0:T(8,128)S(1)}, u32[]{:S(2)}, u32[]{:S(2)}) collective-permute-start(f32[6,8,128]{2,1,0:T(8,128)S(1)} %get-tuple-element.26), channel_id=1, source_target_pairs={{0,20},{4,24},{8,28},{12,16},{16,4},{20,8},{24,12},{28,0},{1,21},{... | collective-permute-start | bytes 73736 | tf_op jit(solution)/shard_map/ppermute | solution.py:590
  12.9 4.5 %collective-permute-start.3 = (f32[6,8,128]{2,1,0:T(8,128)S(1)}, f32[6,8,128]{2,1,0:T(8,128)S(1)}, u32[]{:S(2)}, u32[]{:S(2)}) collective-permute-start(f32[6,8,128]{2,1,0:T(8,128)S(1)} %get-tuple-element.26), channel_id=1, source_target_pairs={{0,4},{4,8},{8,12},{12,0},{16,20},{20,24},{24,28},{28,16},{1,5},{5... | collective-permute-start | bytes 73736 | tf_op jit(solution)/shard_map/ppermute | solution.py:590
  17.1 1.6 %copy-start.3 = (f32[256]{0:T(256)S(1)}, f32[256]{0:T(256)}, u32[]{:S(2)}) copy-start(f32[256]{0:T(256)} %param.13) | copy-start | bytes 3076
  17.1 3.3 %collective-permute-start.6 = (f32[6,8,128]{2,1,0:T(8,128)S(1)}, f32[6,8,128]{2,1,0:T(8,128)S(1)}, u32[]{:S(2)}, u32[]{:S(2)}) collective-permute-start(f32[6,8,128]{2,1,0:T(8,128)S(1)} %get-tuple-element.27), channel_id=1, source_target_pairs={{0,28},{4,16},{8,20},{12,24},{16,12},{20,0},{24,4},{28,8},{1,29},{... | collective-permute-start | bytes 73736 | tf_op jit(solution)/shard_map/ppermute | solution.py:590
  17.4 1.3 %copy-start.2 = (bf16[256,4]{0,1:T(4,128)(2,1)S(1)}, bf16[256,4]{0,1:T(4,128)(2,1)}, u32[]{:S(2)}) copy-start(bf16[256,4]{0,1:T(4,128)(2,1)} %param.15) | copy-start | bytes 6148
  17.4 8.6 %collective-permute-start.2 = (f32[2,12,8,128]{3,2,1,0:T(8,128)S(1)}, f32[2,12,8,128]{3,2,1,0:T(8,128)S(1)}, u32[]{:S(2)}, u32[]{:S(2)}) collective-permute-start(f32[2,12,8,128]{3,2,1,0:T(8,128)S(1)} %get-tuple-element.25), channel_id=1, source_target_pairs={{0,16},{4,20},{8,24},{12,28},{16,0},{20,4},{24,8},{28,12},{1,17},{... | collective-permute-start | bytes 294920 | tf_op jit(solution)/shard_map/ppermute | solution.py:590
  20.3 5.7 %collective-permute-start.4 = (f32[6,8,128]{2,1,0:T(8,128)S(1)}, f32[6,8,128]{2,1,0:T(8,128)S(1)}, u32[]{:S(2)}, u32[]{:S(2)}) collective-permute-start(f32[6,8,128]{2,1,0:T(8,128)S(1)} %get-tuple-element.27), channel_id=1, source_target_pairs={{0,12},{4,0},{8,4},{12,8},{16,28},{20,16},{24,20},{28,24},{1,13},{... | collective-permute-start | bytes 73736 | tf_op jit(solution)/shard_map/ppermute | solution.py:590
  26.0 13.5 %copy-start = (f32[6,4,8,128]{3,2,1,0:T(8,128)S(1)}, f32[6,4,8,128]{3,2,1,0:T(8,128)}, u32[]{:S(2)}) copy-start(f32[6,4,8,128]{3,2,1,0:T(8,128)} %vel.1) | copy-start | bytes 294916
  31.1 5.4 %collective-permute-start.19 = (f32[18,8,128]{2,1,0:T(8,128)S(1)}, f32[18,8,128]{2,1,0:T(8,128)S(1)}, u32[]{:S(2)}, u32[]{:S(2)}) collective-permute-start(f32[18,8,128]{2,1,0:T(8,128)S(1)} %get-tuple-element.38.refs_8_), channel_id=1, source_target_pairs={{0,24},{4,28},{8,16},{12,20},{16,8},{20,12},{24,0},{28,4},{1,25},{... | collective-permute-start | bytes 221192 | tf_op jit(solution)/shard_map/ppermute | solution.py:593
  32.5 5.2 %collective-permute-start.17 = (f32[18,8,128]{2,1,0:T(8,128)S(1)}, f32[18,8,128]{2,1,0:T(8,128)S(1)}, u32[]{:S(2)}, u32[]{:S(2)}) collective-permute-start(f32[18,8,128]{2,1,0:T(8,128)S(1)} %get-tuple-element.38.refs_8_), channel_id=1, source_target_pairs={{0,16},{4,20},{8,24},{12,28},{16,0},{20,4},{24,8},{28,12},{1,17},{... | collective-permute-start | bytes 221192 | tf_op jit(solution)/shard_map/ppermute | solution.py:593
  34.1 4.4 %collective-permute-start.15 = (f32[18,8,128]{2,1,0:T(8,128)S(1)}, f32[18,8,128]{2,1,0:T(8,128)S(1)}, u32[]{:S(2)}, u32[]{:S(2)}) collective-permute-start(f32[18,8,128]{2,1,0:T(8,128)S(1)} %get-tuple-element.38.refs_8_), channel_id=1, source_target_pairs={{0,8},{4,12},{8,0},{12,4},{16,24},{20,28},{24,16},{28,20},{1,9},{5... | collective-permute-start | bytes 221192 | tf_op jit(solution)/shard_map/ppermute | solution.py:593
  34.7 4.3 %collective-permute-start.10 = (f32[4,8,8,128]{3,2,1,0:T(8,128)S(1)}, f32[4,8,8,128]{3,2,1,0:T(8,128)S(1)}, u32[]{:S(2)}, u32[]{:S(2)}) collective-permute-start(f32[4,8,8,128]{3,2,1,0:T(8,128)S(1)} %get-tuple-element.34.refs_0_), channel_id=1, source_target_pairs={{0,4},{4,0},{8,12},{12,8},{16,20},{20,16},{24,28},{28,24},{1,5},{5... | collective-permute-start | bytes 393224 | tf_op jit(solution)/shard_map/ppermute | solution.py:593
  34.7 4.4 %collective-permute-start.11 = (f32[4,8,8,128]{3,2,1,0:T(8,128)S(1)}, f32[4,8,8,128]{3,2,1,0:T(8,128)S(1)}, u32[]{:S(2)}, u32[]{:S(2)}) collective-permute-start(f32[4,8,8,128]{3,2,1,0:T(8,128)S(1)} %collective-permute-done.7.refs_2_), channel_id=1, source_target_pairs={{0,4},{4,0},{8,12},{12,8},{16,20},{20,16},{24,28},{28,24},{1,5},{5... | collective-permute-start | bytes 393224 | tf_op jit(solution)/shard_map/ppermute | solution.py:593
  36.5 1.9 %collective-permute-start.14 = (f32[18,8,128]{2,1,0:T(8,128)S(1)}, f32[18,8,128]{2,1,0:T(8,128)S(1)}, u32[]{:S(2)}, u32[]{:S(2)}) collective-permute-start(f32[18,8,128]{2,1,0:T(8,128)S(1)} %get-tuple-element.38.refs_8_), channel_id=1, source_target_pairs={{0,4},{4,0},{8,12},{12,8},{16,20},{20,16},{24,28},{28,24},{1,5},{5... | collective-permute-start | bytes 221192 | tf_op jit(solution)/shard_map/ppermute | solution.py:593
  37.7 2.5 %collective-permute-start.12 = (f32[4,8,8,128]{3,2,1,0:T(8,128)S(1)}, f32[4,8,8,128]{3,2,1,0:T(8,128)S(1)}, u32[]{:S(2)}, u32[]{:S(2)}) collective-permute-start(f32[4,8,8,128]{3,2,1,0:T(8,128)S(1)} %collective-permute-done.8.refs_4_), channel_id=1, source_target_pairs={{0,4},{4,0},{8,12},{12,8},{16,20},{20,16},{24,28},{28,24},{1,5},{5... | collective-permute-start | bytes 393224 | tf_op jit(solution)/shard_map/ppermute | solution.py:593
  38.5 1.7 %collective-permute-start.13 = (f32[4,8,8,128]{3,2,1,0:T(8,128)S(1)}, f32[4,8,8,128]{3,2,1,0:T(8,128)S(1)}, u32[]{:S(2)}, u32[]{:S(2)}) collective-permute-start(f32[4,8,8,128]{3,2,1,0:T(8,128)S(1)} %collective-permute-done.9.refs_6_), channel_id=1, source_target_pairs={{0,4},{4,0},{8,12},{12,8},{16,20},{20,16},{24,28},{28,24},{1,5},{5... | collective-permute-start | bytes 393224 | tf_op jit(solution)/shard_map/ppermute | solution.py:593
  38.5 1.7 %collective-permute-start.20 = (f32[18,8,128]{2,1,0:T(8,128)S(1)}, f32[18,8,128]{2,1,0:T(8,128)S(1)}, u32[]{:S(2)}, u32[]{:S(2)}) collective-permute-start(f32[18,8,128]{2,1,0:T(8,128)S(1)} %collective-permute-done.19.refs_14_), channel_id=1, source_target_pairs={{0,4},{4,0},{8,12},{12,8},{16,20},{20,16},{24,28},{28,24},{1,5},{5... | collective-permute-start | bytes 221192 | tf_op jit(solution)/shard_map/ppermute | solution.py:593
  39.0 1.3 %collective-permute-start.18 = (f32[18,8,128]{2,1,0:T(8,128)S(1)}, f32[18,8,128]{2,1,0:T(8,128)S(1)}, u32[]{:S(2)}, u32[]{:S(2)}) collective-permute-start(f32[18,8,128]{2,1,0:T(8,128)S(1)} %collective-permute-done.17.refs_12_), channel_id=1, source_target_pairs={{0,4},{4,0},{8,12},{12,8},{16,20},{20,16},{24,28},{28,24},{1,5},{5... | collective-permute-start | bytes 221192 | tf_op jit(solution)/shard_map/ppermute | solution.py:593
  39.1 1.4 %collective-permute-start.16 = (f32[18,8,128]{2,1,0:T(8,128)S(1)}, f32[18,8,128]{2,1,0:T(8,128)S(1)}, u32[]{:S(2)}, u32[]{:S(2)}) collective-permute-start(f32[18,8,128]{2,1,0:T(8,128)S(1)} %collective-permute-done.15.refs_10_), channel_id=1, source_target_pairs={{0,4},{4,0},{8,12},{12,8},{16,20},{20,16},{24,28},{28,24},{1,5},{5... | collective-permute-start | bytes 221192 | tf_op jit(solution)/shard_map/ppermute | solution.py:593
